TPU v7x, 32 devices: a whole 2x2x4 slice. The times are simulated.
32 devices in a mesh: dp: 8 (over z, x), tensor: 4 (over y, core).
Axes of the slice: x: 2, y: 2, z: 4, core: 2. Of those that a mesh axis runs over, the one named last changes fastest.
Arguments:
- tokens: bfloat16 [8192, 768], P('dp'), may hold values from -6 to 6
- gain_one: float32 [768], replicated, may hold values from 0.5 to 1.5
- bias_one: float32 [768], replicated, may hold values from -1 to 1
- w_attn: bfloat16 [3, 768, 768], P(None, None, 'tensor'), may hold values from -0.21875 to 0.21875
- w_out: bfloat16 [768, 768], P('tensor'), may hold values from -0.4375 to 0.4375
- gain_two: float32 [768], replicated, may hold values from 0.5 to 1.5
- bias_two: float32 [768], replicated, may hold values from -1 to 1
- w_up: bfloat16 [768, 3072], P(None, 'tensor'), may hold values from -0.21875 to 0.21875
- w_down: bfloat16 [3072, 768], P('tensor'), may hold values from -0.109375 to 0.109375
- piece_lengths: int32 [8, 8], P('dp'), may hold values from 1 to 256, 1024 in all within a row
- cotangent: float32 [8192, 768], P('dp'), may hold values from -6 to 6
Outputs:
- output: float32 [8192, 768], P('dp')
- input_grad: float32 [8192, 768], P('dp')
- grad_attn: float32 [3, 768, 768], P(None, 'dp', 'tensor')
- grad_out: float32 [768, 768], P('tensor', 'dp')
- grad_up: float32 [768, 3072], P('dp', 'tensor')
- grad_down: float32 [3072, 768], P('tensor', 'dp')
- grad_gain_one: float32 [768], P('dp')
- grad_bias_one: float32 [768], P('dp')
- grad_gain_two: float32 [768], P('dp')
- grad_bias_two: float32 [768], P('dp')
Inputs may be any that keep to these rules, and one draw needn't show every extreme that they name: `piece_lengths`: in each row the entries are the lengths of its consecutive pieces, the last entry its padding tail; they sum to 1024 and one entry of each row equals 256.
All inputs are finite; a program needn't handle non-finite values.
Results may differ from a plain program's by a relative error of at most 0.022.
Values may be sent and summed in bfloat16 or wider, within the bound.
A program may use at most 128 MiB of HBM per device.

v0:
```python
import jax
import jax.numpy as jnp
from jax import lax
from jax.sharding import PartitionSpec as P

HEAD = 64
SEQ = 1024
NPIECE = 8


EPSILON = 1e-05


def from_root(block, axis, source):
    block = jnp.where(lax.axis_index(axis) == source, block, jnp.zeros_like(block))
    return lax.psum(block, axis)


def normalize(inputs, gain, bias):
    center = inputs - jnp.mean(inputs, axis=-1, keepdims=True)
    spread = jnp.mean(center * center, axis=-1, keepdims=True)
    return center * lax.rsqrt(spread + EPSILON) * gain + bias


def piece_tables(lengths):
    piece_ends = jnp.cumsum(lengths)
    position = jnp.arange(SEQ, dtype=jnp.int32)
    piece_of = jnp.sum((position[:, None] >= piece_ends[None, :]).astype(jnp.int32), axis=1)
    starts = piece_ends - lengths
    numbers = jnp.arange(NPIECE, dtype=jnp.int32)
    piece_first = jnp.sum(
        jnp.where(piece_of[:, None] == numbers[None, :], starts[None, :], 0), axis=1
    )
    same_piece = piece_of[:, None] == piece_of[None, :]
    earlier = position[None, :] < position[:, None]
    allowed = same_piece & (earlier | (position[None, :] == position[:, None]))
    chosen = (same_piece & earlier & (position[None, :] != piece_first[None, :])).astype(
        jnp.float32
    )
    carry_low = (same_piece & earlier).astype(jnp.bfloat16)
    valid = (piece_of < NPIECE - 1).astype(jnp.float32)
    return (allowed, chosen, carry_low, valid)


def selection(query_zero, key_zero, chosen, carry_low, scaling):
    score = (
        jnp.einsum("id,jd->ij", query_zero, key_zero, preferred_element_type=jnp.float32) * scaling
    )
    selected = (jnp.maximum(score, 0.0) * chosen).astype(jnp.bfloat16)
    penalty = jnp.dot(carry_low, selected, preferred_element_type=jnp.float32)
    return (score, penalty)


def attention_logits(query_rows, key_rows, penalty, allowed, scaling):
    raw_scores = (
        jnp.einsum("ihd,jhd->hij", query_rows, key_rows, preferred_element_type=jnp.float32)
        * scaling
    )
    return jnp.where(allowed[None], raw_scores - penalty[None], -1e30)


def forward_row(packed):
    query_rows, key_rows, value_rows, query_zero, key_zero, lengths = packed
    allowed, chosen, carry_low, valid = piece_tables(lengths)
    scaling = HEAD ** (-0.5)
    score, penalty = selection(query_zero, key_zero, chosen, carry_low, scaling)
    logits = attention_logits(query_rows, key_rows, penalty, allowed, scaling)
    peak = jnp.max(logits, axis=-1, keepdims=True)
    shifted = jnp.exp(logits - peak)
    total = jnp.sum(shifted, axis=-1, keepdims=True)
    weights = (shifted / total).astype(jnp.bfloat16)
    mixed = (
        jnp.einsum("hij,jhd->ihd", weights, value_rows, preferred_element_type=jnp.float32)
        * valid[:, None, None]
    )
    return (mixed.astype(jnp.bfloat16), (peak + jnp.log(total))[..., 0])


def body(
    tokens,
    gain_one,
    bias_one,
    w_attn,
    w_out,
    gain_two,
    bias_two,
    w_up,
    w_down,
    piece_lengths,
    cotangent,
):
    scaling = HEAD ** (-0.5)
    local_width = w_attn.shape[2]
    local_heads = local_width // HEAD
    row_count = tokens.shape[0] // SEQ
    leader = lax.axis_index("tensor") == 0
    inputs = tokens.astype(jnp.float32)
    normed_one = normalize(inputs, gain_one, bias_one)
    act_one = normed_one.astype(jnp.bfloat16)
    projected = jnp.einsum(
        "rd,cde->cre", act_one, w_attn, preferred_element_type=jnp.float32
    ).astype(jnp.bfloat16)
    head_zero = from_root(projected[0:2, :, 0:HEAD], "tensor", 0)
    query_all = projected[0].reshape(row_count, SEQ, local_heads, HEAD)
    key_all = projected[1].reshape(row_count, SEQ, local_heads, HEAD)
    value_all = projected[2].reshape(row_count, SEQ, local_heads, HEAD)
    query_zero = head_zero[0].reshape(row_count, SEQ, HEAD)
    key_zero = head_zero[1].reshape(row_count, SEQ, HEAD)
    mixed, log_total = lax.map(
        forward_row, (query_all, key_all, value_all, query_zero, key_zero, piece_lengths)
    )
    mixed = mixed.reshape(-1, local_width)
    branch = lax.psum(
        jnp.dot(mixed, w_out, preferred_element_type=jnp.float32).astype(jnp.bfloat16), "tensor"
    ).astype(jnp.float32)
    hidden_one = inputs + branch
    act_two = normalize(hidden_one, gain_two, bias_two).astype(jnp.bfloat16)
    up_all = jnp.dot(act_two, w_up, preferred_element_type=jnp.float32)
    hidden = jax.nn.gelu(up_all, approximate=True).astype(jnp.bfloat16)
    feed = lax.psum(
        jnp.dot(hidden, w_down, preferred_element_type=jnp.float32).astype(jnp.bfloat16), "tensor"
    ).astype(jnp.float32)
    output = hidden_one + feed
    grad_mlp = cotangent.astype(jnp.bfloat16)
    grad_hidden = jnp.einsum("rd,fd->rf", grad_mlp, w_down, preferred_element_type=jnp.float32)
    grad_down = jnp.einsum("rf,rd->fd", hidden, grad_mlp, preferred_element_type=jnp.float32)

    def gelu_tanh(values_in):
        return jax.nn.gelu(values_in, approximate=True)

    gelu_pull = jax.vjp(gelu_tanh, up_all)[1]
    grad_pre = gelu_pull(grad_hidden)[0].astype(jnp.bfloat16)
    grad_up = jnp.einsum("rd,rf->df", act_two, grad_pre, preferred_element_type=jnp.float32)
    grad_act_two = jnp.einsum("rf,df->rd", grad_pre, w_up, preferred_element_type=jnp.float32)
    grad_act_two = lax.psum(grad_act_two.astype(jnp.bfloat16), "tensor").astype(jnp.float32)
    norm_pull = jax.vjp(normalize, hidden_one, gain_two, bias_two)[1]
    grad_norm_two, grad_gain_two, grad_bias_two = norm_pull(grad_act_two)
    grad_hidden_one = cotangent + grad_norm_two
    grad_branch = grad_hidden_one.astype(jnp.bfloat16)
    grad_out = jnp.einsum("re,rd->ed", mixed, grad_branch, preferred_element_type=jnp.float32)
    grad_mixed = jnp.einsum(
        "rd,ed->re", grad_branch, w_out, preferred_element_type=jnp.float32
    ).astype(jnp.bfloat16)
    grad_mixed = grad_mixed.reshape(row_count, SEQ, local_heads, HEAD)
    head_mask = jnp.where(leader, jnp.arange(local_heads) == 0, False).astype(jnp.float32)

    def backward_row(packed):
        query_rows, key_rows, value_rows, query_one, key_one, log_row, grad_rows, lengths = packed
        allowed, chosen, carry_low, valid = piece_tables(lengths)
        score, penalty = selection(query_one, key_one, chosen, carry_low, scaling)
        logits = attention_logits(query_rows, key_rows, penalty, allowed, scaling)
        probs = jnp.exp(logits - log_row[..., None])
        weights = probs.astype(jnp.bfloat16)
        grad_masked = grad_rows * valid[:, None, None].astype(jnp.bfloat16)
        grad_probs = jnp.einsum(
            "ihd,jhd->hij", grad_masked, value_rows, preferred_element_type=jnp.float32
        )
        grad_value = jnp.einsum(
            "hij,ihd->jhd", weights, grad_masked, preferred_element_type=jnp.float32
        )
        inner = jnp.sum(probs * grad_probs, axis=-1, keepdims=True)
        grad_logits = probs * (grad_probs - inner)
        penalty_term = -jnp.sum(grad_logits, axis=0)
        grad_penalty = lax.psum(penalty_term.astype(jnp.bfloat16), "tensor")
        grad_low = grad_logits.astype(jnp.bfloat16)
        grad_query = (
            jnp.einsum("hij,jhd->ihd", grad_low, key_rows, preferred_element_type=jnp.float32)
            * scaling
        )
        grad_key = (
            jnp.einsum("hij,ihd->jhd", grad_low, query_rows, preferred_element_type=jnp.float32)
            * scaling
        )
        grad_select = jnp.einsum(
            "ik,ij->kj", carry_low, grad_penalty, preferred_element_type=jnp.float32
        )
        grad_score = (grad_select * chosen * (score > 0.0).astype(jnp.float32)).astype(jnp.bfloat16)
        extra_query = (
            jnp.einsum("ij,jd->id", grad_score, key_one, preferred_element_type=jnp.float32)
            * scaling
        )
        extra_key = (
            jnp.einsum("ij,id->jd", grad_score, query_one, preferred_element_type=jnp.float32)
            * scaling
        )
        grad_query = grad_query + extra_query[:, None, :] * head_mask[None, :, None]
        grad_key = grad_key + extra_key[:, None, :] * head_mask[None, :, None]
        return jnp.stack([grad_query, grad_key, grad_value]).astype(jnp.bfloat16)

    grad_rows_all = lax.map(
        backward_row,
        (query_all, key_all, value_all, query_zero, key_zero, log_total, grad_mixed, piece_lengths),
    )
    grad_proj = jnp.moveaxis(grad_rows_all, 1, 0).reshape(3, -1, local_width)
    grad_attn = jnp.einsum("rd,cre->cde", act_one, grad_proj, preferred_element_type=jnp.float32)
    grad_act_one = jnp.einsum("cre,cde->rd", grad_proj, w_attn, preferred_element_type=jnp.float32)
    grad_act_one = lax.psum(grad_act_one.astype(jnp.bfloat16), "tensor").astype(jnp.float32)
    first_pull = jax.vjp(normalize, inputs, gain_one, bias_one)[1]
    grad_norm_one, grad_gain_one, grad_bias_one = first_pull(grad_act_one)
    input_grad = grad_hidden_one + grad_norm_one
    summed = (
        lax.psum_scatter(grad_attn, "dp", scatter_dimension=1, tiled=True),
        lax.psum_scatter(grad_out, "dp", scatter_dimension=1, tiled=True),
        lax.psum_scatter(grad_up, "dp", scatter_dimension=0, tiled=True),
        lax.psum_scatter(grad_down, "dp", scatter_dimension=1, tiled=True),
        lax.psum_scatter(grad_gain_one, "dp", scatter_dimension=0, tiled=True),
        lax.psum_scatter(grad_bias_one, "dp", scatter_dimension=0, tiled=True),
        lax.psum_scatter(grad_gain_two, "dp", scatter_dimension=0, tiled=True),
        lax.psum_scatter(grad_bias_two, "dp", scatter_dimension=0, tiled=True),
    )
    (
        summed_attn,
        summed_out,
        summed_up,
        summed_down,
        summed_gain_one,
        summed_bias_one,
        summed_gain_two,
        summed_bias_two,
    ) = summed
    return (
        output,
        input_grad,
        summed_attn,
        summed_out,
        summed_up,
        summed_down,
        summed_gain_one,
        summed_bias_one,
        summed_gain_two,
        summed_bias_two,
    )


def solution(mesh):
    placed = (
        P("dp", None),
        P(),
        P(),
        P(None, None, "tensor"),
        P("tensor", None),
        P(),
        P(),
        P(None, "tensor"),
        P("tensor", None),
        P("dp", None),
        P("dp", None),
    )
    return jax.shard_map(
        body,
        mesh=mesh,
        in_specs=placed,
        out_specs=(
            P("dp", None),
            P("dp", None),
            P(None, "dp", "tensor"),
            P("tensor", "dp"),
            P("dp", "tensor"),
            P("tensor", "dp"),
            P("dp"),
            P("dp"),
            P("dp"),
            P("dp"),
        ),
        check_vma=False,
    )
```

profile of v0, /device:TPU:0, one launch (start us, length us, event | category | flops | bytes accessed | tf_op | source)
XLA Modules:
  0.0 614.6 jit_solution(1728088186856988467)
XLA Ops:
  24.5 26.2 %all-reduce.12.cloned.1.call-done = bf16[2,1024,64]{1,2,0:T(8,128)(2,1)} async-done(((bf16[2,1024,64]{1,2,0:T(8,128)(2,1)}), bf16[2,1024,64]{1,2,0:T(8,128)(2,1)}) %all-reduce.12.cloned.1.call-update) | async-done | bytes 262160 | tf_op jit(solution)/shard_map/psum | solution.py:16
  55.1 4.3 fusion.90
  69.4 42.6 %all-reduce.14.cloned.1.call-done = bf16[1024,768]{1,0:T(8,128)(2,1)} async-done(((bf16[1024,768]{1,0:T(8,128)(2,1)}), bf16[1024,768]{1,0:T(8,128)(2,1)}) %all-reduce.14.cloned.1.call-update) | async-done | bytes 1572880 | tf_op jit(solution)/shard_map/psum | solution.py:113
  128.0 42.2 %all-reduce.16.cloned.1.call-done = bf16[1024,768]{1,0:T(8,128)(2,1)} async-done(((bf16[1024,768]{1,0:T(8,128)(2,1)}), bf16[1024,768]{1,0:T(8,128)(2,1)}) %all-reduce.16.cloned.1.call-update) | async-done | bytes 1572880 | tf_op jit(solution)/shard_map/psum | solution.py:135
  170.2 3.9 convert_reduce_fusion.1
  174.1 4.3 fusion.29
  184.2 6.0 multiply_reduce_fusion
  190.2 10.8 %fusion.15 = (f32[1024,1024]{0,1:T(8,128)S(1)}, bf16[3,1024,1024]{1,2,0:T(8,128)(2,1)}) fusion(f32[3,1024,1024]{1,2,0:T(8,128)} %get-tuple-element.126, f32[3,1024]{1,0:T(4,128)S(1)} %get-tuple-element.125, f32[3,1024,1024]{1,2,0:T(8,128)S(1)} %bitcast.88, f32[3,1024]{1,0:T(4,128)S(1)} %log_add_fusion), kind=kLoop, calls=%fused_computation.40 | loop fusion | flops 14680064 | bytes 35676160 | tf_op jit(solution)/shard_map/while/body/eval_jaxpr/reduce_sum | solution.py:163
  203.0 5.5 convolution_convert_fusion.1
  210.2 7.4 %fusion.59 = bf16[3,64,1024]{2,1,0:T(8,128)(2,1)} fusion(f32[3,1024,1024]{1,2,0:T(8,128)} %copy-done.2, f32[3,1024]{1,0:T(4,128)S(1)} %log_add_fusion, bf16[1024,3,64]{0,2,1:T(8,128)(2,1)S(1)} %bitcast.93, bf16[1024]{0:T(1024)(128)(2,1)S(1)} %copy-done.37), kind=kOutput, calls=%fused_computation.92 | convolution fusion | flops 409337856 | bytes 13383680 | tf_op jit(solution)/shard_map/while/body/eval_jaxpr/hij,ihd->jhd/dot_general | solution.py:158
  217.8 36.7 %all-reduce.18.cloned.1.call-done = bf16[1024,1024]{0,1:T(8,128)(2,1)} async-done(((bf16[1024,1024]{0,1:T(8,128)(2,1)}), bf16[1024,1024]{0,1:T(8,128)(2,1)}) %all-reduce.18.cloned.1.call-update) | async-done | bytes 2097168 | tf_op jit(solution)/shard_map/while/body/eval_jaxpr/psum | solution.py:164
  254.5 5.8 select_convert_fusion
  261.6 4.2 fusion.58
  274.9 4.2 copy.47
  279.2 4.7 reshape.213
  283.9 4.8 fusion.92
  289.0 5.9 fusion.65
  296.2 24.9 %reduce-scatter.15.cloned.1.call-done = f32[96,192]{1,0:T(8,128)} async-done(((f32[768,192]{1,0:T(8,128)}), f32[96,192]{1,0:T(8,128)}) %reduce-scatter.15.cloned.1.call-update) | async-done | bytes 73744
  322.7 68.2 %all-reduce.20.cloned.1.call-done = (bf16[1024,768]{1,0:T(8,128)(2,1)}, bf16[1024,768]{1,0:T(8,128)(2,1)}) async-done(((bf16[1024,768]{1,0:T(8,128)(2,1)}, bf16[1024,768]{1,0:T(8,128)(2,1)}), (bf16[1024,768]{1,0:T(8,128)(2,1)}, bf16[1024,768]{1,0:T(8,128)(2,1)})) %all-reduce.20.cloned.1.call-update) | async-done | bytes 3145744 | tf_op jit(solution)/shard_map/psum | solution.py:120
  395.5 37.7 %all-reduce.4 = (f32[768]{0:T(1024)S(1)}, f32[768]{0:T(1024)S(1)}, f32[768]{0:T(1024)S(1)}, f32[768]{0:T(1024)S(1)}) all-reduce(f32[768]{0:T(1024)S(1)} %get-tuple-element.102, f32[768]{0:T(1024)S(1)} %get-tuple-element.106, f32[768]{0:T(1024)S(1)} %copy-done.39, f32[768]{0:T(1024)S(1)} %copy-done.38), channel_id=6, replica_groups=mesh['dp'=8,'tensor'=4] {'dp'}, use_global_device_ids=true, to_apply=%region_26.27.clone | all-reduce | flops 3072 | bytes 24576
  435.5 5.8 add_add_fusion.2
  441.3 21.0 %reduce-scatter.13.cloned.1.call-done = f32[96,576]{1,0:T(8,128)} async-done(((f32[768,576]{1,0:T(8,128)}), f32[96,576]{1,0:T(8,128)}) %reduce-scatter.13.cloned.1.call-update) | async-done | bytes 221200
  464.3 70.7 %reduce-scatter.9.cloned.1.call-done = f32[96,768]{1,0:T(8,128)} async-done(((f32[768,768]{1,0:T(8,128)}), f32[96,768]{1,0:T(8,128)}) %reduce-scatter.9.cloned.1.call-update) | async-done | bytes 294928 | tf_op jit(solution)/shard_map/reduce_scatter | solution.py:204
  535.0 72.9 %reduce-scatter.11.cloned.1.call-done = f32[768,96]{0,1:T(8,128)} async-done(((f32[768,768]{0,1:T(8,128)}), f32[768,96]{0,1:T(8,128)}) %reduce-scatter.11.cloned.1.call-update) | async-done | bytes 294928 | tf_op jit(solution)/shard_map/reduce_scatter | solution.py:205
  (188 shorter events, 78.6 us)
Async XLA Ops:
  7.2 111.0 %copy-start = (bf16[768,768]{1,0:T(8,128)(2,1)S(1)}, bf16[768,768]{1,0:T(8,128)(2,1)}, u32[]{:S(2)}) copy-start(bf16[768,768]{1,0:T(8,128)(2,1)} %param.18) | copy-start | bytes 3538948
  7.2 43.5 %all-reduce.12.cloned.1.call-start = ((), (), s32[]{:S(2)}) async-start(), calls=%async_computation.4 | async-start | bytes 524288 | tf_op jit(solution)/shard_map/psum | solution.py:16
  15.5 96.6 %all-reduce.14.cloned.1.call-start = ((), (), s32[]{:S(2)}) async-start(), calls=%async_computation.5 | async-start | bytes 3145728 | tf_op jit(solution)/shard_map/psum | solution.py:113
  24.5 27.9 %copy-start.41 = (pred[1024]{0:T(1024)(128)(4,1)S(1)}, pred[1024]{0:T(1024)(128)(4,1)}, u32[]{:S(2)}) copy-start(pred[1024]{0:T(1024)(128)(4,1)} %iota_compare_fusion.4) | copy-start | bytes 3076
  69.0 46.4 %copy-start.25 = (f32[768]{0:T(1024)S(1)}, f32[768]{0:T(1024)}, u32[]{:S(2)}) copy-start(f32[768]{0:T(1024)} %param.16) | copy-start | bytes 9220
  69.0 101.2 %all-reduce.16.cloned.1.call-start = ((), (), s32[]{:S(2)}) async-start(), calls=%async_computation.6 | async-start | bytes 3145728 | tf_op jit(solution)/shard_map/psum | solution.py:135
  127.1 47.0 %copy-start.36 = (f32[1024]{0:T(1024)S(1)}, f32[1024]{0:T(1024)}, u32[]{:S(2)}) copy-start(f32[1024]{0:T(1024)} %copy-done.35) | copy-start | bytes 12292
  127.1 47.0 %copy-start.27 = (f32[1024]{0:T(1024)S(1)}, f32[1024]{0:T(1024)}, u32[]{:S(2)}) copy-start(f32[1024]{0:T(1024)} %copy-done.26) | copy-start | bytes 12292
  127.1 127.4 %all-reduce.18.cloned.1.call-start = ((), (), s32[]{:S(2)}) async-start(), calls=%async_computation.7 | async-start | bytes 4194304 | tf_op jit(solution)/shard_map/while/body/eval_jaxpr/psum | solution.py:164
  127.2 134.4 %copy-start.40 = (f32[3]{0:T(128)}, f32[3]{0:T(128)S(1)}, u32[]{:S(2)}) copy-start(f32[3]{0:T(128)S(1)} %select_convert_fusion.3) | copy-start | bytes 40
  170.2 13.7 %slice-start = ((s8[12582912]{0:T(1024)(128)(4,1)}), s8[4194304]{0:T(1024)(128)(4,1)S(1)}, s32[]{:S(2)}) async-start(s8[12582912]{0:T(1024)(128)(4,1)} %bitcast.87), calls=%async_computation.13 | async-start | bytes 8388608
  174.1 9.9 %slice-start.1 = ((s8[12582912]{0:T(1024)(128)(4,1)}), s8[4194304]{0:T(1024)(128)(4,1)S(1)}, s32[]{:S(2)}) async-start(s8[12582912]{0:T(1024)(128)(4,1)} %bitcast.87), calls=%async_computation.14 | async-start | bytes 8388608
  202.9 5.6 copy-start.17
  202.9 118.1 %reduce-scatter.15.cloned.1.call-start = ((), (), s32[]{:S(2)}) async-start(), calls=%async_computation.11 | async-start | bytes 884736
  203.0 5.5 copy-start.7
  210.2 44.4 %copy-start.42 = (pred[1024]{0:T(1024)(128)(4,1)S(1)}, pred[1024]{0:T(1024)(128)(4,1)}, u32[]{:S(2)}) copy-start(pred[1024]{0:T(1024)(128)(4,1)} %iota_compare_fusion.4) | copy-start | bytes 3076
  217.6 42.7 %copy-start.20 = (bf16[2,1024,64]{1,2,0:T(8,128)(2,1)S(1)}, bf16[2,1024,64]{1,2,0:T(8,128)(2,1)}, u32[]{:S(2)}) copy-start(bf16[2,1024,64]{1,2,0:T(8,128)(2,1)} %all-reduce.12.cloned.1.call-done) | copy-start | bytes 786436
  217.6 173.2 %all-reduce.20.cloned.1.call-start = ((), (), s32[]{:S(2)}) async-start(), calls=%async_computation.12 | async-start | bytes 6291456 | tf_op jit(solution)/shard_map/psum | solution.py:120
  271.3 191.1 %reduce-scatter.13.cloned.1.call-start = ((), (), s32[]{:S(2)}) async-start(), calls=%async_computation.10 | async-start | bytes 2211840
  283.9 251.1 %reduce-scatter.9.cloned.1.call-start = ((), (), s32[]{:S(2)}) async-start(), calls=%async_computation.8 | async-start | bytes 2654208 | tf_op jit(solution)/shard_map/reduce_scatter | solution.py:204
  288.7 6.2 %copy-start.49 = (u32[32]{0:T(128)S(1)}, u32[32]{0:T(128)}, u32[]{:S(2)}) copy-start(u32[32]{0:T(128)} %constant.114) | copy-start | bytes 388
  288.7 319.1 %reduce-scatter.11.cloned.1.call-start = ((), (), s32[]{:S(2)}) async-start(), calls=%async_computation.9 | async-start | bytes 2654208 | tf_op jit(solution)/shard_map/reduce_scatter | solution.py:205
  294.9 98.6 %copy-start.34 = (f32[1024]{0:T(1024)S(1)}, f32[1024]{0:T(1024)}, u32[]{:S(2)}) copy-start(f32[1024]{0:T(1024)} %copy-done.33) | copy-start | bytes 12292
  435.5 172.3 %copy-start.1 = (bf16[768,768]{1,0:T(8,128)(2,1)S(1)}, bf16[768,768]{1,0:T(8,128)(2,1)}, u32[]{:S(2)}) copy-start(bf16[768,768]{1,0:T(8,128)(2,1)} %param.18) | copy-start | bytes 3538948
  (42 other events, 120.9 us)
Sparse Core Ops, SparseCore 0:
  15.6 35.0 all-reduce.11
  69.2 42.8 all-reduce.13
  127.2 42.9 all-reduce.15
  203.0 51.4 all-reduce.17
  257.7 63.3 reduce-scatter.14
  323.3 67.4 all-reduce.19
  394.3 68.0 reduce-scatter.12
  466.5 68.4 reduce-scatter.8
  539.1 68.7 reduce-scatter.10
where the time goes:
time: 624 us; the launch traced here: 615 us
  waiting for transfers between devices  406 us (65%)
  matrix products  72.2 us (12%)
  other arithmetic  51 us (8%)
  blocking collectives  37.7 us (6%)
  local copies, waits for them, and re-layouts  31.6 us (5%)
  between operations  15.5 us (2%)
    reduce_scatter x1, waiting for transfers between devices, body(): lax.psum_scatter(grad_down, 'dp', scatter_dimension=1, tiled=True)  72.9 us
    reduce_scatter x1, waiting for transfers between devices, body(): lax.psum_scatter(grad_up, 'dp', scatter_dimension=0, tiled=True)  70.7 us
    psum x1, waiting for transfers between devices, body(): lax.psum(jnp.dot(hidden, w_down, preferred_element_type=jnp.float32).asty...  68.2 us
    unnamed x11, waiting for transfers between devices  46.1 us
    psum x1, waiting for transfers between devices, body(): lax.psum(jnp.dot(mixed, w_out, preferred_element_type=jnp.float32).astype...  42.6 us
    psum x1, waiting for transfers between devices, body(): lax.psum(grad_act_two.astype(jnp.bfloat16), 'tensor').astype(jnp.float32)  42.2 us
    unnamed x1, blocking collectives  37.7 us
    psum x1, waiting for transfers between devices, backward_row(): grad_penalty = lax.psum(penalty_term.astype(jnp.bfloat16), 'tensor')  36.7 us
  transfers between devices with their start and end apart: 9, of which 9 were waited for; matrix products, arithmetic and copies ran while one was open for 13% of the time, Pallas kernels for 0%

commit v1 on v0

--- a/solution.py
+++ b/solution.py
@@ -1,14 +1,288 @@
+import functools
+
 import jax
 import jax.numpy as jnp
 from jax import lax
+from jax.experimental import pallas as pl
+from jax.experimental.pallas import tpu as pltpu
 from jax.sharding import PartitionSpec as P
 
+F32 = jnp.float32
+BF16 = jnp.bfloat16
+MESH = pl.DeviceIdType.MESH
 HEAD = 64
+EPSILON = 1e-05
+BLOCK = 128
+BAND = 384
+PAD = BAND - BLOCK
+CHUNK = 256
+SCALING = HEAD ** (-0.5)
+NT = (((1,), (1,)), ((), ()))
+TN = (((0,), (0,)), ((), ()))
+
+
+def dot(a, b):
+    return jnp.dot(a, b, preferred_element_type=F32)
+
+
+def dot_nt(a, b):
+    return lax.dot_general(a, b, NT, preferred_element_type=F32)
+
+
+def dot_tn(a, b):
+    return lax.dot_general(a, b, TN, preferred_element_type=F32)
+
+
+def rows_at(index, size):
+    return pl.ds(pl.multiple_of(index * size, size), size)
+
+
+def first_of(position, lengths, pieces):
+    first = jnp.zeros_like(position)
+    end = jnp.int32(0)
+    for piece in range(pieces - 1):
+        size = lengths[0, piece]
+        end = end + size
+        first = jnp.where(position >= end, end, first)
+    return first, position < end
+
+
+def norm_stats(x):
+    center = x - jnp.mean(x, axis=-1, keepdims=True)
+    spread = jnp.mean(center * center, axis=-1, keepdims=True)
+    return center, lax.rsqrt(spread + EPSILON)
+
+
+def remote(src, dst, send, recv, peer):
+    return pltpu.make_async_remote_copy(
+        src_ref=src, dst_ref=dst, send_sem=send, recv_sem=recv, device_id=peer, device_id_type=MESH
+    )
+
+
+def greet(peers):
+    barrier = pltpu.get_barrier_semaphore()
+    for peer in peers:
+        pl.semaphore_signal(barrier, inc=1, device_id=peer, device_id_type=MESH)
+    pl.semaphore_wait(barrier, len(peers))
+
+
+def forward_kernel(
+    pieces,
+    lengths, tokens, gain, bias, w_attn, w_out,
+    act, query, key, value, query0, key0, probs, selected, mixed, w_out_all, w_zero,
+    zero_send, zero_recv, out_send, out_recv, mix_send, mix_recv, local_sem,
+):
+    seq, width = tokens.shape
+    local = w_attn.shape[2]
+    heads = local // HEAD
+    blocks = seq // BLOCK
+    chunks = seq // CHUNK
+    mine = lax.axis_index("tensor")
+    twin = {"tensor": mine ^ 1}
+    across = {"tensor": mine ^ 2}
+    greet((twin, across))
+
+    own = pltpu.make_async_copy(w_out, w_out_all.at[mine], local_sem.at[0])
+    own.start()
+
+    def out_copy(stage, slot, peer):
+        block = w_out_all.at[slot]
+        return remote(block, block, out_send.at[stage], out_recv.at[stage], peer)
+
+    def zero_copy(stage, peer, source):
+        return remote(source, w_zero, zero_send.at[stage], zero_recv.at[0], peer)
+
+    head_cols = w_attn.at[pl.ds(0, 2), :, pl.ds(0, BLOCK)]
+
+    @pl.when(mine == 0)
+    def _():
+        zero_copy(0, across, head_cols).start()
+        zero_copy(1, twin, head_cols).start()
+        w_zero[...] = w_attn[0:2, :, 0:BLOCK]
+
+    own.wait()
+    out_copy(0, mine, across).start()
+    out_copy(1, mine, twin).start()
+
+    lane = lax.broadcasted_iota(jnp.int32, (1, local), 1)
+    for ref in (key, value, key0, selected):
+        ref[0:PAD, :] = jnp.zeros((PAD, ref.shape[1]), ref.dtype)
+
+    def project(step, carry):
+        rows = rows_at(step, CHUNK)
+        padded = pl.ds(pl.multiple_of(step * CHUNK + PAD, CHUNK), CHUNK)
+        center, scale = norm_stats(tokens[rows, :].astype(F32))
+        low = (center * scale * gain[...] + bias[...]).astype(BF16)
+        act[rows, :] = low
+        query[rows, :] = dot(low, w_attn[0]).astype(BF16)
+        key[padded, :] = dot(low, w_attn[1]).astype(BF16)
+        value[padded, :] = dot(low, w_attn[2]).astype(BF16)
+        return carry
+
+    lax.fori_loop(0, chunks, project, 0)
+
+    @pl.when(mine != 0)
+    def _():
+        zero_copy(0, twin, w_zero).wait_recv()
+
+    @pl.when(mine == 2)
+    def _():
+        zero_copy(0, twin, w_zero).start()
+
+    lane0 = lax.broadcasted_iota(jnp.int32, (1, BLOCK), 1)
+    keep0 = jnp.where(lane0 < HEAD, SCALING, 0.0)
+
+    def project0(step, carry):
+        rows = rows_at(step, CHUNK)
+        padded = pl.ds(pl.multiple_of(step * CHUNK + PAD, CHUNK), CHUNK)
+        low = act[rows, :]
+        found = dot(low, w_zero[0]).astype(BF16).astype(F32)
+        query0[rows, :] = (found * keep0).astype(BF16)
+        key0[padded, :] = dot(low, w_zero[1]).astype(BF16)
+        return carry
+
+    lax.fori_loop(0, chunks, project0, 0)
+
+    row = lax.broadcasted_iota(jnp.int32, (BLOCK, 1), 0)
+    column = lax.broadcasted_iota(jnp.int32, (1, BAND), 1) - PAD
+
+    def select(block, carry):
+        rows = rows_at(block, BLOCK)
+        first, _ = first_of(row + block * BLOCK, lengths, pieces)
+        first = first - block * BLOCK
+        band = rows_at(block, BLOCK).start
+        score = dot_nt(query0[rows, :], key0[pl.ds(band, BAND), :])
+        keep = (column > first) & (column < row)
+        selected[pl.ds(band + PAD, BLOCK), :] = jnp.where(
+            keep, jnp.maximum(score, 0.0), 0.0
+        ).astype(BF16)
+        return carry
+
+    lax.fori_loop(0, blocks, select, 0)
+
+    def mix_copy(stage, slot, block, peer):
+        part = mixed.at[slot, rows_at(block, BLOCK)]
+        return remote(part, part, mix_send.at[stage, block], mix_recv.at[stage, block], peer)
+
+    def attend(step, carry):
+        block = blocks - 1 - step
+        rows = rows_at(block, BLOCK)
+        band = rows.start
+        first, valid = first_of(row + block * BLOCK, lengths, pieces)
+        first = first - block * BLOCK
+        inside = column >= first
+        carried = (inside & (column < row)).astype(BF16)
+        parts = [
+            dot(
+                carried[:, part * BLOCK:(part + 1) * BLOCK],
+                selected[pl.ds(band + part * BLOCK, BLOCK), BAND - (part + 1) * BLOCK:],
+            )
+            for part in range(BAND // BLOCK)
+        ]
+        penalty = jnp.concatenate(
+            [
+                sum(parts[part][:, at * BLOCK:(at + 1) * BLOCK] for part in range(at, BAND // BLOCK))
+                for at in range(BAND // BLOCK)
+            ],
+            axis=1,
+        )
+        offset = jnp.where(inside & (column <= row), -penalty, -1e30)
+        queries = query[rows, :].astype(F32)
+        keys = key[pl.ds(band, BAND), :]
+        values = value[pl.ds(band, BAND), :]
+        total = jnp.zeros((BLOCK, local), F32)
+        for head in range(heads):
+            here = (lane >= head * HEAD) & (lane < (head + 1) * HEAD)
+            logits = dot_nt((queries * jnp.where(here, SCALING, 0.0)).astype(BF16), keys) + offset
+            raised = jnp.exp(logits - jnp.max(logits, axis=-1, keepdims=True))
+            low = (raised * (1.0 / jnp.sum(raised, axis=-1, keepdims=True))).astype(BF16)
+            probs[block, head] = low
+            total = jnp.where(here, dot(low, values), total)
+        mixed[mine, rows, :] = (total * valid.astype(F32)).astype(BF16)
+        mix_copy(0, mine, block, across).start()
+        mix_copy(1, mine, block, twin).start()
+        return carry
+
+    lax.fori_loop(0, blocks, attend, 0)
+
+    out_copy(0, mine ^ 2, across).wait_recv()
+    out_copy(2, mine ^ 2, twin).start()
+
+    def relay(step, carry):
+        block = blocks - 1 - step
+        mix_copy(0, mine ^ 2, block, across).wait_recv()
+        mix_copy(2, mine ^ 2, block, twin).start()
+        return carry
+
+    lax.fori_loop(0, blocks, relay, 0)
+
+    def drain(step, carry):
+        block = blocks - 1 - step
+        mix_copy(1, mine ^ 1, block, twin).wait_recv()
+        mix_copy(2, mine ^ 3, block, twin).wait_recv()
+        mix_copy(0, mine, block, across).wait_send()
+        mix_copy(1, mine, block, twin).wait_send()
+        mix_copy(2, mine ^ 2, block, twin).wait_send()
+        return carry
+
+    lax.fori_loop(0, blocks, drain, 0)
+    out_copy(1, mine ^ 1, twin).wait_recv()
+    out_copy(2, mine ^ 3, twin).wait_recv()
+    out_copy(0, mine, across).wait_send()
+    out_copy(1, mine, twin).wait_send()
+    out_copy(2, mine ^ 2, twin).wait_send()
+
+    @pl.when(mine == 0)
+    def _():
+        zero_copy(0, across, head_cols).wait_send()
+        zero_copy(1, twin, head_cols).wait_send()
+
+    @pl.when(mine == 2)
+    def _():
+        zero_copy(0, twin, w_zero).wait_send()
+
+
+VMEM = pl.BlockSpec(memory_space=pltpu.VMEM)
+SMEM = pl.BlockSpec(memory_space=pltpu.SMEM)
+DMA = pltpu.SemaphoreType.DMA
+LIMIT = 66_000_000
+
+
+def forward_call(tokens, gain, bias, w_attn, w_out, lengths):
+    seq, width = tokens.shape
+    local = w_attn.shape[2]
+    heads = local // HEAD
+    blocks = seq // BLOCK
+    shards = lax.axis_size("tensor")
+    shape = jax.ShapeDtypeStruct
+    outs = (
+        shape((seq, width), BF16),
+        shape((seq, local), BF16),
+        shape((seq + PAD, local), BF16),
+        shape((seq + PAD, local), BF16),
+        shape((seq, BLOCK), BF16),
+        shape((seq + PAD, BLOCK), BF16),
+        shape((blocks, heads, BLOCK, BAND), BF16),
+        shape((seq + PAD, BAND), BF16),
+        shape((shards, seq, local), BF16),
+        shape((shards, local, width), BF16),
+        shape((2, width, BLOCK), BF16),
+    )
+    return pl.pallas_call(
+        functools.partial(forward_kernel, lengths.shape[1]),
+        out_shape=outs,
+        in_specs=[SMEM] + [VMEM] * 5,
+        out_specs=(VMEM,) * len(outs),
+        scratch_shapes=[DMA((2,)), DMA((1,)), DMA((3,)), DMA((3,)), DMA((3, blocks)), DMA((3, blocks)), DMA((1,))],
+        compiler_params=pltpu.CompilerParams(
+            collective_id=0, has_side_effects=True, vmem_limit_bytes=LIMIT
+        ),
+        name="forward",
+    )(lengths, tokens, gain, bias, w_attn, w_out)
+
+
 SEQ = 1024
 NPIECE = 8
-
-
-EPSILON = 1e-05
 
 
 def from_root(block, axis, source):
@@ -97,22 +371,21 @@
     inputs = tokens.astype(jnp.float32)
     normed_one = normalize(inputs, gain_one, bias_one)
     act_one = normed_one.astype(jnp.bfloat16)
-    projected = jnp.einsum(
-        "rd,cde->cre", act_one, w_attn, preferred_element_type=jnp.float32
-    ).astype(jnp.bfloat16)
-    head_zero = from_root(projected[0:2, :, 0:HEAD], "tensor", 0)
-    query_all = projected[0].reshape(row_count, SEQ, local_heads, HEAD)
-    key_all = projected[1].reshape(row_count, SEQ, local_heads, HEAD)
-    value_all = projected[2].reshape(row_count, SEQ, local_heads, HEAD)
-    query_zero = head_zero[0].reshape(row_count, SEQ, HEAD)
-    key_zero = head_zero[1].reshape(row_count, SEQ, HEAD)
+    (
+        act_one, query_flat, key_flat, value_flat, query_zero, key_zero, probs_band, selected_band, mixed_all, w_out_all, _
+    ) = forward_call(
+        tokens, gain_one.reshape(1, -1), bias_one.reshape(1, -1), w_attn, w_out, piece_lengths
+    )
+    query_all = query_flat.reshape(row_count, SEQ, local_heads, HEAD)
+    key_all = key_flat[PAD:].reshape(row_count, SEQ, local_heads, HEAD)
+    value_all = value_flat[PAD:].reshape(row_count, SEQ, local_heads, HEAD)
+    query_zero = (query_zero[:, :HEAD] * 8).reshape(row_count, SEQ, HEAD)
+    key_zero = key_zero[PAD:, :HEAD].reshape(row_count, SEQ, HEAD)
     mixed, log_total = lax.map(
         forward_row, (query_all, key_all, value_all, query_zero, key_zero, piece_lengths)
     )
-    mixed = mixed.reshape(-1, local_width)
-    branch = lax.psum(
-        jnp.dot(mixed, w_out, preferred_element_type=jnp.float32).astype(jnp.bfloat16), "tensor"
-    ).astype(jnp.float32)
+    mixed = lax.dynamic_index_in_dim(mixed_all, lax.axis_index("tensor"), 0, keepdims=False)
+    branch = jnp.einsum("sre,sed->rd", mixed_all, w_out_all, preferred_element_type=jnp.float32)
     hidden_one = inputs + branch
     act_two = normalize(hidden_one, gain_two, bias_two).astype(jnp.bfloat16)
     up_all = jnp.dot(act_two, w_up, preferred_element_type=jnp.float32)

time: 624 us -> 565 us (0.905)
  waiting for transfers between devices: 406 us -> 291 us
  Pallas kernels: 0 us -> 37.6 us
  local copies, waits for them, and re-layouts: 31.6 us -> 55.7 us
  other arithmetic: 51 us -> 37.7 us
  matrix products: 72.2 us -> 80.5 us
    psum x2 -> x0, waiting for transfers between devices: 68.8 us -> none  [the longest x1 42.6 us: body(): lax.psum(jnp.dot(mixed, w_out, preferred_element_type=jnp.float32).astype...]
    pallas_call x0 -> x1, Pallas kernels: none -> 37.6 us  [forward_call(): pl.pallas_call(functools.partial(forward_kernel, lengths.shape[1]), out_s...]
    psum x1, waiting for transfers between devices: 42.2 us -> 4.99 us  [body(): lax.psum(grad_act_two.astype(jnp.bfloat16), 'tensor').astype(jnp.float32)]
    unnamed x124 -> x131, local copies, waits for them, and re-layouts: 25.8 us -> 40.3 us
    unnamed x11 -> x9, waiting for transfers between devices: 46.1 us -> 34.1 us
    reduce_sum x4 -> x3, other arithmetic: 12.7 us -> 6.97 us  [normalize(): return center * lax.rsqrt(spread + EPSILON) * gain + bias]
  transfers between devices with their start and end apart: 9 -> 7, of which waited for: 9 -> 7; matrix products, arithmetic and copies ran while one was open for 13% -> 20% of each run, Pallas kernels for 0% -> 0%
where the time goes in v1:
time: 565 us; the launch traced here: 557 us
  waiting for transfers between devices  291 us (52%)
  matrix products  80.5 us (14%)
  local copies, waits for them, and re-layouts  55.7 us (10%)
  other arithmetic  37.7 us (7%)
  Pallas kernels  37.6 us (7%)
  blocking collectives  37.4 us (7%)
  between operations  15.9 us (3%)
    reduce_scatter x1, waiting for transfers between devices, body(): lax.psum_scatter(grad_down, 'dp', scatter_dimension=1, tiled=True)  72.9 us
    reduce_scatter x1, waiting for transfers between devices, body(): lax.psum_scatter(grad_up, 'dp', scatter_dimension=0, tiled=True)  70.7 us
    psum x1, waiting for transfers between devices, body(): lax.psum(jnp.dot(hidden, w_down, preferred_element_type=jnp.float32).asty...  68.2 us
    unnamed x131, local copies, waits for them, and re-layouts  40.3 us
    psum x1, waiting for transfers between devices, backward_row(): grad_penalty = lax.psum(penalty_term.astype(jnp.bfloat16), 'tensor')  39.9 us
    pallas_call x1, Pallas kernels, forward_call(): pl.pallas_call(functools.partial(forward_kernel, lengths.shape[1]), out_s...  37.6 us
    unnamed x1, blocking collectives  37.4 us
    unnamed x9, waiting for transfers between devices  34.1 us
  transfers between devices with their start and end apart: 7, of which 7 were waited for; matrix products, arithmetic and copies ran while one was open for 20% of the time, Pallas kernels for 0%

profile of v1, /device:TPU:0, one launch (start us, length us, event | category | flops | bytes accessed | tf_op | source)
XLA Modules:
  0.0 556.7 jit_solution(1421556598852535978)
XLA Ops:
  13.8 37.6 %forward.1 = (bf16[1024,768]{1,0:T(8,128)(2,1)}, bf16[1024,192]{1,0:T(8,128)(2,1)}, bf16[1280,192]{1,0:T(8,128)(2,1)}, bf16[1280,192]{1,0:T(8,128)(2,1)}, bf16[1...) custom-call(s32[1,8]{1,0:T(1,128)} %lengths.1, ...), custom_call_target="tpu_custom_call" | custom-call | tf_op jit(solution)/shard_map/forward/pallas_call | solution.py:271
  51.4 4.3 fusion.84
  83.7 4.3 fusion.85
  100.9 5.1 convolution_convert_fusion.1
  106.0 5.0 all-reduce.10.cloned.1.call-done
  119.3 10.4 %multiply_reduce_fusion = (f32[3,1024]{1,0:T(4,128)S(1)}, f32[3,1024,1024]{1,2,0:T(8,128)}) fusion(f32[3,1024,1024]{1,2,0:T(8,128)} %copy-done, f32[3,1024]{1,0:T(4,128)S(1)} %log_add_fusion, bf16[1024,3,64]{0,2,1:T(8,128)(2,1)S(1)} %bitcast.83, bf16[1024,3,64]{0,2,1:T(8,128)(2,1)S(1)} %bitcast.77, bf16[1024]{0:T(1024)(128)(2,1)S(1)} %copy-done.43), kind=kOutput, calls=%fused_computation.1 | convolution fusion | flops 412283904 | bytes 25978880 | tf_op jit(solution)/shard_map/while/body/eval_jaxpr/ihd,jhd->hij/dot_general | solution.py:428
  131.9 10.8 %fusion.12 = (f32[1024,1024]{0,1:T(8,128)S(1)}, bf16[3,1024,1024]{1,2,0:T(8,128)(2,1)}) fusion(f32[3,1024,1024]{1,2,0:T(8,128)} %get-tuple-element.146, f32[3,1024]{1,0:T(4,128)S(1)} %get-tuple-element.145, f32[3,1024,1024]{1,2,0:T(8,128)S(1)} %bitcast.75, f32[3,1024]{1,0:T(4,128)S(1)} %log_add_fusion), kind=kLoop, calls=%fused_computation.36 | loop fusion | flops 14680064 | bytes 35676160 | tf_op jit(solution)/shard_map/while/body/eval_jaxpr/reduce_sum | solution.py:436
  148.4 7.8 %fusion.51 = bf16[3,64,1024]{2,1,0:T(8,128)(2,1)} fusion(f32[3,1024,1024]{1,2,0:T(8,128)} %copy-done, f32[3,1024]{1,0:T(4,128)S(1)} %log_add_fusion, bf16[1024,3,64]{0,2,1:T(8,128)(2,1)S(1)} %bitcast.78, bf16[1024]{0:T(1024)(128)(2,1)} %convert_convert_fusion), kind=kOutput, calls=%fused_computation.82 | convolution fusion | flops 409337856 | bytes 13383680 | tf_op jit(solution)/shard_map/while/body/eval_jaxpr/hij,ihd->jhd/dot_general | solution.py:431
  156.2 39.9 %all-reduce.12.cloned.1.call-done = bf16[1024,1024]{0,1:T(8,128)(2,1)} async-done(((bf16[1024,1024]{0,1:T(8,128)(2,1)}), bf16[1024,1024]{0,1:T(8,128)(2,1)}) %all-reduce.12.cloned.1.call-update) | async-done | bytes 2097168 | tf_op jit(solution)/shard_map/while/body/eval_jaxpr/psum | solution.py:437
  196.2 5.9 %select_convert_fusion = bf16[1024,1024]{1,0:T(8,128)(2,1)S(1)} fusion(f32[1024,1024]{1,0:T(8,128)} %copy-done.8, bf16[1024,1024]{0,1:T(8,128)(2,1)} %all-reduce.12.cloned.1.call-done, s32[1024]{0:T(1024)} %copy-done.35, pred[1024]{0:T(1024)(128)(4,1)} %copy-done.48), kind=kOutput, calls=%fused_computation.27 | convolution fusion | flops 2161115136 | bytes 8393728 | tf_op jit(solution)/shard_map/while/body/eval_jaxpr/ik,ij->kj/dot_general | solution.py:447
  203.5 4.9 fusion.49
  208.4 4.2 fusion.50
  216.0 4.0 fusion.42
  220.0 4.2 copy.104
  224.3 4.7 reshape.220
  229.3 4.8 fusion.87
  234.1 5.9 %fusion.55 = f32[768,768]{0,1:T(8,128)} fusion(f32[1024,768]{1,0:T(8,128)} %param.21, f32[1024,768]{1,0:T(8,128)} %copy-done.53), kind=kOutput, calls=%fused_computation.88 | convolution fusion | flops 1215823872 | bytes 8650752 | tf_op jit(solution)/shard_map/rf,rd->fd/dot_general | solution.py:399
  243.0 19.8 %reduce-scatter.15.cloned.1.call-done = f32[96,192]{1,0:T(8,128)} async-done(((f32[768,192]{1,0:T(8,128)}), f32[96,192]{1,0:T(8,128)}) %reduce-scatter.15.cloned.1.call-update) | async-done | bytes 73744
  264.5 68.2 %all-reduce.14.cloned.1.call-done = (bf16[1024,768]{0,1:T(8,128)(2,1)}, bf16[1024,768]{0,1:T(8,128)(2,1)}) async-done(((bf16[1024,768]{0,1:T(8,128)(2,1)}, bf16[1024,768]{0,1:T(8,128)(2,1)}), (bf16[1024,768]{0,1:T(8,128)(2,1)}, bf16[1024,768]{0,1:T(8,128)(2,1)})) %all-reduce.14.cloned.1.call-update) | async-done | bytes 3145744 | tf_op jit(solution)/shard_map/psum | solution.py:393
  337.6 37.4 %all-reduce.4 = (f32[768]{0:T(1024)S(1)}, f32[768]{0:T(1024)S(1)}, f32[768]{0:T(1024)S(1)}, f32[768]{0:T(1024)S(1)}) all-reduce(f32[768]{0:T(1024)S(1)} %get-tuple-element.122, f32[768]{0:T(1024)S(1)} %get-tuple-element.126, f32[768]{0:T(1024)S(1)} %copy-done.45, f32[768]{0:T(1024)S(1)} %copy-done.44), channel_id=6, replica_groups=mesh['dp'=8,'tensor'=4] {'dp'}, use_global_device_ids=true, to_apply=%region_24.25.clone | all-reduce | flops 3072 | bytes 24576
  377.4 6.4 %add_add_fusion.2 = (f32[1024,768]{0,1:T(8,128)}, f32[1024,768]{0,1:T(8,128)}) fusion(bf16[1024,768]{0,1:T(8,128)(2,1)} %copy.77, bf16[1024,768]{0,1:T(8,128)(2,1)} %get-tuple-element.134, f32[1024]{0:T(1024)S(1)} %negate_multiply_fusion, f32[1024]{0:T(1024)S(1)} %get-tuple-element.139, f32[1024]{0:T(1024)S(1)} %get-tuple-element.140, ...), kind=kLoop, calls=%fused_computation.51 | loop fusion | flops 16515072 | bytes 18913280 | tf_op jit(solution)/shard_map/add | solution.py:473
  389.8 14.2 %reduce-scatter.13.cloned.1.call-done = f32[96,576]{1,0:T(8,128)} async-done(((f32[768,576]{1,0:T(8,128)}), f32[96,576]{1,0:T(8,128)}) %reduce-scatter.13.cloned.1.call-update) | async-done | bytes 221200
  405.9 70.7 %reduce-scatter.9.cloned.1.call-done = f32[96,768]{1,0:T(8,128)} async-done(((f32[768,768]{1,0:T(8,128)}), f32[96,768]{1,0:T(8,128)}) %reduce-scatter.9.cloned.1.call-update) | async-done | bytes 294928 | tf_op jit(solution)/shard_map/reduce_scatter | solution.py:477
  476.5 72.9 %reduce-scatter.11.cloned.1.call-done = f32[768,96]{0,1:T(8,128)} async-done(((f32[768,768]{0,1:T(8,128)}), f32[768,96]{0,1:T(8,128)}) %reduce-scatter.11.cloned.1.call-update) | async-done | bytes 294928 | tf_op jit(solution)/shard_map/reduce_scatter | solution.py:478
  (188 shorter events, 87.6 us)
Async XLA Ops:
  7.2 103.8 %all-reduce.10.cloned.1.call-start = ((), (), s32[]{:S(2)}) async-start(), calls=%async_computation.4 | async-start | bytes 3145728 | tf_op jit(solution)/shard_map/psum | solution.py:408
  67.7 128.5 %all-reduce.12.cloned.1.call-start = ((), (), s32[]{:S(2)}) async-start(), calls=%async_computation.5 | async-start | bytes 4194304 | tf_op jit(solution)/shard_map/while/body/eval_jaxpr/psum | solution.py:437
  68.5 21.3 %copy-start.35 = (s32[1024]{0:T(1024)}, s32[1024]{0:T(1024)S(1)}, u32[]{:S(2)}) copy-start(s32[1024]{0:T(1024)S(1)} %convert_reduce_fusion.3) | copy-start | bytes 12292
  70.1 10.8 %copy-start.48 = (pred[1024]{0:T(1024)(128)(4,1)}, pred[1024]{0:T(1024)(128)(4,1)S(1)}, u32[]{:S(2)}) copy-start(pred[1024]{0:T(1024)(128)(4,1)S(1)} %iota_compare_fusion.4) | copy-start | bytes 3076
  93.3 7.6 %copy-start.28 = (f32[3,1024]{1,0:T(4,128)S(1)}, f32[3,1024]{1,0:T(4,128)}, u32[]{:S(2)}) copy-start(f32[3,1024]{1,0:T(4,128)} %copy-done.27) | copy-start | bytes 36868
  100.9 10.1 %copy-start.25 = (f32[1024]{0:T(1024)S(1)}, f32[1024]{0:T(1024)}, u32[]{:S(2)}) copy-start(f32[1024]{0:T(1024)} %copy-done.24) | copy-start | bytes 12292
  100.9 10.1 %copy-start.30 = (f32[768]{0:T(1024)S(1)}, f32[768]{0:T(1024)}, u32[]{:S(2)}) copy-start(f32[768]{0:T(1024)} %param.16) | copy-start | bytes 9220
  106.0 8.1 %copy-start.42 = (f32[1024]{0:T(1024)S(1)}, f32[1024]{0:T(1024)}, u32[]{:S(2)}) copy-start(f32[1024]{0:T(1024)} %copy-done.41) | copy-start | bytes 12292
  106.0 8.1 %copy-start.33 = (f32[1024]{0:T(1024)S(1)}, f32[1024]{0:T(1024)}, u32[]{:S(2)}) copy-start(f32[1024]{0:T(1024)} %copy-done.32) | copy-start | bytes 12292
  119.2 10.4 %slice-start = ((s8[12582912]{0:T(1024)(128)(4,1)}), s8[4194304]{0:T(1024)(128)(4,1)S(1)}, s32[]{:S(2)}) async-start(s8[12582912]{0:T(1024)(128)(4,1)} %bitcast.74), calls=%async_computation.11 | async-start | bytes 8388608
  119.2 11.4 %slice-start.1 = ((s8[12582912]{0:T(1024)(128)(4,1)}), s8[4194304]{0:T(1024)(128)(4,1)S(1)}, s32[]{:S(2)}) async-start(s8[12582912]{0:T(1024)(128)(4,1)} %bitcast.74), calls=%async_computation.12 | async-start | bytes 8388608
  119.3 12.6 %slice-start.2 = ((s8[12582912]{0:T(1024)(128)(4,1)}), s8[4194304]{0:T(1024)(128)(4,1)S(1)}, s32[]{:S(2)}) async-start(s8[12582912]{0:T(1024)(128)(4,1)} %bitcast.74), calls=%async_computation.13 | async-start | bytes 8388608
  144.6 118.3 %reduce-scatter.15.cloned.1.call-start = ((), (), s32[]{:S(2)}) async-start(), calls=%async_computation.9 | async-start | bytes 884736
  156.2 46.7 %copy-start.18 = (bf16[1024,128]{1,0:T(8,128)(2,1)S(1)}, bf16[1024,128]{1,0:T(8,128)(2,1)}, u32[]{:S(2)}) copy-start(bf16[1024,128]{1,0:T(8,128)(2,1)} %get-tuple-element.76) | copy-start | bytes 786436
  156.2 176.4 %all-reduce.14.cloned.1.call-start = ((), (), s32[]{:S(2)}) async-start(), calls=%async_computation.10 | async-start | bytes 6291456 | tf_op jit(solution)/shard_map/psum | solution.py:393
  216.0 188.0 %reduce-scatter.13.cloned.1.call-start = ((), (), s32[]{:S(2)}) async-start(), calls=%async_computation.8 | async-start | bytes 2211840
  229.0 247.6 %reduce-scatter.9.cloned.1.call-start = ((), (), s32[]{:S(2)}) async-start(), calls=%async_computation.6 | async-start | bytes 2654208 | tf_op jit(solution)/shard_map/reduce_scatter | solution.py:477
  234.1 315.3 %reduce-scatter.11.cloned.1.call-start = ((), (), s32[]{:S(2)}) async-start(), calls=%async_computation.7 | async-start | bytes 2654208 | tf_op jit(solution)/shard_map/reduce_scatter | solution.py:478
  240.0 92.6 %copy-start.36 = (f32[768]{0:T(1024)S(1)}, f32[768]{0:T(1024)}, u32[]{:S(2)}) copy-start(f32[768]{0:T(1024)} %param.12) | copy-start | bytes 9220
  332.6 44.7 %copy-start.26 = (f32[1024]{0:T(1024)S(1)}, f32[1024]{0:T(1024)}, u32[]{:S(2)}) copy-start(f32[1024]{0:T(1024)} %copy-done.24) | copy-start | bytes 12292
  332.7 44.7 %copy-start.31 = (f32[768]{0:T(1024)S(1)}, f32[768]{0:T(1024)}, u32[]{:S(2)}) copy-start(f32[768]{0:T(1024)} %param.16) | copy-start | bytes 9220
  332.7 44.7 %copy-start.34 = (f32[1024]{0:T(1024)S(1)}, f32[1024]{0:T(1024)}, u32[]{:S(2)}) copy-start(f32[1024]{0:T(1024)} %copy-done.32) | copy-start | bytes 12292
  332.7 44.7 %copy-start.38 = (f32[1024]{0:T(1024)S(1)}, f32[1024]{0:T(1024)}, u32[]{:S(2)}) copy-start(f32[1024]{0:T(1024)} %copy-done.37) | copy-start | bytes 12292
  332.7 44.7 %copy-start.40 = (f32[1024]{0:T(1024)S(1)}, f32[1024]{0:T(1024)}, u32[]{:S(2)}) copy-start(f32[1024]{0:T(1024)} %copy-done.39) | copy-start | bytes 12292
  (41 other events, 117.1 us)
Sparse Core Ops, SparseCore 0:
  67.8 43.1 all-reduce.9
  144.7 51.4 all-reduce.11
  199.5 63.3 reduce-scatter.14
  265.1 67.4 all-reduce.13
  335.9 67.9 reduce-scatter.12
  407.9 68.5 reduce-scatter.8
  480.6 68.7 reduce-scatter.10

commit v2 on v1

v2 whole, which is shorter than its diff:
```python
import functools

import jax
import jax.numpy as jnp
from jax import lax
from jax.experimental import pallas as pl
from jax.experimental.pallas import tpu as pltpu
from jax.sharding import PartitionSpec as P

F32 = jnp.float32
BF16 = jnp.bfloat16
MESH = pl.DeviceIdType.MESH
HEAD = 64
EPSILON = 1e-05
BLOCK = 128
BAND = 384
PAD = BAND - BLOCK
CHUNK = 256
SCALING = HEAD ** (-0.5)
NT = (((1,), (1,)), ((), ()))
TN = (((0,), (0,)), ((), ()))


def dot(a, b):
    return jnp.dot(a, b, preferred_element_type=F32)


def dot_nt(a, b):
    return lax.dot_general(a, b, NT, preferred_element_type=F32)


def dot_tn(a, b):
    return lax.dot_general(a, b, TN, preferred_element_type=F32)


def rows_at(index, size):
    return pl.ds(pl.multiple_of(index * size, size), size)


def first_of(position, lengths, pieces):
    first = jnp.zeros_like(position)
    end = jnp.int32(0)
    for piece in range(pieces - 1):
        size = lengths[0, piece]
        end = end + size
        first = jnp.where(position >= end, end, first)
    return first, position < end


def norm_stats(x):
    center = x - jnp.mean(x, axis=-1, keepdims=True)
    spread = jnp.mean(center * center, axis=-1, keepdims=True)
    return center, lax.rsqrt(spread + EPSILON)


def remote(src, dst, send, recv, peer):
    return pltpu.make_async_remote_copy(
        src_ref=src, dst_ref=dst, send_sem=send, recv_sem=recv, device_id=peer, device_id_type=MESH
    )


def greet(peers):
    barrier = pltpu.get_barrier_semaphore()
    for peer in peers:
        pl.semaphore_signal(barrier, inc=1, device_id=peer, device_id_type=MESH)
    pl.semaphore_wait(barrier, len(peers))


def forward_kernel(
    pieces,
    lengths, tokens, gain, bias, w_attn, w_out,
    act, query, key, value, query0, key0, probs, selected, mixed, w_out_all, w_zero,
    zero_send, zero_recv, out_send, out_recv, mix_send, mix_recv, local_sem,
):
    seq, width = tokens.shape
    local = w_attn.shape[2]
    heads = local // HEAD
    blocks = seq // BLOCK
    chunks = seq // CHUNK
    mine = lax.axis_index("tensor")
    twin = {"tensor": mine ^ 1}
    across = {"tensor": mine ^ 2}
    greet((twin, across))

    own = pltpu.make_async_copy(w_out, w_out_all.at[mine], local_sem.at[0])
    own.start()

    def out_copy(stage, slot, peer):
        block = w_out_all.at[slot]
        return remote(block, block, out_send.at[stage], out_recv.at[stage], peer)

    def zero_copy(stage, peer, source):
        return remote(source, w_zero, zero_send.at[stage], zero_recv.at[0], peer)

    head_cols = w_attn.at[pl.ds(0, 2), :, pl.ds(0, BLOCK)]

    @pl.when(mine == 0)
    def _():
        zero_copy(0, across, head_cols).start()
        zero_copy(1, twin, head_cols).start()
        w_zero[...] = w_attn[0:2, :, 0:BLOCK]

    own.wait()
    out_copy(0, mine, across).start()
    out_copy(1, mine, twin).start()

    lane = lax.broadcasted_iota(jnp.int32, (1, local), 1)
    for ref in (key, value, key0, selected):
        ref[0:PAD, :] = jnp.zeros((PAD, ref.shape[1]), ref.dtype)

    def project(step, carry):
        rows = rows_at(step, CHUNK)
        padded = pl.ds(pl.multiple_of(step * CHUNK + PAD, CHUNK), CHUNK)
        center, scale = norm_stats(tokens[rows, :].astype(F32))
        low = (center * scale * gain[...] + bias[...]).astype(BF16)
        act[rows, :] = low
        query[rows, :] = dot(low, w_attn[0]).astype(BF16)
        key[padded, :] = dot(low, w_attn[1]).astype(BF16)
        value[padded, :] = dot(low, w_attn[2]).astype(BF16)
        return carry

    lax.fori_loop(0, chunks, project, 0)

    @pl.when(mine != 0)
    def _():
        zero_copy(0, twin, w_zero).wait_recv()

    @pl.when(mine == 2)
    def _():
        zero_copy(0, twin, w_zero).start()

    lane0 = lax.broadcasted_iota(jnp.int32, (1, BLOCK), 1)
    keep0 = jnp.where(lane0 < HEAD, SCALING, 0.0)

    def project0(step, carry):
        rows = rows_at(step, CHUNK)
        padded = pl.ds(pl.multiple_of(step * CHUNK + PAD, CHUNK), CHUNK)
        low = act[rows, :]
        found = dot(low, w_zero[0]).astype(BF16).astype(F32)
        query0[rows, :] = (found * keep0).astype(BF16)
        key0[padded, :] = dot(low, w_zero[1]).astype(BF16)
        return carry

    lax.fori_loop(0, chunks, project0, 0)

    row = lax.broadcasted_iota(jnp.int32, (BLOCK, 1), 0)
    column = lax.broadcasted_iota(jnp.int32, (1, BAND), 1) - PAD

    def select(block, carry):
        rows = rows_at(block, BLOCK)
        first, _ = first_of(row + block * BLOCK, lengths, pieces)
        first = first - block * BLOCK
        band = rows_at(block, BLOCK).start
        score = dot_nt(query0[rows, :], key0[pl.ds(band, BAND), :])
        keep = (column > first) & (column < row)
        selected[pl.ds(band + PAD, BLOCK), :] = jnp.where(
            keep, jnp.maximum(score, 0.0), 0.0
        ).astype(BF16)
        return carry

    lax.fori_loop(0, blocks, select, 0)

    def mix_copy(stage, slot, block, peer):
        part = mixed.at[slot, rows_at(block, BLOCK)]
        return remote(part, part, mix_send.at[stage, block], mix_recv.at[stage, block], peer)

    def attend(step, carry):
        block = blocks - 1 - step
        rows = rows_at(block, BLOCK)
        band = rows.start
        first, valid = first_of(row + block * BLOCK, lengths, pieces)
        first = first - block * BLOCK
        inside = column >= first
        carried = (inside & (column < row)).astype(BF16)
        parts = [
            dot(
                carried[:, part * BLOCK:(part + 1) * BLOCK],
                selected[pl.ds(band + part * BLOCK, BLOCK), BAND - (part + 1) * BLOCK:],
            )
            for part in range(BAND // BLOCK)
        ]
        penalty = jnp.concatenate(
            [
                sum(parts[part][:, at * BLOCK:(at + 1) * BLOCK] for part in range(at, BAND // BLOCK))
                for at in range(BAND // BLOCK)
            ],
            axis=1,
        )
        offset = jnp.where(inside & (column <= row), -penalty, -1e30)
        queries = query[rows, :].astype(F32)
        keys = key[pl.ds(band, BAND), :]
        values = value[pl.ds(band, BAND), :]
        total = jnp.zeros((BLOCK, local), F32)
        for head in range(heads):
            here = (lane >= head * HEAD) & (lane < (head + 1) * HEAD)
            logits = dot_nt((queries * jnp.where(here, SCALING, 0.0)).astype(BF16), keys) + offset
            raised = jnp.exp(logits - jnp.max(logits, axis=-1, keepdims=True))
            low = (raised * (1.0 / jnp.sum(raised, axis=-1, keepdims=True))).astype(BF16)
            probs[block, head] = low
            total = jnp.where(here, dot(low, values), total)
        mixed[mine, rows, :] = (total * valid.astype(F32)).astype(BF16)
        mix_copy(0, mine, block, across).start()
        mix_copy(1, mine, block, twin).start()
        return carry

    lax.fori_loop(0, blocks, attend, 0)

    out_copy(0, mine ^ 2, across).wait_recv()
    out_copy(2, mine ^ 2, twin).start()

    def relay(step, carry):
        block = blocks - 1 - step
        mix_copy(0, mine ^ 2, block, across).wait_recv()
        mix_copy(2, mine ^ 2, block, twin).start()
        return carry

    lax.fori_loop(0, blocks, relay, 0)

    def drain(step, carry):
        block = blocks - 1 - step
        mix_copy(1, mine ^ 1, block, twin).wait_recv()
        mix_copy(2, mine ^ 3, block, twin).wait_recv()
        mix_copy(0, mine, block, across).wait_send()
        mix_copy(1, mine, block, twin).wait_send()
        mix_copy(2, mine ^ 2, block, twin).wait_send()
        return carry

    lax.fori_loop(0, blocks, drain, 0)
    out_copy(1, mine ^ 1, twin).wait_recv()
    out_copy(2, mine ^ 3, twin).wait_recv()
    out_copy(0, mine, across).wait_send()
    out_copy(1, mine, twin).wait_send()
    out_copy(2, mine ^ 2, twin).wait_send()

    @pl.when(mine == 0)
    def _():
        zero_copy(0, across, head_cols).wait_send()
        zero_copy(1, twin, head_cols).wait_send()

    @pl.when(mine == 2)
    def _():
        zero_copy(0, twin, w_zero).wait_send()


VMEM = pl.BlockSpec(memory_space=pltpu.VMEM)
SMEM = pl.BlockSpec(memory_space=pltpu.SMEM)
DMA = pltpu.SemaphoreType.DMA
LIMIT = 67_000_000


def forward_call(tokens, gain, bias, w_attn, w_out, lengths):
    seq, width = tokens.shape
    local = w_attn.shape[2]
    heads = local // HEAD
    blocks = seq // BLOCK
    shards = lax.axis_size("tensor")
    shape = jax.ShapeDtypeStruct
    outs = (
        shape((seq, width), BF16),
        shape((seq, local), BF16),
        shape((seq + PAD, local), BF16),
        shape((seq + PAD, local), BF16),
        shape((seq, BLOCK), BF16),
        shape((seq + PAD, BLOCK), BF16),
        shape((blocks, heads, BLOCK, BAND), BF16),
        shape((seq + PAD, BAND), BF16),
        shape((shards, seq, local), BF16),
        shape((shards, local, width), BF16),
        shape((2, width, BLOCK), BF16),
    )
    return pl.pallas_call(
        functools.partial(forward_kernel, lengths.shape[1]),
        out_shape=outs,
        in_specs=[SMEM] + [VMEM] * 5,
        out_specs=(VMEM,) * len(outs),
        scratch_shapes=[DMA((2,)), DMA((1,)), DMA((3,)), DMA((3,)), DMA((3, blocks)), DMA((3, blocks)), DMA((1,))],
        compiler_params=pltpu.CompilerParams(
            collective_id=0, has_side_effects=True, vmem_limit_bytes=LIMIT
        ),
        name="forward",
    )(lengths, tokens, gain, bias, w_attn, w_out)


GELU_ROOT = 0.7978845608028654
GELU_CUBE = 0.044715


def bit_reverse(value, bits):
    return sum(((value >> at) & 1) << (bits - 1 - at) for at in range(bits))


def groups_of_eight(x):
    return jnp.sum(x.reshape(x.shape[0] // 8, 8, x.shape[1]), axis=0)


class Sum:
    def __init__(self, source, pair, other, result, send, recv):
        self.refs = source, pair, other, result
        self.send, self.recv = send, recv
        mine = lax.axis_index("tensor")
        self.core = mine & 1
        self.twin, self.across = {"tensor": mine ^ 1}, {"tensor": mine ^ 2}

    def half(self, chunk, core):
        return pl.ds(pl.multiple_of(chunk * CHUNK + core * BLOCK, BLOCK), BLOCK)

    def copy(self, stage, chunk):
        source, pair, other, result = self.refs
        own, theirs = self.half(chunk, self.core), self.half(chunk, 1 - self.core)
        src, dst, peer = (
            (source.at[theirs], pair.at[chunk], self.twin),
            (pair.at[chunk], other.at[chunk], self.across),
            (result.at[own], result.at[own], self.twin),
        )[stage]
        return remote(src, dst, self.send.at[stage, chunk], self.recv.at[stage, chunk], peer)

    def first(self, chunk):
        self.copy(0, chunk).start()

    def second(self, chunk):
        source, pair, other, result = self.refs
        self.copy(0, chunk).wait_recv()
        own = source[self.half(chunk, self.core), :].astype(F32)
        pair[chunk] = (own + pair[chunk].astype(F32)).astype(BF16)
        self.copy(1, chunk).start()

    def third(self, chunk):
        source, pair, other, result = self.refs
        self.copy(1, chunk).wait_recv()
        total = pair[chunk].astype(F32) + other[chunk].astype(F32)
        result[self.half(chunk, self.core), :] = total.astype(BF16)
        self.copy(2, chunk).start()

    def ready(self, chunk):
        self.copy(2, chunk).wait_recv()

    def drain(self, chunks):
        def one(chunk, carry):
            for stage in range(3):
                self.copy(stage, chunk).wait_send()
            return carry

        lax.fori_loop(0, chunks, one, 0)


class Scatter:
    def __init__(self, start, lands, send, recv):
        self.refs = (start, *lands)
        self.send, self.recv = send, recv
        self.parts = start.shape[0]
        self.me = lax.axis_index("dp")

    def copy(self, level):
        size = self.parts >> (level + 1)
        bit = (self.me >> level) & 1
        return remote(
            self.refs[level].at[pl.ds((1 - bit) * size, size)],
            self.refs[level + 1],
            self.send.at[level],
            self.recv.at[level],
            {"dp": self.me ^ (1 << level)},
        )

    def go(self, level):
        self.copy(level).start()

    def add(self, level):
        size = self.parts >> (level + 1)
        bit = (self.me >> level) & 1
        here, landed = self.refs[level], self.refs[level + 1]
        self.copy(level).wait_recv()

        def one(part, carry):
            total = here[bit * size + part].astype(F32) + landed[part].astype(F32)
            landed[part] = total.astype(landed.dtype)
            return carry

        lax.fori_loop(0, size, one, 0)

    def drain(self):
        for level in range(len(self.refs) - 1):
            self.copy(level).wait_send()


def backward_kernel(
    pieces, levels,
    lengths, tokens, gain_one, gain_two, bias_two, w_attn, w_up, w_down, cotangent,
    act, query, key, value, query0, key0, probs, selected, mixed, w_out_all, w_zero,
    out_delta, grad_in, out_attn, out_out, out_up, out_down, out_gains,
    hidden_one, act_two, hidden, grad_pre, grad_branch, grad_mixed,
    feed_s, feed_a, feed_b, two_s, two_a, two_b, two_r, one_s, one_a, one_b, one_r,
    grad_key, grad_value, grad_sel, grad_key0, grad_proj, gain_sum, grad_query0,
    exchange, *rest,
):
    seq, width = tokens.shape
    local = w_attn.shape[2]
    heads = local // HEAD
    blocks, chunks = seq // BLOCK, seq // CHUNK
    parts = 1 << levels
    own_rows = width // parts
    rest = list(rest)
    take = lambda count: [rest.pop(0) for _ in range(count)]
    mlp_refs, attn_refs, gain_refs = take(levels + 1), take(levels + 1), take(levels + 1)
    sums_send, sums_recv, scat_send, scat_recv, ex_send, ex_recv = take(6)
    mine = lax.axis_index("tensor")
    me = lax.axis_index("dp")
    peers = [{"tensor": mine ^ step} for step in (1, 2, 3)]
    greet(tuple(peers) + tuple({"dp": me ^ (1 << level)} for level in range(levels)))

    feed = Sum(feed_s, feed_a, feed_b, out_delta, sums_send.at[0], sums_recv.at[0])
    two = Sum(two_s, two_a, two_b, two_r, sums_send.at[1], sums_recv.at[1])
    one = Sum(one_s, one_a, one_b, one_r, sums_send.at[2], sums_recv.at[2])
    mlp = Scatter(mlp_refs[0], mlp_refs[1:], scat_send.at[0], scat_recv.at[0])
    attn = Scatter(attn_refs[0], attn_refs[1:], scat_send.at[1], scat_recv.at[1])
    gains = Scatter(gain_refs[0], gain_refs[1:], scat_send.at[2], scat_recv.at[2])

    for ref in (grad_key, grad_value, grad_sel, grad_key0):
        ref[...] = jnp.zeros(ref.shape, ref.dtype)
    gain_sum[...] = jnp.zeros(gain_sum.shape, F32)

    def feed_forward(step, carry):
        chunk = chunks - 1 - step
        rows = rows_at(chunk, CHUNK)
        branch = sum(dot(mixed[shard, rows, :], w_out_all[shard]) for shard in range(mixed.shape[0]))
        after = tokens[rows, :].astype(F32) + branch
        hidden_one[rows, :] = after
        center, scale = norm_stats(after)
        low = (center * scale * gain_two[...] + bias_two[...]).astype(BF16)
        act_two[rows, :] = low
        up = dot(low, w_up[...])
        square = up * up
        bent = jnp.tanh(GELU_ROOT * (up + GELU_CUBE * (square * up)))
        units = (0.5 * up * (1.0 + bent)).astype(BF16)
        hidden[rows, :] = units
        slope = 0.5 * (1.0 + bent) + (0.5 * GELU_ROOT) * up * (1.0 - bent * bent) * (
            1.0 + (3.0 * GELU_CUBE) * square
        )
        low_cot = cotangent[rows, :].astype(BF16)
        before = (dot_nt(low_cot, w_down[...]) * slope).astype(BF16)
        grad_pre[rows, :] = before
        two_s[rows, :] = dot_nt(before, w_up[...]).astype(BF16)
        two.first(chunk)
        feed_s[rows, :] = (dot(units, w_down[...]) + branch * (1.0 / mixed.shape[0])).astype(BF16)
        feed.first(chunk)

        @pl.when(step > 0)
        def _():
            two.second(chunk + 1)

        return carry

    lax.fori_loop(0, chunks, feed_forward, 0)
    two.second(0)

    def spread(target, columns, found, offset):
        for at in range(found.shape[0] // own_rows):
            part = bit_reverse(offset // own_rows + at, levels)
            target[part, :, columns[0]:columns[1]] = found[at * own_rows:(at + 1) * own_rows].astype(BF16)

    half = width // 2
    for strip in range(2):
        cut = slice(strip * half, (strip + 1) * half)
        spread(mlp_refs[0], (0, w_up.shape[1]), dot_tn(act_two[:, cut], grad_pre[...]), strip * half)
        spread(
            mlp_refs[0], (w_up.shape[1], 2 * w_up.shape[1]),
            dot_tn(cotangent[:, cut].astype(BF16), hidden[...]), strip * half,
        )
    mlp.go(0)

    row = lax.broadcasted_iota(jnp.int32, (BLOCK, 1), 0)
    across_row = lax.broadcasted_iota(jnp.int32, (1, BLOCK), 1)
    down_band = lax.broadcasted_iota(jnp.int32, (BAND, 1), 0) - PAD
    lane = lax.broadcasted_iota(jnp.int32, (1, local), 1)
    here = [(lane >= head * HEAD) & (lane < (head + 1) * HEAD) for head in range(heads)]
    lane0 = lax.broadcasted_iota(jnp.int32, (1, BLOCK), 1)

    def pick(found):
        total = found[-1]
        for head in range(heads - 1):
            total = jnp.where(here[head], found[head], total)
        return total

    def attend_back(block):
        rows = rows_at(block, BLOCK)
        band = pl.ds(rows.start, BAND)
        first, _ = first_of(across_row + block * BLOCK, lengths, pieces)
        first = first - block * BLOCK
        carried = ((down_band >= first) & (down_band < across_row)).astype(BF16)
        grads = grad_mixed[rows, :]
        wide = grads.astype(F32)
        queries, keys, values = query[rows, :], key[band, :], value[band, :]
        loss = jnp.zeros((BLOCK, BAND), F32)
        queried, keyed, valued = [], [], []
        for head in range(heads):
            low = probs[block, head]
            chance = low.astype(F32)
            grad = dot_nt((wide * here[head].astype(F32)).astype(BF16), values)
            inner = jnp.sum(chance * grad, axis=-1, keepdims=True)
            logits = chance * (grad - inner)
            loss = loss - logits
            logits = logits.astype(BF16)
            queried.append(dot(logits, keys))
            keyed.append(dot_tn(logits, queries))
            valued.append(dot_tn(low, grads))
        grad_key[band, :] = grad_key[band, :] + pick(keyed)
        grad_value[band, :] = grad_value[band, :] + pick(valued)
        loss = loss.astype(BF16)
        for part in range(BAND // BLOCK):
            reach = (part + 1) * BLOCK
            rows_k = pl.ds(pl.multiple_of(rows.start + part * BLOCK, BLOCK), BLOCK)
            grad_sel[rows_k, BAND - reach:] = grad_sel[rows_k, BAND - reach:] + dot(
                carried[part * BLOCK:(part + 1) * BLOCK], loss[:, :reach]
            )
        own = pl.ds(pl.multiple_of(rows.start + PAD, BLOCK), BLOCK)
        score = jnp.where(selected[own, :] > 0, grad_sel[own, :], 0.0).astype(BF16)
        from_key = dot(score, key0[band, :])
        grad_query0[rows, :] = jnp.where(lane0 < HEAD, from_key * SCALING, 0.0).astype(BF16)
        grad_key0[band, :] = grad_key0[band, :] + dot_tn(score, query0[rows, :])
        return (pick(queried) * SCALING).astype(BF16)

    def back(step, carry):
        chunk = chunks - 1 - step
        rows = rows_at(chunk, CHUNK)
        padded = pl.ds(pl.multiple_of(chunk * CHUNK + PAD, CHUNK), CHUNK)
        two.third(chunk)
        center, scale = norm_stats(hidden_one[rows, :])
        unit = center * scale
        two.ready(chunk)
        grad = two_r[rows, :].astype(F32)
        gain_sum[2] = gain_sum[2] + groups_of_eight(grad * unit)
        gain_sum[3] = gain_sum[3] + groups_of_eight(grad)
        e = grad * gain_two[...]
        total = cotangent[rows, :] + scale * (
            e - jnp.mean(e, axis=-1, keepdims=True) - unit * jnp.mean(e * unit, axis=-1, keepdims=True)
        )
        hidden_one[rows, :] = total
        low = total.astype(BF16)
        grad_branch[rows, :] = low
        position = lax.broadcasted_iota(jnp.int32, (CHUNK, 1), 0) + chunk * CHUNK
        _, valid = first_of(position, lengths, pieces)
        grad_mixed[rows, :] = (
            dot_nt(low, w_out_all[mine]).astype(BF16).astype(F32) * valid.astype(F32)
        ).astype(BF16)
        upper = attend_back(2 * chunk + 1)
        lower = attend_back(2 * chunk)
        grad_q = jnp.concatenate([lower, upper], axis=0)
        grad_k = (grad_key[padded, :] * SCALING).astype(BF16)
        grad_v = grad_value[padded, :].astype(BF16)
        grad_q0 = grad_query0[rows, :]
        grad_k0 = grad_key0[padded, :]
        extra = grad_q0.astype(F32) + pltpu.roll(grad_k0, HEAD, 1)
        grad_proj[rows, :] = jnp.concatenate(
            [extra, grad_q.astype(F32), grad_k.astype(F32), grad_v.astype(F32)], axis=1
        ).astype(BF16)
        partial = (
            dot_nt(grad_q, w_attn[0])
            + dot_nt(grad_k, w_attn[1])
            + dot_nt(grad_v, w_attn[2])
            + dot_nt(grad_q0, w_zero[0])
            + dot_nt(grad_k0.astype(BF16), w_zero[1])
        )
        one_s[rows, :] = partial.astype(BF16)
        one.first(chunk)
        center, scale = norm_stats(tokens[rows, :].astype(F32))
        gain_sum[0] = gain_sum[0] + groups_of_eight(partial * (center * scale))
        gain_sum[1] = gain_sum[1] + groups_of_eight(partial)

        @pl.when(step > 0)
        def _():
            one.second(chunk + 1)

        feed.second(chunk)
        return carry

    lax.fori_loop(0, chunks, back, 0)
    one.second(0)

    packed = grad_proj.shape[1]
    for strip in range(2):
        cut = slice(strip * half, (strip + 1) * half)
        spread(attn_refs[0], (0, packed), dot_tn(act[:, cut], grad_proj[...]), strip * half)
        spread(attn_refs[0], (packed, packed + local), dot_tn(grad_branch[:, cut], mixed[mine]), strip * half)
    attn.go(0)
    sums = [jnp.sum(gain_sum[at], axis=0, keepdims=True) for at in range(4)]
    sums = jnp.concatenate(sums[:2] + [found * (1.0 / mixed.shape[0]) for found in sums[2:]], axis=0)
    gain_refs[0][...] = jnp.zeros(gain_refs[0].shape, F32)
    for at in range(parts):
        gain_refs[0][bit_reverse(at, levels), 0:4, 0:own_rows] = sums[:, at * own_rows:(at + 1) * own_rows]
    gains.go(0)

    for level in range(levels):
        for scatter in (mlp, gains, attn):
            scatter.add(level)
            if level < levels - 1:
                scatter.go(level + 1)

    final = attn_refs[-1][0].astype(F32)
    exchange[mine, 0:8, :] = gain_refs[-1][0]
    exchange[mine, 8:8 + own_rows, :] = final[:, 0:BLOCK]

    def ex_copy(step, slot, peer):
        block = exchange.at[slot]
        return remote(block, block, ex_send.at[step], ex_recv.at[step], peer)

    for step, peer in enumerate(peers):
        ex_copy(step, mine, peer).start()

    def finish(step, carry):
        chunk = chunks - 1 - step
        rows = rows_at(chunk, CHUNK)
        one.third(chunk)
        center, scale = norm_stats(tokens[rows, :].astype(F32))
        unit = center * scale
        feed.third(chunk)
        one.ready(chunk)
        e = one_r[rows, :].astype(F32) * gain_one[...]
        grad_in[rows, :] = (
            hidden_one[rows, :]
            + scale
            * (e - jnp.mean(e, axis=-1, keepdims=True) - unit * jnp.mean(e * unit, axis=-1, keepdims=True))
        ).astype(BF16)
        return carry

    lax.fori_loop(0, chunks, finish, 0)

    ending = mlp_refs[-1][0].astype(F32)
    out_up[...] = ending[:, :w_up.shape[1]]
    out_down[...] = ending[:, w_up.shape[1]:]
    out_out[...] = final[:, packed:]
    for step, peer in enumerate(peers):
        ex_copy(step, mine ^ (step + 1), peer).wait_recv()
    total = exchange[0]
    for shard in range(1, mixed.shape[0]):
        total = total + exchange[shard]
    out_gains[...] = total[0:8]
    lead = (mine == 0).astype(F32)
    extra = total[8:8 + own_rows] * lead
    adds = (jnp.where(lane0 < HEAD, extra, 0.0), jnp.where(lane0 < HEAD, pltpu.roll(extra, HEAD, 1), 0.0))
    for at in range(3):
        base = final[:, BLOCK + at * local:BLOCK + (at + 1) * local]
        if at < 2:
            base = jnp.concatenate([base[:, :BLOCK] + adds[at], base[:, BLOCK:]], axis=1)
        out_attn[at] = base

    def settle(chunk, carry):
        feed.ready(chunk)
        return carry

    lax.fori_loop(0, chunks, settle, 0)
    for each in (feed, two, one):
        each.drain(chunks)
    for scatter in (mlp, attn, gains):
        scatter.drain()
    for step, peer in enumerate(peers):
        ex_copy(step, mine, peer).wait_send()


def backward_call(lengths, tokens, gain_one, gain_two, bias_two, w_attn, w_up, w_down, cotangent, saved):
    seq, width = tokens.shape
    local = w_attn.shape[2]
    units = w_up.shape[1]
    parts = lax.axis_size("dp")
    levels = parts.bit_length() - 1
    own_rows = width // parts
    chunks = seq // CHUNK
    shards = lax.axis_size("tensor")
    shape = jax.ShapeDtypeStruct
    packed = BLOCK + 3 * local
    outs = (
        shape((seq, width), BF16),
        shape((seq, width), BF16),
        shape((3, own_rows, local), F32),
        shape((own_rows, local), F32),
        shape((own_rows, units), F32),
        shape((own_rows, units), F32),
        shape((8, BLOCK), F32),
    )

    def scatter(columns, rows, dtype):
        return [
            pltpu.VMEM((max(parts >> level, 1), rows, columns), dtype) for level in range(levels + 1)
        ]

    full = lambda dtype: pltpu.VMEM((seq, width), dtype)
    half = lambda: pltpu.VMEM((chunks, BLOCK, width), BF16)
    high = -(-own_rows // 8) * 8
    scratch = (
        [full(F32), full(BF16), full(BF16), full(BF16), full(BF16), pltpu.VMEM((seq, local), BF16)]
        + [full(BF16), half(), half()]
        + [full(BF16), half(), half(), full(BF16)]
        + [full(BF16), half(), half(), full(BF16)]
        + [pltpu.VMEM((seq + PAD, local), F32)] * 2
        + [pltpu.VMEM((seq + PAD, BAND), F32), pltpu.VMEM((seq + PAD, BLOCK), F32)]
        + [pltpu.VMEM((seq, packed), BF16), pltpu.VMEM((4, 8, width), F32), pltpu.VMEM((seq, BLOCK), BF16)]
        + [pltpu.VMEM((shards, 8 + high, BLOCK), F32)]
        + scatter(2 * units, own_rows, BF16)
        + scatter(packed + local, own_rows, BF16)
        + scatter(BLOCK, 8, F32)
        + [DMA((3, 3, chunks)), DMA((3, 3, chunks)), DMA((3, levels)), DMA((3, levels)), DMA((3,)), DMA((3,))]
    )
    operands = (lengths, tokens, gain_one, gain_two, bias_two, w_attn, w_up, w_down, cotangent, *saved)
    return pl.pallas_call(
        functools.partial(backward_kernel, lengths.shape[1], levels),
        out_shape=outs,
        in_specs=[SMEM] + [VMEM] * (len(operands) - 1),
        out_specs=(VMEM,) * len(outs),
        scratch_shapes=scratch,
        compiler_params=pltpu.CompilerParams(
            collective_id=1, has_side_effects=True, vmem_limit_bytes=LIMIT
        ),
        name="backward",
    )(*operands)


def body(
    tokens, gain_one, bias_one, w_attn, w_out, gain_two, bias_two, w_up, w_down, piece_lengths, cotangent
):
    flat = lambda vector: vector.reshape(1, -1)
    saved = forward_call(tokens, flat(gain_one), flat(bias_one), w_attn, w_out, piece_lengths)
    delta, grad_in, grad_attn, grad_out, grad_up, grad_down, gains = backward_call(
        piece_lengths, tokens, flat(gain_one), flat(gain_two), flat(bias_two), w_attn, w_up, w_down, cotangent, saved
    )
    own = grad_up.shape[0]
    return (
        tokens.astype(F32) + delta.astype(F32),
        grad_in.astype(F32),
        grad_attn,
        grad_out.T,
        grad_up,
        grad_down.T,
        gains[0, :own],
        gains[1, :own],
        gains[2, :own],
        gains[3, :own],
    )


def solution(mesh):
    placed = (
        P("dp", None), P(), P(), P(None, None, "tensor"), P("tensor", None), P(), P(),
        P(None, "tensor"), P("tensor", None), P("dp", None), P("dp", None),
    )
    return jax.shard_map(
        body,
        mesh=mesh,
        in_specs=placed,
        out_specs=(
            P("dp", None), P("dp", None), P(None, "dp", "tensor"), P("tensor", "dp"), P("dp", "tensor"),
            P("tensor", "dp"), P("dp"), P("dp"), P("dp"), P("dp"),
        ),
        check_vma=False,
    )
```

time: 565 us -> 159 us (0.28); the launches traced: 557 us -> 158 us
  waiting for transfers between devices: 291 us -> 0 us
  Pallas kernels: 37.6 us -> 139 us
  matrix products: 80.5 us -> 0 us
  local copies, waits for them, and re-layouts: 55.7 us -> 12.5 us
  blocking collectives: 37.4 us -> 0 us
  other arithmetic: 37.7 us -> 5.9 us
  between operations: 15.9 us -> 0.67 us
    reduce_scatter x2 -> x0, waiting for transfers between devices: 144 us -> none  [the longest x1 72.9 us: body(): lax.psum_scatter(grad_down, 'dp', scatter_dimension=1, tiled=True)]
    psum x3 -> x0, waiting for transfers between devices: 113 us -> none  [the longest x1 68.2 us: body(): lax.psum(jnp.dot(hidden, w_down, preferred_element_type=jnp.float32).asty...]
    pallas_call x0 -> x1, Pallas kernels: none -> 102 us  [backward_call(): pl.pallas_call(functools.partial(backward_kernel, lengths.shape[1], level...]
    dot_general x20 -> x0, matrix products: 77.5 us -> none  [the longest x1 10.4 us: backward_row(): jnp.einsum('ihd,jhd->hij', grad_masked, value_rows, preferred_element_typ...]
    unnamed x1 -> x0, blocking collectives: 37.4 us -> none
    unnamed x131 -> x13, local copies, waits for them, and re-layouts: 40.3 us -> 6.11 us
    unnamed x9 -> x0, waiting for transfers between devices: 34.1 us -> none
    reduce_sum x10 -> x0, other arithmetic: 24.9 us -> none  [the longest x1 10.8 us: backward_row(): penalty_term = -jnp.sum(grad_logits, axis=0)]
  transfers between devices with their start and end apart: 7 -> 0, of which waited for: 7 -> 0; matrix products, arithmetic and copies ran while one was open for 20% -> 0% of each run, Pallas kernels for 0% -> 0%
where the time goes in v2:
time: 159 us; the launch traced here: 158 us
  Pallas kernels  139 us (87%)
  local copies, waits for them, and re-layouts  12.5 us (8%)
  other arithmetic  5.9 us (4%)
    pallas_call x1, Pallas kernels, backward_call(): pl.pallas_call(functools.partial(backward_kernel, lengths.shape[1], level...  102 us
    pallas_call x1, Pallas kernels, forward_call(): pl.pallas_call(functools.partial(forward_kernel, lengths.shape[1]), out_s...  37.5 us
    unnamed x13, local copies, waits for them, and re-layouts  6.11 us
    reshape x4, local copies, waits for them, and re-layouts, body(): flat = lambda vector: vector.reshape(1, -1)  5.07 us
    add x1, other arithmetic, body(): tokens.astype(F32) + delta.astype(F32)  4 us

profile of v2, /device:TPU:0, one launch (start us, length us, event | category | flops | bytes accessed | tf_op | source)
XLA Modules:
  0.0 158.2 jit_solution(5265823849823267715)
XLA Ops:
  0.6 1.3 reshape.33.gain.gain_one
  1.9 1.3 reshape.36.bias
  3.2 1.3 reshape.34.gain_two
  4.4 1.3 reshape.35.bias_two
  5.7 2.3 %copy.22.w_attn = bf16[3,768,192]{2,1,0:T(8,128)(2,1)} copy(bf16[3,768,192]{1,2,0:T(8,128)(2,1)} %param.14) | data formatting | bytes 1769472 | tf_op args[3]
  8.0 37.5 %forward.1 = (bf16[1024,768]{1,0:T(8,128)(2,1)}, bf16[1024,192]{1,0:T(8,128)(2,1)}, bf16[1280,192]{1,0:T(8,128)(2,1)}, bf16[1280,192]{1,0:T(8,128)(2,1)}, bf16[1...) custom-call(s32[1,8]{1,0:T(1,128)} %lengths.3, ...), custom_call_target="tpu_custom_call" | custom-call | tf_op jit(solution)/shard_map/forward/pallas_call | solution.py:271
  45.5 101.6 %backward.1 = (bf16[1024,768]{1,0:T(8,128)(2,1)}, bf16[1024,768]{1,0:T(8,128)(2,1)}, f32[3,96,192]{2,1,0:T(8,128)}, f32[96,192]{1,0:T(8,128)}, f32[96,768]{1,0:T...) custom-call(s32[1,8]{1,0:T(1,128)} %lengths.3, bf16[1024,768]{1,0:T(8,128)(2,1)} %tokens.3, ...), custom_call_target="tpu_custom_call" | custom-call | tf_op jit(solution)/shard_map/backward/pallas_call | solution.py:702
  147.2 1.4 slice_bitcast_fusion
  148.5 1.6 %copy.23 = f32[192,96]{1,0:T(8,128)} copy(f32[192,96]{0,1:T(8,128)} %bitcast.11) | data formatting | bytes 147456
  150.1 0.0 copy-start
  150.1 4.0 %convert_add_fusion = f32[1024,768]{1,0:T(8,128)} fusion(bf16[1024,768]{1,0:T(8,128)(2,1)} %get-tuple-element.39, bf16[1024,768]{1,0:T(8,128)(2,1)} %tokens.3), kind=kLoop, calls=%fused_computation | loop fusion | flops 2359296 | bytes 6291456 | tf_op jit(solution)/shard_map/add | solution.py:725
  154.1 0.0 copy-done
  154.2 0.0 copy-start.3
  154.2 0.0 copy-start.2
  154.2 0.0 copy-start.1
  154.2 1.9 %convert_element_type.11 = f32[1024,768]{1,0:T(8,128)} convert(bf16[1024,768]{1,0:T(8,128)(2,1)S(1)} %copy-done) | non-fusion elementwise | flops 786432 | bytes 4718592 | tf_op jit(solution)/shard_map/convert_element_type | solution.py:726
  156.1 0.0 copy-done.3
  156.1 0.7 copy.27
  156.8 0.0 copy-done.2
  156.8 0.7 copy.28
  157.5 0.0 copy-done.1
  157.5 0.7 copy.29
Async XLA Ops:
  150.1 4.0 %copy-start = (bf16[1024,768]{1,0:T(8,128)(2,1)S(1)}, bf16[1024,768]{1,0:T(8,128)(2,1)}, u32[]{:S(2)}) copy-start(bf16[1024,768]{1,0:T(8,128)(2,1)} %get-tuple-element.40) | copy-start | bytes 4718596
  154.2 1.9 %copy-start.3 = (f32[3,96,192]{2,1,0:T(8,128)S(1)}, f32[3,96,192]{2,1,0:T(8,128)}, u32[]{:S(2)}) copy-start(f32[3,96,192]{2,1,0:T(8,128)} %get-tuple-element.72) | copy-start | bytes 663556
  154.2 2.6 %copy-start.2 = (f32[96,768]{1,0:T(8,128)S(1)}, f32[96,768]{1,0:T(8,128)}, u32[]{:S(2)}) copy-start(f32[96,768]{1,0:T(8,128)} %get-tuple-element.74) | copy-start | bytes 884740
  154.2 3.3 %copy-start.1 = (f32[96,768]{1,0:T(8,128)S(1)}, f32[96,768]{1,0:T(8,128)}, u32[]{:S(2)}) copy-start(f32[96,768]{1,0:T(8,128)} %get-tuple-element.44) | copy-start | bytes 884740

commit v3 on v2

v3 whole, which is shorter than its diff:
```python
import functools

import jax
import jax.numpy as jnp
from jax import lax
from jax.experimental import pallas as pl
from jax.experimental.pallas import tpu as pltpu
from jax.sharding import PartitionSpec as P

F32 = jnp.float32
BF16 = jnp.bfloat16
MESH = pl.DeviceIdType.MESH
HEAD = 64
EPSILON = 1e-05
BLOCK = 128
BAND = 384
PAD = BAND - BLOCK
CHUNK = 256
SCALING = HEAD ** (-0.5)
NT = (((1,), (1,)), ((), ()))
TN = (((0,), (0,)), ((), ()))


def dot(a, b):
    return jnp.dot(a, b, preferred_element_type=F32)


def dot_nt(a, b):
    return lax.dot_general(a, b, NT, preferred_element_type=F32)


def dot_tn(a, b):
    return lax.dot_general(a, b, TN, preferred_element_type=F32)


def rows_at(index, size):
    return pl.ds(pl.multiple_of(index * size, size), size)


def first_of(position, lengths, pieces):
    first = jnp.zeros_like(position)
    end = jnp.int32(0)
    for piece in range(pieces - 1):
        size = lengths[0, piece]
        end = end + size
        first = jnp.where(position >= end, end, first)
    return first, position < end


def norm_stats(x):
    center = x - jnp.mean(x, axis=-1, keepdims=True)
    spread = jnp.mean(center * center, axis=-1, keepdims=True)
    return center, lax.rsqrt(spread + EPSILON)


def remote(src, dst, send, recv, peer):
    return pltpu.make_async_remote_copy(
        src_ref=src, dst_ref=dst, send_sem=send, recv_sem=recv, device_id=peer, device_id_type=MESH
    )


def greet(peers):
    barrier = pltpu.get_barrier_semaphore()
    for peer in peers:
        pl.semaphore_signal(barrier, inc=1, device_id=peer, device_id_type=MESH)
    pl.semaphore_wait(barrier, len(peers))


GELU_ROOT = 0.7978845608028654
GELU_CUBE = 0.044715


def bit_reverse(value, bits):
    return sum(((value >> at) & 1) << (bits - 1 - at) for at in range(bits))


def groups_of_eight(x):
    return jnp.sum(x.reshape(x.shape[0] // 8, 8, x.shape[1]), axis=0)


class Sum:
    def __init__(self, source, pair, other, result, send, recv):
        self.refs = source, pair, other, result
        self.send, self.recv = send, recv
        mine = lax.axis_index("tensor")
        self.core = mine & 1
        self.twin, self.across = {"tensor": mine ^ 1}, {"tensor": mine ^ 2}

    def half(self, chunk, core):
        return pl.ds(pl.multiple_of(chunk * CHUNK + core * BLOCK, BLOCK), BLOCK)

    def copy(self, stage, chunk):
        source, pair, other, result = self.refs
        own, theirs = self.half(chunk, self.core), self.half(chunk, 1 - self.core)
        src, dst, peer = (
            (source.at[theirs], pair.at[chunk], self.twin),
            (pair.at[chunk], other.at[chunk], self.across),
            (result.at[own], result.at[own], self.twin),
        )[stage]
        return remote(src, dst, self.send.at[stage, chunk], self.recv.at[stage, chunk], peer)

    def first(self, chunk):
        self.copy(0, chunk).start()

    def second(self, chunk):
        source, pair, other, result = self.refs
        self.copy(0, chunk).wait_recv()
        own = source[self.half(chunk, self.core), :].astype(F32)
        pair[chunk] = (own + pair[chunk].astype(F32)).astype(BF16)
        self.copy(1, chunk).start()

    def third(self, chunk):
        source, pair, other, result = self.refs
        self.copy(1, chunk).wait_recv()
        self.copy(1, chunk).wait_send()
        total = pair[chunk].astype(F32) + other[chunk].astype(F32)
        result[self.half(chunk, self.core), :] = total.astype(BF16)
        self.copy(2, chunk).start()

    def ready(self, chunk):
        self.copy(2, chunk).wait_recv()

    def sent(self, chunk, *stages):
        for stage in stages:
            self.copy(stage, chunk).wait_send()


class Scatter:
    def __init__(self, start, lands, send, recv):
        self.refs = (start, *lands)
        self.send, self.recv = send, recv
        self.parts = start.shape[0]
        self.me = lax.axis_index("dp")

    def copy(self, level):
        size = self.parts >> (level + 1)
        bit = (self.me >> level) & 1
        return remote(
            self.refs[level].at[pl.ds((1 - bit) * size, size)],
            self.refs[level + 1],
            self.send.at[level],
            self.recv.at[level],
            {"dp": self.me ^ (1 << level)},
        )

    def go(self, level):
        self.copy(level).start()

    def add(self, level):
        size = self.parts >> (level + 1)
        bit = (self.me >> level) & 1
        here, landed = self.refs[level], self.refs[level + 1]
        self.copy(level).wait_recv()

        def one(part, carry):
            total = here[bit * size + part].astype(F32) + landed[part].astype(F32)
            landed[part] = total.astype(landed.dtype)
            return carry

        lax.fori_loop(0, size, one, 0)

    def drain(self):
        for level in range(len(self.refs) - 1):
            self.copy(level).wait_send()


def layer_kernel(
    pieces, levels,
    lengths, gain_one, bias_one, gain_two, bias_two,
    tokens_hbm, w_attn_hbm, w_out_hbm, w_up_hbm, w_down_hbm, cotangent_hbm,
    out_delta, grad_in, out_attn, out_out, out_up, out_down, out_gains,
    tokens, w_attn, w_out_all, w_zero, w_up, w_down, cotangent,
    act, query, key, value, query0, key0, probs, selected, mixed,
    stacks, scores, chances, offsets, lost,
    hidden_one, act_two, hidden, grad_pre, grad_mixed,
    feed_s, feed_a, feed_b, two_s, two_a, two_b, one_b,
    grad_key, grad_value, grad_sel, grad_key0, grad_proj, gain_sum, grad_query0,
    exchange, *rest,
):
    seq, width = tokens.shape
    local = w_attn.shape[1]
    heads = local // HEAD
    blocks, chunks = seq // BLOCK, seq // CHUNK
    shards = mixed.shape[0]
    parts = 1 << levels
    own_rows = width // parts
    rest = list(rest)
    take = lambda count: [rest.pop(0) for _ in range(count)]
    mlp_refs, attn_refs, gain_refs = take(levels + 1), take(levels + 1), take(levels + 1)
    zero_send, zero_recv, out_send, out_recv, mix_send, mix_recv = take(6)
    sums_send, sums_recv, scat_send, scat_recv, ex_send, ex_recv, load_sem, tokens_sem = take(8)
    mine = lax.axis_index("tensor")
    me = lax.axis_index("dp")
    twin = {"tensor": mine ^ 1}
    across = {"tensor": mine ^ 2}
    peers = [{"tensor": mine ^ step} for step in (1, 2, 3)]

    loads = [
        pltpu.make_async_copy(source, target, load_sem.at[at])
        for at, (source, target) in enumerate((
            (w_attn_hbm, w_attn), (w_out_hbm, w_out_all.at[mine]),
            (w_up_hbm, w_up), (w_down_hbm, w_down), (cotangent_hbm, cotangent),
        ))
    ]
    attn_load, out_load, up_load, down_load, cot_load = loads

    def token_load(chunk):
        rows = rows_at(chunk, CHUNK)
        return pltpu.make_async_copy(tokens_hbm.at[rows], tokens.at[rows], tokens_sem.at[chunk])

    out_load.start()
    token_load(0).start()
    attn_load.start()
    for chunk in range(1, chunks):
        token_load(chunk).start()
    greet(tuple(peers) + tuple({"dp": me ^ (1 << level)} for level in range(levels)))
    for load in loads[2:]:
        load.start()

    def out_copy(stage, slot, peer):
        block = w_out_all.at[slot]
        return remote(block, block, out_send.at[stage], out_recv.at[stage], peer)

    def zero_copy(stage, peer, source):
        return remote(source, w_zero, zero_send.at[stage], zero_recv.at[0], peer)

    head_rows = w_attn.at[pl.ds(0, 2), pl.ds(0, BLOCK)]
    out_load.wait()
    out_copy(1, mine, twin).start()
    attn_load.wait()

    @pl.when(mine == 0)
    def _():
        zero_copy(0, across, head_rows).start()
        zero_copy(1, twin, head_rows).start()
        w_zero[...] = w_attn[0:2, 0:BLOCK]

    out_copy(0, mine, across).start()

    lane = lax.broadcasted_iota(jnp.int32, (1, local), 1)
    here = [(lane >= head * HEAD) & (lane < (head + 1) * HEAD) for head in range(heads)]
    lane0 = lax.broadcasted_iota(jnp.int32, (1, BLOCK), 1)
    row = lax.broadcasted_iota(jnp.int32, (BLOCK, 1), 0)
    column = lax.broadcasted_iota(jnp.int32, (1, BAND), 1) - PAD
    for ref in (key, value, key0, selected):
        ref[0:PAD, :] = jnp.zeros((PAD, ref.shape[1]), ref.dtype)
    for ref in (grad_key, grad_value, grad_sel, grad_key0):
        ref[...] = jnp.zeros(ref.shape, ref.dtype)
    gain_sum[...] = jnp.zeros(gain_sum.shape, F32)

    def pick(found):
        total = found[(heads - 1) * BLOCK:]
        for head in range(heads - 1):
            total = jnp.where(here[head], found[head * BLOCK:(head + 1) * BLOCK], total)
        return total

    def stack(target, wide, scale):
        for head in range(heads):
            target[head * BLOCK:(head + 1) * BLOCK, :] = jnp.where(here[head], wide * scale, 0.0).astype(BF16)

    def project(step, carry):
        rows = rows_at(step, CHUNK)
        padded = pl.ds(pl.multiple_of(step * CHUNK + PAD, CHUNK), CHUNK)
        token_load(step).wait()
        center, scale = norm_stats(tokens[rows, :].astype(F32))
        low = (center * scale * gain_one[...] + bias_one[...]).astype(BF16)
        act[rows, :] = low
        query[rows, :] = dot_nt(low, w_attn[0]).astype(BF16)
        key[padded, :] = dot_nt(low, w_attn[1]).astype(BF16)
        value[padded, :] = dot_nt(low, w_attn[2]).astype(BF16)
        return carry

    lax.fori_loop(0, chunks, project, 0)

    @pl.when(mine != 0)
    def _():
        zero_copy(0, twin, w_zero).wait_recv()

    @pl.when(mine == 2)
    def _():
        zero_copy(0, twin, w_zero).start()

    keep0 = jnp.where(lane0 < HEAD, SCALING, 0.0)

    def project0(step, carry):
        rows = rows_at(step, CHUNK)
        padded = pl.ds(pl.multiple_of(step * CHUNK + PAD, CHUNK), CHUNK)
        low = act[rows, :]
        found = dot_nt(low, w_zero[0]).astype(BF16).astype(F32)
        query0[rows, :] = (found * keep0).astype(BF16)
        key0[padded, :] = dot_nt(low, w_zero[1]).astype(BF16)
        return carry

    lax.fori_loop(0, chunks, project0, 0)

    def select(block, carry):
        rows = rows_at(block, BLOCK)
        first, _ = first_of(row + block * BLOCK, lengths, pieces)
        first = first - block * BLOCK
        score = dot_nt(query0[rows, :], key0[pl.ds(rows.start, BAND), :])
        keep = (column > first) & (column < row)
        own = pl.ds(pl.multiple_of(rows.start + PAD, BLOCK), BLOCK)
        selected[own, :] = jnp.where(keep, jnp.maximum(score, 0.0), 0.0).astype(BF16)
        return carry

    lax.fori_loop(0, blocks, select, 0)

    def mix_copy(stage, slot, block, peer):
        part = mixed.at[slot, rows_at(block, BLOCK)]
        return remote(part, part, mix_send.at[stage, block], mix_recv.at[stage, block], peer)

    GROUP = 32
    places = BAND // BLOCK

    def attend_block(block, lot):
        rows = rows_at(block, BLOCK)
        band = rows.start
        first, valid = first_of(row + block * BLOCK, lengths, pieces)
        first = first - block * BLOCK
        inside = column >= first
        carried = (inside & (column < row)).astype(BF16)
        found = [
            dot(
                carried[:, part * BLOCK:(part + 1) * BLOCK],
                selected[pl.ds(pl.multiple_of(band + part * BLOCK, BLOCK), BLOCK), BAND - (part + 1) * BLOCK:],
            )
            for part in range(places)
        ]
        for at in range(places):
            cut = slice(at * BLOCK, (at + 1) * BLOCK)
            penalty = sum(found[part][:, cut] for part in range(at, places))
            offsets[lot, :, cut] = jnp.where((inside & (column <= row))[:, cut], -penalty, -1e30)
        stack(stacks.at[lot], query[rows, :].astype(F32), SCALING)
        scores[lot] = dot_nt(stacks[lot], key[pl.ds(band, BAND), :])
        for group in range(heads * BLOCK // GROUP):
            cut = slice(group * GROUP, (group + 1) * GROUP)
            at = group * GROUP % BLOCK
            logits = scores[lot, cut, :] + offsets[lot, at:at + GROUP, :]
            raised = jnp.exp(logits - jnp.max(logits, axis=-1, keepdims=True))
            chances[lot, cut, :] = (raised * (1.0 / jnp.sum(raised, axis=-1, keepdims=True))).astype(BF16)
        low = chances[lot]
        total = pick(dot(low, value[pl.ds(band, BAND), :]))
        return low, (total * valid.astype(F32)).astype(BF16)

    def attend(step, carry):
        chunk = chunks - 1 - step
        done = [attend_block(2 * chunk + lot, lot) for lot in range(2)]
        for lot in (1, 0):
            block = 2 * chunk + lot
            probs[block] = done[lot][0]
            mixed[mine, rows_at(block, BLOCK), :] = done[lot][1]
            mix_copy(0, mine, block, across).start()
            mix_copy(1, mine, block, twin).start()
        return carry

    lax.fori_loop(0, chunks, attend, 0)

    out_copy(0, mine ^ 2, across).wait_recv()
    out_copy(2, mine ^ 2, twin).start()

    def relay(chunk):
        for lot in (1, 0):
            block = 2 * chunk + lot
            mix_copy(0, mine ^ 2, block, across).wait_recv()
            mix_copy(2, mine ^ 2, block, twin).start()

    relay(chunks - 1)
    out_copy(1, mine ^ 1, twin).wait_recv()
    out_copy(2, mine ^ 3, twin).wait_recv()
    for load in loads[2:]:
        load.wait()

    feed = Sum(feed_s, feed_a, feed_b, out_delta, sums_send.at[0], sums_recv.at[0])
    two = Sum(two_s, two_a, two_b, grad_in, sums_send.at[1], sums_recv.at[1])
    one = Sum(two_s, two_a, one_b, grad_in, sums_send.at[2], sums_recv.at[2])
    mlp = Scatter(mlp_refs[0], mlp_refs[1:], scat_send.at[0], scat_recv.at[0])
    attn = Scatter(attn_refs[0], attn_refs[1:], scat_send.at[1], scat_recv.at[1])
    gains = Scatter(gain_refs[0], gain_refs[1:], scat_send.at[2], scat_recv.at[2])

    def feed_forward(step, carry):
        chunk = chunks - 1 - step
        rows = rows_at(chunk, CHUNK)

        @pl.when(chunk > 0)
        def _():
            relay(chunk - 1)

        for lot in (1, 0):
            block = 2 * chunk + lot
            mix_copy(1, mine ^ 1, block, twin).wait_recv()
            mix_copy(2, mine ^ 3, block, twin).wait_recv()
        branch = sum(dot(mixed[shard, rows, :], w_out_all[shard]) for shard in range(shards))
        after = tokens[rows, :].astype(F32) + branch
        hidden_one[rows, :] = after
        center, scale = norm_stats(after)
        low = (center * scale * gain_two[...] + bias_two[...]).astype(BF16)
        act_two[rows, :] = low
        up = dot(low, w_up[...])
        square = up * up
        bent = jnp.tanh(GELU_ROOT * (up + GELU_CUBE * (square * up)))
        units = (0.5 * up * (1.0 + bent)).astype(BF16)
        hidden[rows, :] = units
        slope = 0.5 * (1.0 + bent) + (0.5 * GELU_ROOT) * up * (1.0 - bent * bent) * (
            1.0 + (3.0 * GELU_CUBE) * square
        )
        before = (dot_nt(cotangent[rows, :].astype(BF16), w_down[...]) * slope).astype(BF16)
        grad_pre[rows, :] = before
        two_s[rows, :] = dot_nt(before, w_up[...]).astype(BF16)
        two.first(chunk)
        feed_s[rows, :] = (dot(units, w_down[...]) + branch * (1.0 / shards)).astype(BF16)
        feed.first(chunk)
        two.second(chunk)
        return carry

    lax.fori_loop(0, chunks, feed_forward, 0)

    def spread(target, columns, found, offset):
        for at in range(found.shape[0] // own_rows):
            part = bit_reverse(offset // own_rows + at, levels)
            target[part, :, columns[0]:columns[1]] = found[at * own_rows:(at + 1) * own_rows].astype(BF16)

    half = width // 2
    units = w_up.shape[1]
    for strip in range(2):
        cut = slice(strip * half, (strip + 1) * half)
        spread(mlp_refs[0], (0, units), dot_tn(act_two[:, cut], grad_pre[...]), strip * half)
        spread(mlp_refs[0], (units, 2 * units), dot_tn(cotangent[:, cut].astype(BF16), hidden[...]), strip * half)
    mlp.go(0)

    across_row = lax.broadcasted_iota(jnp.int32, (1, BLOCK), 1)
    down_band = lax.broadcasted_iota(jnp.int32, (BAND, 1), 0) - PAD

    def attend_back(block, lot):
        rows = rows_at(block, BLOCK)
        band = pl.ds(rows.start, BAND)
        first, _ = first_of(across_row + block * BLOCK, lengths, pieces)
        first = first - block * BLOCK
        carried = ((down_band >= first) & (down_band < across_row)).astype(BF16)
        stack(stacks.at[lot], grad_mixed[rows, :].astype(F32), 1.0)
        stack(stacks.at[2 + lot], query[rows, :].astype(F32), SCALING)
        scores[lot] = dot_nt(stacks[lot], value[band, :])
        for group in range(BLOCK // GROUP):
            loss = jnp.zeros((GROUP, BAND), F32)
            for head in range(heads):
                cut = slice(head * BLOCK + group * GROUP, head * BLOCK + (group + 1) * GROUP)
                chance = probs[block, cut, :].astype(F32)
                grad = scores[lot, cut, :]
                weighed = chance * grad
                logits = weighed - chance * jnp.sum(weighed, axis=-1, keepdims=True)
                loss = loss - logits
                chances[lot, cut, :] = logits.astype(BF16)
            lost[lot, group * GROUP:(group + 1) * GROUP, :] = loss.astype(BF16)
        logits = chances[lot]
        queried = pick(dot(logits, key[band, :]))
        keyed = dot_tn(logits, stacks[2 + lot])
        valued = dot_tn(probs[block], stacks[lot])
        selects = [
            dot(carried[part * BLOCK:(part + 1) * BLOCK], lost[lot, :, :(part + 1) * BLOCK])
            for part in range(places)
        ]
        return (queried * SCALING).astype(BF16), keyed, valued, selects

    def attend_add(block, lot, keyed, valued, selects):
        rows = rows_at(block, BLOCK)
        band = pl.ds(rows.start, BAND)
        grad_key[band, :] = grad_key[band, :] + keyed
        grad_value[band, :] = grad_value[band, :] + valued
        for part in range(places):
            reach = (part + 1) * BLOCK
            rows_k = pl.ds(pl.multiple_of(rows.start + part * BLOCK, BLOCK), BLOCK)
            grad_sel[rows_k, BAND - reach:] = grad_sel[rows_k, BAND - reach:] + selects[part]
        own = pl.ds(pl.multiple_of(rows.start + PAD, BLOCK), BLOCK)
        score = jnp.where(selected[own, :] > 0, grad_sel[own, :], 0.0).astype(BF16)
        from_key = dot(score, key0[band, :])
        grad_query0[rows, :] = jnp.where(lane0 < HEAD, from_key * SCALING, 0.0).astype(BF16)
        grad_key0[band, :] = grad_key0[band, :] + dot_tn(score, query0[rows, :])

    def back(step, carry):
        chunk = chunks - 1 - step
        rows = rows_at(chunk, CHUNK)
        padded = pl.ds(pl.multiple_of(chunk * CHUNK + PAD, CHUNK), CHUNK)
        two.third(chunk)
        center, scale = norm_stats(hidden_one[rows, :])
        unit = center * scale
        two.ready(chunk)
        grad = grad_in[rows, :].astype(F32)
        gain_sum[2] = gain_sum[2] + groups_of_eight(grad * unit)
        gain_sum[3] = gain_sum[3] + groups_of_eight(grad)
        e = grad * gain_two[...]
        total = cotangent[rows, :] + scale * (
            e - jnp.mean(e, axis=-1, keepdims=True) - unit * jnp.mean(e * unit, axis=-1, keepdims=True)
        )
        hidden_one[rows, :] = total
        position = lax.broadcasted_iota(jnp.int32, (CHUNK, 1), 0) + chunk * CHUNK
        _, valid = first_of(position, lengths, pieces)
        grad_mixed[rows, :] = (
            dot_nt(total.astype(BF16), w_out_all[mine]).astype(BF16).astype(F32) * valid.astype(F32)
        ).astype(BF16)
        upper, *upper_adds = attend_back(2 * chunk + 1, 1)
        lower, *lower_adds = attend_back(2 * chunk, 0)
        attend_add(2 * chunk + 1, 1, *upper_adds)
        attend_add(2 * chunk, 0, *lower_adds)
        grad_q = jnp.concatenate([lower, upper], axis=0)
        grad_k = grad_key[padded, :].astype(BF16)
        grad_v = grad_value[padded, :].astype(BF16)
        grad_q0 = grad_query0[rows, :]
        grad_k0 = grad_key0[padded, :]
        extra = grad_q0.astype(F32) + pltpu.roll(grad_k0, HEAD, 1)
        grad_proj[rows, :] = jnp.concatenate(
            [extra, grad_q.astype(F32), grad_k.astype(F32), grad_v.astype(F32)], axis=1
        ).astype(BF16)
        partial = (
            dot(grad_q, w_attn[0])
            + dot(grad_k, w_attn[1])
            + dot(grad_v, w_attn[2])
            + dot(grad_q0, w_zero[0])
            + dot(grad_k0.astype(BF16), w_zero[1])
        )
        two.sent(chunk, 0, 2)
        two_s[rows, :] = partial.astype(BF16)
        one.first(chunk)
        center, scale = norm_stats(tokens[rows, :].astype(F32))
        gain_sum[0] = gain_sum[0] + groups_of_eight(partial * (center * scale))
        gain_sum[1] = gain_sum[1] + groups_of_eight(partial)
        one.second(chunk)
        feed.second(chunk)
        return carry

    lax.fori_loop(0, chunks, back, 0)

    packed = grad_proj.shape[1]
    for strip in range(2):
        cut = slice(strip * half, (strip + 1) * half)
        spread(attn_refs[0], (0, packed), dot_tn(act[:, cut], grad_proj[...]), strip * half)
        spread(
            attn_refs[0], (packed, packed + local),
            dot_tn(hidden_one[:, cut].astype(BF16), mixed[mine]), strip * half,
        )
    attn.go(0)
    sums = [jnp.sum(gain_sum[at], axis=0, keepdims=True) for at in range(4)]
    sums = jnp.concatenate(sums[:2] + [found * (1.0 / shards) for found in sums[2:]], axis=0)
    gain_refs[0][...] = jnp.zeros(gain_refs[0].shape, F32)
    for at in range(parts):
        gain_refs[0][bit_reverse(at, levels), 0:4, 0:own_rows] = sums[:, at * own_rows:(at + 1) * own_rows]
    gains.go(0)

    for level in range(levels):
        for scatter in (mlp, gains, attn):
            scatter.add(level)
            if level < levels - 1:
                scatter.go(level + 1)

    final = attn_refs[-1][0].astype(F32)
    exchange[mine, 0:8, :] = gain_refs[-1][0]
    exchange[mine, 8:8 + own_rows, :] = final[:, 0:BLOCK]

    def ex_copy(step, slot, peer):
        block = exchange.at[slot]
        return remote(block, block, ex_send.at[step], ex_recv.at[step], peer)

    for step, peer in enumerate(peers):
        ex_copy(step, mine, peer).start()

    def finish(step, carry):
        chunk = chunks - 1 - step
        rows = rows_at(chunk, CHUNK)
        one.third(chunk)
        center, scale = norm_stats(tokens[rows, :].astype(F32))
        unit = center * scale
        feed.third(chunk)
        one.ready(chunk)
        e = grad_in[rows, :].astype(F32) * gain_one[...]
        found = (
            hidden_one[rows, :]
            + scale
            * (e - jnp.mean(e, axis=-1, keepdims=True) - unit * jnp.mean(e * unit, axis=-1, keepdims=True))
        ).astype(BF16)
        one.sent(chunk, 2)
        grad_in[rows, :] = found
        return carry

    lax.fori_loop(0, chunks, finish, 0)

    ending = mlp_refs[-1][0].astype(F32)
    out_up[...] = ending[:, :units]
    out_down[...] = ending[:, units:]
    out_out[...] = final[:, packed:]
    for step, peer in enumerate(peers):
        ex_copy(step, mine ^ (step + 1), peer).wait_recv()
    total = exchange[0]
    for shard in range(1, shards):
        total = total + exchange[shard]
    out_gains[...] = total[0:8]
    lead = (mine == 0).astype(F32)
    extra = total[8:8 + own_rows] * lead
    adds = (jnp.where(lane0 < HEAD, extra, 0.0), jnp.where(lane0 < HEAD, pltpu.roll(extra, HEAD, 1), 0.0))
    for at in range(3):
        base = final[:, BLOCK + at * local:BLOCK + (at + 1) * local]
        if at < 2:
            base = jnp.concatenate([base[:, :BLOCK] + adds[at], base[:, BLOCK:]], axis=1)
        out_attn[at] = base

    def settle(chunk, carry):
        feed.ready(chunk)
        feed.sent(chunk, 0, 2)
        one.sent(chunk, 0)
        for lot in range(2):
            block = 2 * chunk + lot
            mix_copy(0, mine, block, across).wait_send()
            mix_copy(1, mine, block, twin).wait_send()
            mix_copy(2, mine ^ 2, block, twin).wait_send()
        return carry

    lax.fori_loop(0, chunks, settle, 0)
    for scatter in (mlp, attn, gains):
        scatter.drain()
    for step, peer in enumerate(peers):
        ex_copy(step, mine, peer).wait_send()
    out_copy(0, mine, across).wait_send()
    out_copy(1, mine, twin).wait_send()
    out_copy(2, mine ^ 2, twin).wait_send()

    @pl.when(mine == 0)
    def _():
        zero_copy(0, across, head_rows).wait_send()
        zero_copy(1, twin, head_rows).wait_send()

    @pl.when(mine == 2)
    def _():
        zero_copy(0, twin, w_zero).wait_send()


VMEM = pl.BlockSpec(memory_space=pltpu.VMEM)
SMEM = pl.BlockSpec(memory_space=pltpu.SMEM)
ANY = pl.BlockSpec(memory_space=pl.ANY)
DMA = pltpu.SemaphoreType.DMA
LIMIT = 67_000_000


def layer_call(tokens, gain_one, bias_one, w_attn, w_out, gain_two, bias_two, w_up, w_down, lengths, cotangent):
    seq, width = tokens.shape
    local = w_attn.shape[1]
    units = w_up.shape[1]
    heads = local // HEAD
    parts = lax.axis_size("dp")
    levels = parts.bit_length() - 1
    own_rows = width // parts
    blocks, chunks = seq // BLOCK, seq // CHUNK
    shards = lax.axis_size("tensor")
    shape = jax.ShapeDtypeStruct
    packed = BLOCK + 3 * local
    outs = (
        shape((seq, width), BF16),
        shape((seq, width), BF16),
        shape((3, own_rows, local), F32),
        shape((own_rows, local), F32),
        shape((own_rows, units), F32),
        shape((own_rows, units), F32),
        shape((8, BLOCK), F32),
    )

    def scatter(columns, rows, dtype):
        return [
            pltpu.VMEM((max(parts >> level, 1), rows, columns), dtype) for level in range(levels + 1)
        ]

    low = lambda *dims: pltpu.VMEM(dims, BF16)
    wide = lambda *dims: pltpu.VMEM(dims, F32)
    high = -(-own_rows // 8) * 8
    stacked = heads * BLOCK
    scratch = (
        [low(seq, width), low(3, local, width), low(shards, local, width), low(2, BLOCK, width)]
        + [low(width, units), low(units, width), wide(seq, width)]
        + [low(seq, width), low(seq, local), low(seq + PAD, local), low(seq + PAD, local)]
        + [low(seq, BLOCK), low(seq + PAD, BLOCK), low(blocks, stacked, BAND), low(seq + PAD, BAND)]
        + [low(shards, seq, local)]
        + [low(4, stacked, local), wide(2, stacked, BAND), low(2, stacked, BAND), wide(2, BLOCK, BAND), low(2, BLOCK, BAND)]
        + [wide(seq, width), low(seq, width), low(seq, units), low(seq, units), low(seq, local)]
        + [low(seq, width), low(chunks, BLOCK, width), low(chunks, BLOCK, width)]
        + [low(seq, width), low(chunks, BLOCK, width), low(chunks, BLOCK, width), low(chunks, BLOCK, width)]
        + [wide(seq + PAD, local)] * 2
        + [wide(seq + PAD, BAND), wide(seq + PAD, BLOCK)]
        + [low(seq, packed), wide(4, 8, width), low(seq, BLOCK)]
        + [wide(shards, 8 + high, BLOCK)]
        + scatter(2 * units, own_rows, BF16)
        + scatter(packed + local, own_rows, BF16)
        + scatter(BLOCK, 8, F32)
        + [DMA((2,)), DMA((1,)), DMA((3,)), DMA((3,)), DMA((3, blocks)), DMA((3, blocks))]
        + [DMA((3, 3, chunks)), DMA((3, 3, chunks)), DMA((3, levels)), DMA((3, levels)), DMA((3,)), DMA((3,))]
        + [DMA((5,)), DMA((chunks,))]
    )
    operands = (
        lengths, gain_one, bias_one, gain_two, bias_two, tokens, w_attn, w_out, w_up, w_down, cotangent,
    )
    return pl.pallas_call(
        functools.partial(layer_kernel, lengths.shape[1], levels),
        out_shape=outs,
        in_specs=[SMEM] + [VMEM] * 4 + [ANY] * 6,
        out_specs=(VMEM,) * len(outs),
        scratch_shapes=scratch,
        compiler_params=pltpu.CompilerParams(
            collective_id=0, has_side_effects=True, vmem_limit_bytes=LIMIT
        ),
        name="layer",
    )(*operands)


def body(
    tokens, gain_one, bias_one, w_attn, w_out, gain_two, bias_two, w_up, w_down, piece_lengths, cotangent
):
    flat = lambda vector: vector.reshape(1, -1)
    delta, grad_in, grad_attn, grad_out, grad_up, grad_down, gains = layer_call(
        tokens, flat(gain_one), flat(bias_one), jnp.swapaxes(w_attn, 1, 2), w_out, flat(gain_two), flat(bias_two),
        w_up, w_down, piece_lengths, cotangent,
    )
    own = grad_up.shape[0]
    return (
        tokens.astype(F32) + delta.astype(F32),
        grad_in.astype(F32),
        grad_attn,
        grad_out.T,
        grad_up,
        grad_down.T,
        gains[0, :own],
        gains[1, :own],
        gains[2, :own],
        gains[3, :own],
    )


def solution(mesh):
    placed = (
        P("dp", None), P(), P(), P(None, None, "tensor"), P("tensor", None), P(), P(),
        P(None, "tensor"), P("tensor", None), P("dp", None), P("dp", None),
    )
    return jax.shard_map(
        body,
        mesh=mesh,
        in_specs=placed,
        out_specs=(
            P("dp", None), P("dp", None), P(None, "dp", "tensor"), P("tensor", "dp"), P("dp", "tensor"),
            P("tensor", "dp"), P("dp"), P("dp"), P("dp"), P("dp"),
        ),
        check_vma=False,
    )
```

time: 159 us -> 139 us (0.87)
  Pallas kernels: 139 us -> 122 us
  local copies, waits for them, and re-layouts: 12.5 us -> 10.2 us
    pallas_call x2 -> x1, Pallas kernels: 139 us -> 122 us  [layer_call(): pl.pallas_call(functools.partial(layer_kernel, lengths.shape[1], levels),...]
    unnamed x13 -> x12, local copies, waits for them, and re-layouts: 6.11 us -> 3.79 us
where the time goes in v3:
time: 139 us
  Pallas kernels  122 us (88%)
  local copies, waits for them, and re-layouts  10.2 us (7%)
  other arithmetic  5.9 us (4%)
    pallas_call x1, Pallas kernels, layer_call(): pl.pallas_call(functools.partial(layer_kernel, lengths.shape[1], levels),...  122 us
    reshape x4, local copies, waits for them, and re-layouts, body(): flat = lambda vector: vector.reshape(1, -1)  5.07 us
    add x1, other arithmetic, body(): tokens.astype(F32) + delta.astype(F32)  4 us
    unnamed x12, local copies, waits for them, and re-layouts  3.79 us

profile of v3, /device:TPU:0, one launch (start us, length us, event | category | flops | bytes accessed | tf_op | source)
XLA Modules:
  0.0 139.2 jit_solution(4673270000544656898)
XLA Ops:
  0.6 1.3 reshape.32.gain_one
  1.9 1.3 reshape.33.bias_one
  3.2 1.3 reshape.34.gain_two
  4.4 1.3 reshape.35.bias_two
  5.7 122.4 %layer.1 = (bf16[1024,768]{1,0:T(8,128)(2,1)}, bf16[1024,768]{1,0:T(8,128)(2,1)}, f32[3,96,192]{2,1,0:T(8,128)}, f32[96,192]{1,0:T(8,128)}, f32[96,768]{1,0:T(8,...) custom-call(s32[1,8]{1,0:T(1,128)} %lengths.1, f32[1,768]{1,0:T(1,128)} %reshape.32.gain_one, f32[1,768]{1,0:T(1,128)} %reshape.33.bias_one, ...), custom_call_target="tpu_custom_call" | custom-call | tf_op jit(solution)/shard_map/layer/pallas_call | solution.py:695
  128.1 1.3 slice_bitcast_fusion
  129.5 1.6 %copy.21 = f32[192,96]{1,0:T(8,128)} copy(f32[192,96]{0,1:T(8,128)} %bitcast.13) | data formatting | bytes 147456
  131.1 0.0 copy-start
  131.1 4.0 %convert_add_fusion = f32[1024,768]{1,0:T(8,128)} fusion(bf16[1024,768]{1,0:T(8,128)(2,1)} %get-tuple-element.17, bf16[1024,768]{1,0:T(8,128)(2,1)} %tokens_hbm.1), kind=kLoop, calls=%fused_computation | loop fusion | flops 2359296 | bytes 6291456 | tf_op jit(solution)/shard_map/add | solution.py:718
  135.1 0.0 copy-done
  135.1 0.0 copy-start.3
  135.1 0.0 copy-start.2
  135.1 0.0 copy-start.1
  135.1 1.9 %convert_element_type.11 = f32[1024,768]{1,0:T(8,128)} convert(bf16[1024,768]{1,0:T(8,128)(2,1)S(1)} %copy-done) | non-fusion elementwise | flops 786432 | bytes 4718592 | tf_op jit(solution)/shard_map/convert_element_type | solution.py:719
  137.0 0.0 copy-done.3
  137.0 0.7 copy.25
  137.7 0.0 copy-done.2
  137.7 0.7 copy.26
  138.4 0.0 copy-done.1
  138.4 0.7 copy.27
Async XLA Ops:
  131.1 4.0 %copy-start = (bf16[1024,768]{1,0:T(8,128)(2,1)S(1)}, bf16[1024,768]{1,0:T(8,128)(2,1)}, u32[]{:S(2)}) copy-start(bf16[1024,768]{1,0:T(8,128)(2,1)} %get-tuple-element.18) | copy-start | bytes 4718596
  135.1 1.9 %copy-start.3 = (f32[3,96,192]{2,1,0:T(8,128)S(1)}, f32[3,96,192]{2,1,0:T(8,128)}, u32[]{:S(2)}) copy-start(f32[3,96,192]{2,1,0:T(8,128)} %get-tuple-element.50) | copy-start | bytes 663556
  135.1 2.6 %copy-start.2 = (f32[96,768]{1,0:T(8,128)S(1)}, f32[96,768]{1,0:T(8,128)}, u32[]{:S(2)}) copy-start(f32[96,768]{1,0:T(8,128)} %get-tuple-element.52) | copy-start | bytes 884740
  135.1 3.3 %copy-start.1 = (f32[96,768]{1,0:T(8,128)S(1)}, f32[96,768]{1,0:T(8,128)}, u32[]{:S(2)}) copy-start(f32[96,768]{1,0:T(8,128)} %get-tuple-element.22) | copy-start | bytes 884740

commit v4 on v3

--- a/solution.py
+++ b/solution.py
@@ -70,8 +70,8 @@
 GELU_CUBE = 0.044715
 
 
-def bit_reverse(value, bits):
-    return sum(((value >> at) & 1) << (bits - 1 - at) for at in range(bits))
+def place(value, order):
+    return sum(((value >> bit) & 1) << (len(order) - 1 - at) for at, bit in enumerate(order))
 
 
 def groups_of_eight(x):
@@ -126,21 +126,21 @@
 
 
 class Scatter:
-    def __init__(self, start, lands, send, recv):
-        self.refs = (start, *lands)
+    def __init__(self, refs, order, send, recv):
+        self.refs, self.order = refs, order
         self.send, self.recv = send, recv
-        self.parts = start.shape[0]
+        self.parts = refs[0].shape[0]
         self.me = lax.axis_index("dp")
 
     def copy(self, level):
         size = self.parts >> (level + 1)
-        bit = (self.me >> level) & 1
+        bit = (self.me >> self.order[level]) & 1
         return remote(
             self.refs[level].at[pl.ds((1 - bit) * size, size)],
             self.refs[level + 1],
             self.send.at[level],
             self.recv.at[level],
-            {"dp": self.me ^ (1 << level)},
+            {"dp": self.me ^ (1 << self.order[level])},
         )
 
     def go(self, level):
@@ -148,7 +148,7 @@
 
     def add(self, level):
         size = self.parts >> (level + 1)
-        bit = (self.me >> level) & 1
+        bit = (self.me >> self.order[level]) & 1
         here, landed = self.refs[level], self.refs[level + 1]
         self.copy(level).wait_recv()
 
@@ -158,6 +158,17 @@
             return carry
 
         lax.fori_loop(0, size, one, 0)
+
+    def put(self, columns, found, offset):
+        rows = self.refs[0].shape[1]
+        for at in range(found.shape[0] // rows):
+            part = place(offset // rows + at, self.order)
+            self.refs[0][part, :, columns] = found[at * rows:(at + 1) * rows].astype(BF16)
+
+    def step(self, level):
+        self.add(level)
+        if level + 1 < len(self.order):
+            self.go(level + 1)
 
     def drain(self):
         for level in range(len(self.refs) - 1):
@@ -186,7 +197,7 @@
     own_rows = width // parts
     rest = list(rest)
     take = lambda count: [rest.pop(0) for _ in range(count)]
-    mlp_refs, attn_refs, gain_refs = take(levels + 1), take(levels + 1), take(levels + 1)
+    scatter_refs = [take(levels + 1) for _ in range(5)]
     zero_send, zero_recv, out_send, out_recv, mix_send, mix_recv = take(6)
     sums_send, sums_recv, scat_send, scat_recv, ex_send, ex_recv, load_sem, tokens_sem = take(8)
     mine = lax.axis_index("tensor")
@@ -224,7 +235,7 @@
     def zero_copy(stage, peer, source):
         return remote(source, w_zero, zero_send.at[stage], zero_recv.at[0], peer)
 
-    head_rows = w_attn.at[pl.ds(0, 2), pl.ds(0, BLOCK)]
+    head_rows = w_attn.at[pl.ds(0, 2), pl.ds(0, HEAD)]
     out_load.wait()
     out_copy(1, mine, twin).start()
     attn_load.wait()
@@ -233,13 +244,12 @@
     def _():
         zero_copy(0, across, head_rows).start()
         zero_copy(1, twin, head_rows).start()
-        w_zero[...] = w_attn[0:2, 0:BLOCK]
+        w_zero[...] = w_attn[0:2, 0:HEAD]
 
     out_copy(0, mine, across).start()
 
     lane = lax.broadcasted_iota(jnp.int32, (1, local), 1)
     here = [(lane >= head * HEAD) & (lane < (head + 1) * HEAD) for head in range(heads)]
-    lane0 = lax.broadcasted_iota(jnp.int32, (1, BLOCK), 1)
     row = lax.broadcasted_iota(jnp.int32, (BLOCK, 1), 0)
     column = lax.broadcasted_iota(jnp.int32, (1, BAND), 1) - PAD
     for ref in (key, value, key0, selected):
@@ -263,7 +273,7 @@
         padded = pl.ds(pl.multiple_of(step * CHUNK + PAD, CHUNK), CHUNK)
         token_load(step).wait()
         center, scale = norm_stats(tokens[rows, :].astype(F32))
-        low = (center * scale * gain_one[...] + bias_one[...]).astype(BF16)
+        low = (center * scale * gain_one[...].reshape(1, width) + bias_one[...].reshape(1, width)).astype(BF16)
         act[rows, :] = low
         query[rows, :] = dot_nt(low, w_attn[0]).astype(BF16)
         key[padded, :] = dot_nt(low, w_attn[1]).astype(BF16)
@@ -280,14 +290,12 @@
     def _():
         zero_copy(0, twin, w_zero).start()
 
-    keep0 = jnp.where(lane0 < HEAD, SCALING, 0.0)
-
     def project0(step, carry):
         rows = rows_at(step, CHUNK)
         padded = pl.ds(pl.multiple_of(step * CHUNK + PAD, CHUNK), CHUNK)
         low = act[rows, :]
         found = dot_nt(low, w_zero[0]).astype(BF16).astype(F32)
-        query0[rows, :] = (found * keep0).astype(BF16)
+        query0[rows, :] = (found * SCALING).astype(BF16)
         key0[padded, :] = dot_nt(low, w_zero[1]).astype(BF16)
         return carry
 
@@ -373,9 +381,13 @@
     feed = Sum(feed_s, feed_a, feed_b, out_delta, sums_send.at[0], sums_recv.at[0])
     two = Sum(two_s, two_a, two_b, grad_in, sums_send.at[1], sums_recv.at[1])
     one = Sum(two_s, two_a, one_b, grad_in, sums_send.at[2], sums_recv.at[2])
-    mlp = Scatter(mlp_refs[0], mlp_refs[1:], scat_send.at[0], scat_recv.at[0])
-    attn = Scatter(attn_refs[0], attn_refs[1:], scat_send.at[1], scat_recv.at[1])
-    gains = Scatter(gain_refs[0], gain_refs[1:], scat_send.at[2], scat_recv.at[2])
+    straight = tuple(range(levels))
+    turned = (1, 0, *straight[2:]) if levels > 1 else straight
+    ups, downs, firsts, lasts, gains = (
+        Scatter(refs, order, scat_send.at[at], scat_recv.at[at])
+        for at, (refs, order) in enumerate(zip(scatter_refs, (straight, turned, straight, turned, straight)))
+    )
+    gain_refs = gains.refs
 
     def feed_forward(step, carry):
         chunk = chunks - 1 - step
@@ -393,7 +405,7 @@
         after = tokens[rows, :].astype(F32) + branch
         hidden_one[rows, :] = after
         center, scale = norm_stats(after)
-        low = (center * scale * gain_two[...] + bias_two[...]).astype(BF16)
+        low = (center * scale * gain_two[...].reshape(1, width) + bias_two[...].reshape(1, width)).astype(BF16)
         act_two[rows, :] = low
         up = dot(low, w_up[...])
         square = up * up
@@ -414,18 +426,16 @@
 
     lax.fori_loop(0, chunks, feed_forward, 0)
 
-    def spread(target, columns, found, offset):
-        for at in range(found.shape[0] // own_rows):
-            part = bit_reverse(offset // own_rows + at, levels)
-            target[part, :, columns[0]:columns[1]] = found[at * own_rows:(at + 1) * own_rows].astype(BF16)
-
     half = width // 2
     units = w_up.shape[1]
-    for strip in range(2):
-        cut = slice(strip * half, (strip + 1) * half)
-        spread(mlp_refs[0], (0, units), dot_tn(act_two[:, cut], grad_pre[...]), strip * half)
-        spread(mlp_refs[0], (units, 2 * units), dot_tn(cotangent[:, cut].astype(BF16), hidden[...]), strip * half)
-    mlp.go(0)
+    every = slice(None)
+    cuts = [slice(strip * half, (strip + 1) * half) for strip in range(2)]
+    for cut in cuts:
+        ups.put(every, dot_tn(act_two[:, cut], grad_pre[...]), cut.start)
+    ups.go(0)
+    for cut in cuts:
+        downs.put(every, dot_tn(cotangent[:, cut].astype(BF16), hidden[...]), cut.start)
+    downs.go(0)
 
     across_row = lax.broadcasted_iota(jnp.int32, (1, BLOCK), 1)
     down_band = lax.broadcasted_iota(jnp.int32, (BAND, 1), 0) - PAD
@@ -472,7 +482,7 @@
         own = pl.ds(pl.multiple_of(rows.start + PAD, BLOCK), BLOCK)
         score = jnp.where(selected[own, :] > 0, grad_sel[own, :], 0.0).astype(BF16)
         from_key = dot(score, key0[band, :])
-        grad_query0[rows, :] = jnp.where(lane0 < HEAD, from_key * SCALING, 0.0).astype(BF16)
+        grad_query0[rows, :] = (from_key * SCALING).astype(BF16)
         grad_key0[band, :] = grad_key0[band, :] + dot_tn(score, query0[rows, :])
 
     def back(step, carry):
@@ -486,7 +496,7 @@
         grad = grad_in[rows, :].astype(F32)
         gain_sum[2] = gain_sum[2] + groups_of_eight(grad * unit)
         gain_sum[3] = gain_sum[3] + groups_of_eight(grad)
-        e = grad * gain_two[...]
+        e = grad * gain_two[...].reshape(1, width)
         total = cotangent[rows, :] + scale * (
             e - jnp.mean(e, axis=-1, keepdims=True) - unit * jnp.mean(e * unit, axis=-1, keepdims=True)
         )
@@ -505,9 +515,8 @@
         grad_v = grad_value[padded, :].astype(BF16)
         grad_q0 = grad_query0[rows, :]
         grad_k0 = grad_key0[padded, :]
-        extra = grad_q0.astype(F32) + pltpu.roll(grad_k0, HEAD, 1)
         grad_proj[rows, :] = jnp.concatenate(
-            [extra, grad_q.astype(F32), grad_k.astype(F32), grad_v.astype(F32)], axis=1
+            [grad_q0.astype(F32), grad_k0, grad_q.astype(F32), grad_k.astype(F32), grad_v.astype(F32)], axis=1
         ).astype(BF16)
         partial = (
             dot(grad_q, w_attn[0])
@@ -524,35 +533,42 @@
         gain_sum[1] = gain_sum[1] + groups_of_eight(partial)
         one.second(chunk)
         feed.second(chunk)
+
+        @pl.when(step == chunks - 2)
+        def _():
+            ups.step(0)
+            downs.step(0)
+
         return carry
 
     lax.fori_loop(0, chunks, back, 0)
 
-    packed = grad_proj.shape[1]
-    for strip in range(2):
-        cut = slice(strip * half, (strip + 1) * half)
-        spread(attn_refs[0], (0, packed), dot_tn(act[:, cut], grad_proj[...]), strip * half)
-        spread(
-            attn_refs[0], (packed, packed + local),
-            dot_tn(hidden_one[:, cut].astype(BF16), mixed[mine]), strip * half,
-        )
-    attn.go(0)
+    split = firsts.refs[0].shape[2]
+    for cut in cuts:
+        firsts.put(every, dot_tn(act[:, cut], grad_proj[:, :split]), cut.start)
+    firsts.go(0)
+    for cut in cuts:
+        lasts.put(slice(0, local), dot_tn(act[:, cut], grad_proj[:, split:]), cut.start)
+        lasts.put(slice(local, 2 * local), dot_tn(hidden_one[:, cut].astype(BF16), mixed[mine]), cut.start)
+    lasts.go(0)
     sums = [jnp.sum(gain_sum[at], axis=0, keepdims=True) for at in range(4)]
     sums = jnp.concatenate(sums[:2] + [found * (1.0 / shards) for found in sums[2:]], axis=0)
     gain_refs[0][...] = jnp.zeros(gain_refs[0].shape, F32)
     for at in range(parts):
-        gain_refs[0][bit_reverse(at, levels), 0:4, 0:own_rows] = sums[:, at * own_rows:(at + 1) * own_rows]
+        gain_refs[0][place(at, straight), 0:4, 0:own_rows] = sums[:, at * own_rows:(at + 1) * own_rows]
     gains.go(0)
 
-    for level in range(levels):
-        for scatter in (mlp, gains, attn):
-            scatter.add(level)
-            if level < levels - 1:
-                scatter.go(level + 1)
-
-    final = attn_refs[-1][0].astype(F32)
+    for level in range(1, levels):
+        ups.step(level)
+        downs.step(level)
+        for each in (gains, firsts, lasts):
+            each.step(level - 1)
+    for each in (gains, firsts, lasts):
+        each.step(levels - 1)
+
+    final = firsts.refs[-1][0].astype(F32)
     exchange[mine, 0:8, :] = gain_refs[-1][0]
-    exchange[mine, 8:8 + own_rows, :] = final[:, 0:BLOCK]
+    exchange[mine, 8:8 + own_rows, :] = final[:, :BLOCK]
 
     def ex_copy(step, slot, peer):
         block = exchange.at[slot]
@@ -569,7 +585,7 @@
         unit = center * scale
         feed.third(chunk)
         one.ready(chunk)
-        e = grad_in[rows, :].astype(F32) * gain_one[...]
+        e = grad_in[rows, :].astype(F32) * gain_one[...].reshape(1, width)
         found = (
             hidden_one[rows, :]
             + scale
@@ -581,24 +597,20 @@
 
     lax.fori_loop(0, chunks, finish, 0)
 
-    ending = mlp_refs[-1][0].astype(F32)
-    out_up[...] = ending[:, :units]
-    out_down[...] = ending[:, units:]
-    out_out[...] = final[:, packed:]
+    out_up[...] = ups.refs[-1][0]
+    out_down[...] = downs.refs[-1][0]
+    out_out[...] = lasts.refs[-1][0, :, local:].astype(F32)
     for step, peer in enumerate(peers):
         ex_copy(step, mine ^ (step + 1), peer).wait_recv()
     total = exchange[0]
     for shard in range(1, shards):
         total = total + exchange[shard]
     out_gains[...] = total[0:8]
-    lead = (mine == 0).astype(F32)
-    extra = total[8:8 + own_rows] * lead
-    adds = (jnp.where(lane0 < HEAD, extra, 0.0), jnp.where(lane0 < HEAD, pltpu.roll(extra, HEAD, 1), 0.0))
-    for at in range(3):
+    extra = total[8:8 + own_rows] * (mine == 0).astype(F32)
+    for at, found in enumerate((extra[:, :HEAD], extra[:, HEAD:])):
         base = final[:, BLOCK + at * local:BLOCK + (at + 1) * local]
-        if at < 2:
-            base = jnp.concatenate([base[:, :BLOCK] + adds[at], base[:, BLOCK:]], axis=1)
-        out_attn[at] = base
+        out_attn[at] = jnp.concatenate([base[:, :HEAD] + found, base[:, HEAD:]], axis=1)
+    out_attn[2] = lasts.refs[-1][0, :, :local].astype(F32)
 
     def settle(chunk, carry):
         feed.ready(chunk)
@@ -612,8 +624,8 @@
         return carry
 
     lax.fori_loop(0, chunks, settle, 0)
-    for scatter in (mlp, attn, gains):
-        scatter.drain()
+    for each in (ups, downs, firsts, lasts, gains):
+        each.drain()
     for step, peer in enumerate(peers):
         ex_copy(step, mine, peer).wait_send()
     out_copy(0, mine, across).wait_send()
@@ -654,8 +666,8 @@
         shape((seq, width), BF16),
         shape((3, own_rows, local), F32),
         shape((own_rows, local), F32),
-        shape((own_rows, units), F32),
-        shape((own_rows, units), F32),
+        shape((own_rows, units), BF16),
+        shape((own_rows, units), BF16),
         shape((8, BLOCK), F32),
     )
 
@@ -669,24 +681,26 @@
     high = -(-own_rows // 8) * 8
     stacked = heads * BLOCK
     scratch = (
-        [low(seq, width), low(3, local, width), low(shards, local, width), low(2, BLOCK, width)]
+        [low(seq, width), low(3, local, width), low(shards, local, width), low(2, HEAD, width)]
         + [low(width, units), low(units, width), wide(seq, width)]
         + [low(seq, width), low(seq, local), low(seq + PAD, local), low(seq + PAD, local)]
-        + [low(seq, BLOCK), low(seq + PAD, BLOCK), low(blocks, stacked, BAND), low(seq + PAD, BAND)]
+        + [low(seq, HEAD), low(seq + PAD, HEAD), low(blocks, stacked, BAND), low(seq + PAD, BAND)]
         + [low(shards, seq, local)]
         + [low(4, stacked, local), wide(2, stacked, BAND), low(2, stacked, BAND), wide(2, BLOCK, BAND), low(2, BLOCK, BAND)]
         + [wide(seq, width), low(seq, width), low(seq, units), low(seq, units), low(seq, local)]
         + [low(seq, width), low(chunks, BLOCK, width), low(chunks, BLOCK, width)]
         + [low(seq, width), low(chunks, BLOCK, width), low(chunks, BLOCK, width), low(chunks, BLOCK, width)]
         + [wide(seq + PAD, local)] * 2
-        + [wide(seq + PAD, BAND), wide(seq + PAD, BLOCK)]
-        + [low(seq, packed), wide(4, 8, width), low(seq, BLOCK)]
+        + [wide(seq + PAD, BAND), wide(seq + PAD, HEAD)]
+        + [low(seq, packed), wide(4, 8, width), low(seq, HEAD)]
         + [wide(shards, 8 + high, BLOCK)]
-        + scatter(2 * units, own_rows, BF16)
-        + scatter(packed + local, own_rows, BF16)
+        + scatter(units, own_rows, BF16)
+        + scatter(units, own_rows, BF16)
+        + scatter(BLOCK + 2 * local, own_rows, BF16)
+        + scatter(2 * local, own_rows, BF16)
         + scatter(BLOCK, 8, F32)
         + [DMA((2,)), DMA((1,)), DMA((3,)), DMA((3,)), DMA((3, blocks)), DMA((3, blocks))]
-        + [DMA((3, 3, chunks)), DMA((3, 3, chunks)), DMA((3, levels)), DMA((3, levels)), DMA((3,)), DMA((3,))]
+        + [DMA((3, 3, chunks)), DMA((3, 3, chunks)), DMA((5, levels)), DMA((5, levels)), DMA((3,)), DMA((3,))]
         + [DMA((5,)), DMA((chunks,))]
     )
     operands = (
@@ -705,27 +719,54 @@
     )(*operands)
 
 
+def output_kernel(tokens, delta, grad, attn, out, up, down, gains, output, grad_in, to_attn, to_out, to_up, to_down, *to_gains):
+    output[...] = tokens[...].astype(F32) + delta[...].astype(F32)
+    grad_in[...] = grad[...].astype(F32)
+
+    @pl.when(pl.program_id(0) == 0)
+    def _():
+        to_attn[...] = attn[...]
+        to_out[...] = out[...].T
+        to_up[...] = up[...].astype(F32)
+        to_down[...] = down[...].astype(F32)
+        for at, ref in enumerate(to_gains):
+            ref[...] = gains[at, :ref.shape[0]]
+
+
+def output_call(tokens, delta, grad, attn, out, up, down, gains):
+    rows, width = tokens.shape
+    own = up.shape[0]
+    shape = jax.ShapeDtypeStruct
+    outs = (
+        [shape((rows, width), F32)] * 2
+        + [shape(attn.shape, F32), shape(out.shape[::-1], F32), shape(up.shape, F32), shape(down.shape, F32)]
+        + [shape((own,), F32)] * 4
+    )
+    block = pl.BlockSpec((CHUNK, width), lambda at: (at, 0))
+
+    def whole(leaf):
+        rank = len(leaf.shape)
+        return pl.BlockSpec(leaf.shape, lambda at: (0,) * rank)
+
+    return pl.pallas_call(
+        output_kernel,
+        grid=(rows // CHUNK,),
+        out_shape=outs,
+        in_specs=[block] * 3 + [whole(leaf) for leaf in (attn, out, up, down, gains)],
+        out_specs=[block] * 2 + [whole(leaf) for leaf in outs[2:]],
+        name="outputs",
+    )(tokens, delta, grad, attn, out, up, down, gains)
+
+
 def body(
     tokens, gain_one, bias_one, w_attn, w_out, gain_two, bias_two, w_up, w_down, piece_lengths, cotangent
 ):
-    flat = lambda vector: vector.reshape(1, -1)
-    delta, grad_in, grad_attn, grad_out, grad_up, grad_down, gains = layer_call(
-        tokens, flat(gain_one), flat(bias_one), jnp.swapaxes(w_attn, 1, 2), w_out, flat(gain_two), flat(bias_two),
+    found = layer_call(
+        tokens, gain_one, bias_one, jnp.swapaxes(w_attn, 1, 2), w_out, gain_two, bias_two,
         w_up, w_down, piece_lengths, cotangent,
     )
-    own = grad_up.shape[0]
-    return (
-        tokens.astype(F32) + delta.astype(F32),
-        grad_in.astype(F32),
-        grad_attn,
-        grad_out.T,
-        grad_up,
-        grad_down.T,
-        gains[0, :own],
-        gains[1, :own],
-        gains[2, :own],
-        gains[3, :own],
-    )
+    output, grad_in, grad_attn, grad_out, grad_up, grad_down, *gains = output_call(tokens, *found)
+    return (output, grad_in, grad_attn, grad_out, grad_up, grad_down.T, *gains)
 
 
 def solution(mesh):

time: 139 us -> 113 us (0.81)
  local copies, waits for them, and re-layouts: 10.2 us -> 0 us
  Pallas kernels: 122 us -> 113 us
  other arithmetic: 5.9 us -> 0 us
    pallas_call x1, Pallas kernels: 122 us -> 106 us  [layer_call(): pl.pallas_call(functools.partial(layer_kernel, lengths.shape[1], levels),...]
    pallas_call x0 -> x1, Pallas kernels: none -> 6.27 us  [output_call(): pl.pallas_call(output_kernel, grid=(rows // CHUNK,), out_shape=outs, in_s...]
    reshape x4 -> x0, local copies, waits for them, and re-layouts: 5.07 us -> none  [body(): flat = lambda vector: vector.reshape(1, -1)]
    add x1 -> x0, other arithmetic: 4 us -> none  [body(): tokens.astype(F32) + delta.astype(F32)]
    unnamed x12 -> x0, local copies, waits for them, and re-layouts: 3.79 us -> none
    convert_element_type x1 -> x0, other arithmetic: 1.9 us -> none  [body(): grad_in.astype(F32)]
where the time goes in v4:
time: 113 us
  Pallas kernels  113 us (100%)
    pallas_call x1, Pallas kernels, layer_call(): pl.pallas_call(functools.partial(layer_kernel, lengths.shape[1], levels),...  106 us
    pallas_call x1, Pallas kernels, output_call(): pl.pallas_call(output_kernel, grid=(rows // CHUNK,), out_shape=outs, in_s...  6.27 us

profile of v4, /device:TPU:0, one launch (start us, length us, event | category | flops | bytes accessed | tf_op | source)
XLA Modules:
  0.0 113.2 jit_solution(1629154822119073831)
XLA Ops:
  0.6 106.3 %layer.1 = (bf16[1024,768]{1,0:T(8,128)(2,1)}, bf16[1024,768]{1,0:T(8,128)(2,1)}, f32[3,96,192]{2,1,0:T(8,128)}, f32[96,192]{1,0:T(8,128)}, bf16[96,768]{1,0:T(8...) custom-call(s32[1,8]{1,0:T(1,128)} %lengths.1, f32[768]{0:T(1024)} %gain_one.1, f32[768]{0:T(1024)} %bias_one.1, ...), custom_call_target="tpu_custom_call" | custom-call | tf_op jit(solution)/shard_map/layer/pallas_call | solution.py:709
  106.9 6.3 %outputs.1 = (f32[1024,768]{1,0:T(8,128)}, f32[1024,768]{1,0:T(8,128)}, f32[3,96,192]{2,1,0:T(8,128)}, f32[192,96]{1,0:T(8,128)}, f32[96,768]{1,0:T(8,128)}, /*i...) custom-call(bf16[1024,768]{1,0:T(8,128)(2,1)} %tokens.1, ...), custom_call_target="tpu_custom_call" | custom-call | tf_op jit(solution)/shard_map/outputs/pallas_call | solution.py:751

commit v5 on v4

--- a/solution.py
+++ b/solution.py
@@ -179,8 +179,8 @@
     pieces, levels,
     lengths, gain_one, bias_one, gain_two, bias_two,
     tokens_hbm, w_attn_hbm, w_out_hbm, w_up_hbm, w_down_hbm, cotangent_hbm,
-    out_delta, grad_in, out_attn, out_out, out_up, out_down, out_gains,
-    tokens, w_attn, w_out_all, w_zero, w_up, w_down, cotangent,
+    output_hbm, grad_hbm, out_attn, out_out, out_up, out_down, out_gains,
+    out_delta, grad_in, tokens, w_attn, w_out_all, w_zero, w_up, w_down, cotangent,
     act, query, key, value, query0, key0, probs, selected, mixed,
     stacks, scores, chances, offsets, lost,
     hidden_one, act_two, hidden, grad_pre, grad_mixed,
@@ -197,9 +197,10 @@
     own_rows = width // parts
     rest = list(rest)
     take = lambda count: [rest.pop(0) for _ in range(count)]
-    scatter_refs = [take(levels + 1) for _ in range(5)]
-    zero_send, zero_recv, out_send, out_recv, mix_send, mix_recv = take(6)
-    sums_send, sums_recv, scat_send, scat_recv, ex_send, ex_recv, load_sem, tokens_sem = take(8)
+    scatter_refs = [take(levels + 1) for _ in range(8)]
+    part_send, part_recv, zero_send, zero_recv, out_send, out_recv, mix_send, mix_recv = take(8)
+    sums_send, sums_recv, scat_send, scat_recv, ex_send, ex_recv = take(6)
+    load_sem, tokens_sem, store_sem = take(3)
     mine = lax.axis_index("tensor")
     me = lax.axis_index("dp")
     twin = {"tensor": mine ^ 1}
@@ -235,6 +236,18 @@
     def zero_copy(stage, peer, source):
         return remote(source, w_zero, zero_send.at[stage], zero_recv.at[0], peer)
 
+    quarters = 4
+    quarter = lax.rem(me, quarters)
+    piece = local // quarters
+
+    def part_copy(stage):
+        slot = mine if stage == 0 else mine ^ 2
+        start = (quarter, quarter, quarter // 2 * 2)[stage]
+        peer = (across, {"dp": me ^ 1}, {"dp": me ^ 2})[stage]
+        size = (piece, piece, 2 * piece)[stage]
+        block = w_out_all.at[slot, pl.ds(pl.multiple_of(start * piece, piece), size)]
+        return remote(block, block, part_send.at[stage], part_recv.at[stage], peer)
+
     head_rows = w_attn.at[pl.ds(0, 2), pl.ds(0, HEAD)]
     out_load.wait()
     out_copy(1, mine, twin).start()
@@ -246,7 +259,7 @@
         zero_copy(1, twin, head_rows).start()
         w_zero[...] = w_attn[0:2, 0:HEAD]
 
-    out_copy(0, mine, across).start()
+    part_copy(0).start()
 
     lane = lax.broadcasted_iota(jnp.int32, (1, local), 1)
     here = [(lane >= head * HEAD) & (lane < (head + 1) * HEAD) for head in range(heads)]
@@ -254,10 +267,6 @@
     column = lax.broadcasted_iota(jnp.int32, (1, BAND), 1) - PAD
     for ref in (key, value, key0, selected):
         ref[0:PAD, :] = jnp.zeros((PAD, ref.shape[1]), ref.dtype)
-    for ref in (grad_key, grad_value, grad_sel, grad_key0):
-        ref[...] = jnp.zeros(ref.shape, ref.dtype)
-    gain_sum[...] = jnp.zeros(gain_sum.shape, F32)
-
     def pick(found):
         total = found[(heads - 1) * BLOCK:]
         for head in range(heads - 1):
@@ -282,21 +291,39 @@
 
     lax.fori_loop(0, chunks, project, 0)
 
-    @pl.when(mine != 0)
+    part_copy(0).wait_recv()
+    part_copy(1).start()
+
+    for load in loads[2:]:
+        load.wait()
+
+    def back_down(step, carry):
+        rows = rows_at(step, CHUNK)
+        grad_pre[rows, :] = dot_nt(cotangent[rows, :].astype(BF16), w_down[...]).astype(BF16)
+        return carry
+
+    lax.fori_loop(0, chunks, back_down, 0)
+
+    @pl.when(mine == 2)
     def _():
         zero_copy(0, twin, w_zero).wait_recv()
-
-    @pl.when(mine == 2)
+        zero_copy(0, twin, w_zero).start()
+
+    for ref in (grad_key, grad_value, grad_sel, grad_key0):
+        ref[...] = jnp.zeros(ref.shape, ref.dtype)
+    gain_sum[...] = jnp.zeros(gain_sum.shape, F32)
+
+    @pl.when((mine & 1) == 1)
     def _():
-        zero_copy(0, twin, w_zero).start()
+        zero_copy(0, twin, w_zero).wait_recv()
 
     def project0(step, carry):
         rows = rows_at(step, CHUNK)
         padded = pl.ds(pl.multiple_of(step * CHUNK + PAD, CHUNK), CHUNK)
         low = act[rows, :]
-        found = dot_nt(low, w_zero[0]).astype(BF16).astype(F32)
-        query0[rows, :] = (found * SCALING).astype(BF16)
-        key0[padded, :] = dot_nt(low, w_zero[1]).astype(BF16)
+        found = dot_nt(low, w_zero[...].reshape(2 * HEAD, width)).astype(BF16).astype(F32)
+        query0[rows, :] = (found[:, :HEAD] * SCALING).astype(BF16)
+        key0[padded, :] = found[:, HEAD:].astype(BF16)
         return carry
 
     lax.fori_loop(0, chunks, project0, 0)
@@ -312,10 +339,18 @@
         return carry
 
     lax.fori_loop(0, blocks, select, 0)
+    part_copy(1).wait_recv()
+    part_copy(2).start()
 
     def mix_copy(stage, slot, block, peer):
         part = mixed.at[slot, rows_at(block, BLOCK)]
         return remote(part, part, mix_send.at[stage, block], mix_recv.at[stage, block], peer)
+
+    def relay(chunk):
+        for lot in (1, 0):
+            block = 2 * chunk + lot
+            mix_copy(0, mine ^ 2, block, across).wait_recv()
+            mix_copy(2, mine ^ 2, block, twin).start()
 
     GROUP = 32
     places = BAND // BLOCK
@@ -352,6 +387,12 @@
 
     def attend(step, carry):
         chunk = chunks - 1 - step
+
+        @pl.when(step == chunks - 1)
+        def _():
+            part_copy(2).wait_recv()
+            out_copy(2, mine ^ 2, twin).start()
+
         done = [attend_block(2 * chunk + lot, lot) for lot in range(2)]
         for lot in (1, 0):
             block = 2 * chunk + lot
@@ -359,33 +400,23 @@
             mixed[mine, rows_at(block, BLOCK), :] = done[lot][1]
             mix_copy(0, mine, block, across).start()
             mix_copy(1, mine, block, twin).start()
+
         return carry
 
     lax.fori_loop(0, chunks, attend, 0)
-
-    out_copy(0, mine ^ 2, across).wait_recv()
-    out_copy(2, mine ^ 2, twin).start()
-
-    def relay(chunk):
-        for lot in (1, 0):
-            block = 2 * chunk + lot
-            mix_copy(0, mine ^ 2, block, across).wait_recv()
-            mix_copy(2, mine ^ 2, block, twin).start()
 
     relay(chunks - 1)
     out_copy(1, mine ^ 1, twin).wait_recv()
     out_copy(2, mine ^ 3, twin).wait_recv()
-    for load in loads[2:]:
-        load.wait()
 
     feed = Sum(feed_s, feed_a, feed_b, out_delta, sums_send.at[0], sums_recv.at[0])
     two = Sum(two_s, two_a, two_b, grad_in, sums_send.at[1], sums_recv.at[1])
     one = Sum(two_s, two_a, one_b, grad_in, sums_send.at[2], sums_recv.at[2])
     straight = tuple(range(levels))
     turned = (1, 0, *straight[2:]) if levels > 1 else straight
-    ups, downs, firsts, lasts, gains = (
+    ups_a, ups_b, downs_a, downs_b, firsts, lasts, extras, gains = (
         Scatter(refs, order, scat_send.at[at], scat_recv.at[at])
-        for at, (refs, order) in enumerate(zip(scatter_refs, (straight, turned, straight, turned, straight)))
+        for at, (refs, order) in enumerate(zip(scatter_refs, (straight, straight, turned, turned, straight, turned, straight, straight)))
     )
     gain_refs = gains.refs
 
@@ -408,6 +439,15 @@
         low = (center * scale * gain_two[...].reshape(1, width) + bias_two[...].reshape(1, width)).astype(BF16)
         act_two[rows, :] = low
         up = dot(low, w_up[...])
+
+        @pl.when(step > 1)
+        def _():
+            two.second(chunk + 1)
+
+        @pl.when(step > 1)
+        def _():
+            feed.second(chunk + 2)
+
         square = up * up
         bent = jnp.tanh(GELU_ROOT * (up + GELU_CUBE * (square * up)))
         units = (0.5 * up * (1.0 + bent)).astype(BF16)
@@ -415,27 +455,41 @@
         slope = 0.5 * (1.0 + bent) + (0.5 * GELU_ROOT) * up * (1.0 - bent * bent) * (
             1.0 + (3.0 * GELU_CUBE) * square
         )
-        before = (dot_nt(cotangent[rows, :].astype(BF16), w_down[...]) * slope).astype(BF16)
+        before = (grad_pre[rows, :].astype(F32) * slope).astype(BF16)
         grad_pre[rows, :] = before
         two_s[rows, :] = dot_nt(before, w_up[...]).astype(BF16)
         two.first(chunk)
         feed_s[rows, :] = (dot(units, w_down[...]) + branch * (1.0 / shards)).astype(BF16)
         feed.first(chunk)
-        two.second(chunk)
+
+        @pl.when(step == 0)
+        def _():
+            two.second(chunk)
+
         return carry
 
     lax.fori_loop(0, chunks, feed_forward, 0)
+    two.second(0)
+    feed.second(1)
 
     half = width // 2
     units = w_up.shape[1]
     every = slice(None)
     cuts = [slice(strip * half, (strip + 1) * half) for strip in range(2)]
+    fore, aft = slice(0, units // 2), slice(units // 2, units)
     for cut in cuts:
-        ups.put(every, dot_tn(act_two[:, cut], grad_pre[...]), cut.start)
-    ups.go(0)
+        found = dot_tn(act_two[:, cut], grad_pre[...])
+        ups_a.put(every, found[:, fore], cut.start)
+        ups_b.put(every, found[:, aft], cut.start)
+    ups_a.go(0)
+    two.third(chunks - 1)
+    ups_b.go(0)
     for cut in cuts:
-        downs.put(every, dot_tn(cotangent[:, cut].astype(BF16), hidden[...]), cut.start)
-    downs.go(0)
+        found = dot_tn(cotangent[:, cut].astype(BF16), hidden[...])
+        downs_a.put(every, found[:, fore], cut.start)
+        downs_b.put(every, found[:, aft], cut.start)
+    downs_a.go(0)
+    downs_b.go(0)
 
     across_row = lax.broadcasted_iota(jnp.int32, (1, BLOCK), 1)
     down_band = lax.broadcasted_iota(jnp.int32, (BAND, 1), 0) - PAD
@@ -489,7 +543,6 @@
         chunk = chunks - 1 - step
         rows = rows_at(chunk, CHUNK)
         padded = pl.ds(pl.multiple_of(chunk * CHUNK + PAD, CHUNK), CHUNK)
-        two.third(chunk)
         center, scale = norm_stats(hidden_one[rows, :])
         unit = center * scale
         two.ready(chunk)
@@ -506,8 +559,33 @@
         grad_mixed[rows, :] = (
             dot_nt(total.astype(BF16), w_out_all[mine]).astype(BF16).astype(F32) * valid.astype(F32)
         ).astype(BF16)
+
+        @pl.when(step == chunks - 2)
+        def _():
+            ups_a.step(0)
+            downs_a.step(0)
+
+        @pl.when(step == chunks - 1)
+        def _():
+            ups_a.step(1)
+            downs_a.step(1)
+
         upper, *upper_adds = attend_back(2 * chunk + 1, 1)
         lower, *lower_adds = attend_back(2 * chunk, 0)
+
+        @pl.when(step > 0)
+        def _():
+            one.second(chunk + 1)
+
+        @pl.when(step == 0)
+        def _():
+            feed.second(0)
+
+        @pl.when(step == chunks - 1)
+        def _():
+            ups_b.step(1)
+            downs_b.step(1)
+
         attend_add(2 * chunk + 1, 1, *upper_adds)
         attend_add(2 * chunk, 0, *lower_adds)
         grad_q = jnp.concatenate([lower, upper], axis=0)
@@ -531,54 +609,54 @@
         center, scale = norm_stats(tokens[rows, :].astype(F32))
         gain_sum[0] = gain_sum[0] + groups_of_eight(partial * (center * scale))
         gain_sum[1] = gain_sum[1] + groups_of_eight(partial)
-        one.second(chunk)
-        feed.second(chunk)
 
         @pl.when(step == chunks - 2)
         def _():
-            ups.step(0)
-            downs.step(0)
+            ups_b.step(0)
+            downs_b.step(0)
+
+        @pl.when(step < chunks - 1)
+        def _():
+            two.third(chunk - 1)
 
         return carry
 
     lax.fori_loop(0, chunks, back, 0)
 
-    split = firsts.refs[0].shape[2]
     for cut in cuts:
-        firsts.put(every, dot_tn(act[:, cut], grad_proj[:, :split]), cut.start)
-    firsts.go(0)
-    for cut in cuts:
-        lasts.put(slice(0, local), dot_tn(act[:, cut], grad_proj[:, split:]), cut.start)
-        lasts.put(slice(local, 2 * local), dot_tn(hidden_one[:, cut].astype(BF16), mixed[mine]), cut.start)
-    lasts.go(0)
+        extras.put(every, dot_tn(act[:, cut], grad_proj[:, :BLOCK]), cut.start)
+    extras.go(0)
+    one.second(0)
     sums = [jnp.sum(gain_sum[at], axis=0, keepdims=True) for at in range(4)]
     sums = jnp.concatenate(sums[:2] + [found * (1.0 / shards) for found in sums[2:]], axis=0)
     gain_refs[0][...] = jnp.zeros(gain_refs[0].shape, F32)
     for at in range(parts):
         gain_refs[0][place(at, straight), 0:4, 0:own_rows] = sums[:, at * own_rows:(at + 1) * own_rows]
     gains.go(0)
-
-    for level in range(1, levels):
-        ups.step(level)
-        downs.step(level)
-        for each in (gains, firsts, lasts):
-            each.step(level - 1)
-    for each in (gains, firsts, lasts):
-        each.step(levels - 1)
-
-    final = firsts.refs[-1][0].astype(F32)
-    exchange[mine, 0:8, :] = gain_refs[-1][0]
-    exchange[mine, 8:8 + own_rows, :] = final[:, :BLOCK]
+    for cut in cuts:
+        lasts.put(slice(0, local), dot_tn(act[:, cut], grad_proj[:, BLOCK + 2 * local:]), cut.start)
+        lasts.put(slice(local, 2 * local), dot_tn(hidden_one[:, cut].astype(BF16), mixed[mine]), cut.start)
+    lasts.go(0)
+    for cut in cuts:
+        firsts.put(every, dot_tn(act[:, cut], grad_proj[:, BLOCK:BLOCK + 2 * local]), cut.start)
+    firsts.go(0)
 
     def ex_copy(step, slot, peer):
         block = exchange.at[slot]
         return remote(block, block, ex_send.at[step], ex_recv.at[step], peer)
 
-    for step, peer in enumerate(peers):
-        ex_copy(step, mine, peer).start()
-
-    def finish(step, carry):
-        chunk = chunks - 1 - step
+    def swap():
+        exchange[mine, 0:8, :] = gain_refs[-1][0]
+        exchange[mine, 8:8 + own_rows, :] = extras.refs[-1][0].astype(F32)
+        for step, peer in enumerate(peers):
+            ex_copy(step, mine, peer).start()
+
+    def store(which, chunk):
+        rows = rows_at(chunk, CHUNK)
+        source, target = ((out_delta, output_hbm), (grad_in, grad_hbm))[which]
+        return pltpu.make_async_copy(source.at[rows], target.at[rows], store_sem.at[which, chunk])
+
+    def finish(chunk):
         rows = rows_at(chunk, CHUNK)
         one.third(chunk)
         center, scale = norm_stats(tokens[rows, :].astype(F32))
@@ -586,36 +664,66 @@
         feed.third(chunk)
         one.ready(chunk)
         e = grad_in[rows, :].astype(F32) * gain_one[...].reshape(1, width)
-        found = (
-            hidden_one[rows, :]
-            + scale
-            * (e - jnp.mean(e, axis=-1, keepdims=True) - unit * jnp.mean(e * unit, axis=-1, keepdims=True))
-        ).astype(BF16)
+        found = hidden_one[rows, :] + scale * (
+            e - jnp.mean(e, axis=-1, keepdims=True) - unit * jnp.mean(e * unit, axis=-1, keepdims=True)
+        )
         one.sent(chunk, 2)
-        grad_in[rows, :] = found
-        return carry
-
-    lax.fori_loop(0, chunks, finish, 0)
-
-    out_up[...] = ups.refs[-1][0]
-    out_down[...] = downs.refs[-1][0]
-    out_out[...] = lasts.refs[-1][0, :, local:].astype(F32)
+        grad_in[rows, :] = found.astype(BF16)
+        store(1, chunk).start()
+
+    def give(chunk):
+        rows = rows_at(chunk, CHUNK)
+        feed.ready(chunk)
+        found = tokens[rows, :].astype(F32) + out_delta[rows, :].astype(F32)
+        feed.sent(chunk, 2)
+        out_delta[rows, :] = found.astype(BF16)
+        store(0, chunk).start()
+
+    left = list(range(chunks))
+    finish(left.pop())
+    give(left[-1] + 1)
+    finish(left.pop())
+    for level in range(levels):
+        for each in (extras, gains):
+            each.step(level)
+        if level == levels - 1:
+            swap()
+        for each in (lasts, firsts):
+            each.step(level)
+        if level >= 2:
+            for each in (ups_a, downs_a, ups_b, downs_b):
+                each.step(level)
+        if left:
+            give(left[-1] + 1)
+            finish(left.pop())
+    while left:
+        give(left[-1] + 1)
+        finish(left.pop())
+    give(0)
+
+    for ref, pair in ((out_up, (ups_a, ups_b)), (out_down, (downs_a, downs_b))):
+        ref[:, fore] = pair[0].refs[-1][0]
+        ref[:, aft] = pair[1].refs[-1][0]
     for step, peer in enumerate(peers):
         ex_copy(step, mine ^ (step + 1), peer).wait_recv()
     total = exchange[0]
     for shard in range(1, shards):
         total = total + exchange[shard]
     out_gains[...] = total[0:8]
+    final = firsts.refs[-1][0].astype(F32)
     extra = total[8:8 + own_rows] * (mine == 0).astype(F32)
     for at, found in enumerate((extra[:, :HEAD], extra[:, HEAD:])):
-        base = final[:, BLOCK + at * local:BLOCK + (at + 1) * local]
+        base = final[:, at * local:(at + 1) * local]
         out_attn[at] = jnp.concatenate([base[:, :HEAD] + found, base[:, HEAD:]], axis=1)
     out_attn[2] = lasts.refs[-1][0, :, :local].astype(F32)
+    out_out[...] = lasts.refs[-1][0, :, local:].astype(F32)
 
     def settle(chunk, carry):
-        feed.ready(chunk)
-        feed.sent(chunk, 0, 2)
+        feed.sent(chunk, 0)
         one.sent(chunk, 0)
+        store(0, chunk).wait()
+        store(1, chunk).wait()
+
         for lot in range(2):
             block = 2 * chunk + lot
             mix_copy(0, mine, block, across).wait_send()
@@ -624,11 +732,12 @@
         return carry
 
     lax.fori_loop(0, chunks, settle, 0)
-    for each in (ups, downs, firsts, lasts, gains):
+    for each in (ups_a, ups_b, downs_a, downs_b, firsts, lasts, extras, gains):
         each.drain()
     for step, peer in enumerate(peers):
         ex_copy(step, mine, peer).wait_send()
-    out_copy(0, mine, across).wait_send()
+    for stage in range(3):
+        part_copy(stage).wait_send()
     out_copy(1, mine, twin).wait_send()
     out_copy(2, mine ^ 2, twin).wait_send()
 
@@ -660,7 +769,6 @@
     blocks, chunks = seq // BLOCK, seq // CHUNK
     shards = lax.axis_size("tensor")
     shape = jax.ShapeDtypeStruct
-    packed = BLOCK + 3 * local
     outs = (
         shape((seq, width), BF16),
         shape((seq, width), BF16),
@@ -678,10 +786,9 @@
 
     low = lambda *dims: pltpu.VMEM(dims, BF16)
     wide = lambda *dims: pltpu.VMEM(dims, F32)
-    high = -(-own_rows // 8) * 8
     stacked = heads * BLOCK
     scratch = (
-        [low(seq, width), low(3, local, width), low(shards, local, width), low(2, HEAD, width)]
+        [low(seq, width), low(seq, width), low(seq, width), low(3, local, width), low(shards, local, width), low(2, HEAD, width)]
         + [low(width, units), low(units, width), wide(seq, width)]
         + [low(seq, width), low(seq, local), low(seq + PAD, local), low(seq + PAD, local)]
         + [low(seq, HEAD), low(seq + PAD, HEAD), low(blocks, stacked, BAND), low(seq + PAD, BAND)]
@@ -692,16 +799,19 @@
         + [low(seq, width), low(chunks, BLOCK, width), low(chunks, BLOCK, width), low(chunks, BLOCK, width)]
         + [wide(seq + PAD, local)] * 2
         + [wide(seq + PAD, BAND), wide(seq + PAD, HEAD)]
-        + [low(seq, packed), wide(4, 8, width), low(seq, HEAD)]
-        + [wide(shards, 8 + high, BLOCK)]
-        + scatter(units, own_rows, BF16)
-        + scatter(units, own_rows, BF16)
-        + scatter(BLOCK + 2 * local, own_rows, BF16)
+        + [low(seq, BLOCK + 3 * local), wide(4, 8, width), low(seq, HEAD)]
+        + [wide(shards, 8 - own_rows // -8 * 8, BLOCK)]
+        + scatter(units // 2, own_rows, BF16)
+        + scatter(units // 2, own_rows, BF16)
+        + scatter(units // 2, own_rows, BF16)
+        + scatter(units // 2, own_rows, BF16)
         + scatter(2 * local, own_rows, BF16)
+        + scatter(2 * local, own_rows, BF16)
+        + scatter(BLOCK, own_rows, BF16)
         + scatter(BLOCK, 8, F32)
-        + [DMA((2,)), DMA((1,)), DMA((3,)), DMA((3,)), DMA((3, blocks)), DMA((3, blocks))]
-        + [DMA((3, 3, chunks)), DMA((3, 3, chunks)), DMA((5, levels)), DMA((5, levels)), DMA((3,)), DMA((3,))]
-        + [DMA((5,)), DMA((chunks,))]
+        + [DMA((3,)), DMA((3,)), DMA((2,)), DMA((1,)), DMA((3,)), DMA((3,)), DMA((3, blocks)), DMA((3, blocks))]
+        + [DMA((3, 3, chunks)), DMA((3, 3, chunks)), DMA((8, levels)), DMA((8, levels)), DMA((3,)), DMA((3,))]
+        + [DMA((5,)), DMA((chunks,)), DMA((2, chunks))]
     )
     operands = (
         lengths, gain_one, bias_one, gain_two, bias_two, tokens, w_attn, w_out, w_up, w_down, cotangent,
@@ -710,7 +820,7 @@
         functools.partial(layer_kernel, lengths.shape[1], levels),
         out_shape=outs,
         in_specs=[SMEM] + [VMEM] * 4 + [ANY] * 6,
-        out_specs=(VMEM,) * len(outs),
+        out_specs=(ANY,) * 2 + (VMEM,) * (len(outs) - 2),
         scratch_shapes=scratch,
         compiler_params=pltpu.CompilerParams(
             collective_id=0, has_side_effects=True, vmem_limit_bytes=LIMIT
@@ -719,9 +829,9 @@
     )(*operands)
 
 
-def output_kernel(tokens, delta, grad, attn, out, up, down, gains, output, grad_in, to_attn, to_out, to_up, to_down, *to_gains):
-    output[...] = tokens[...].astype(F32) + delta[...].astype(F32)
-    grad_in[...] = grad[...].astype(F32)
+def output_kernel(output, grad_in, attn, out, up, down, gains, to_output, to_grad, to_attn, to_out, to_up, to_down, *to_gains):
+    to_output[...] = output[...].astype(F32)
+    to_grad[...] = grad_in[...].astype(F32)
 
     @pl.when(pl.program_id(0) == 0)
     def _():
@@ -733,8 +843,8 @@
             ref[...] = gains[at, :ref.shape[0]]
 
 
-def output_call(tokens, delta, grad, attn, out, up, down, gains):
-    rows, width = tokens.shape
+def output_call(output, grad_in, attn, out, up, down, gains):
+    rows, width = output.shape
     own = up.shape[0]
     shape = jax.ShapeDtypeStruct
     outs = (
@@ -752,10 +862,10 @@
         output_kernel,
         grid=(rows // CHUNK,),
         out_shape=outs,
-        in_specs=[block] * 3 + [whole(leaf) for leaf in (attn, out, up, down, gains)],
+        in_specs=[block] * 2 + [whole(leaf) for leaf in (attn, out, up, down, gains)],
         out_specs=[block] * 2 + [whole(leaf) for leaf in outs[2:]],
         name="outputs",
-    )(tokens, delta, grad, attn, out, up, down, gains)
+    )(output, grad_in, attn, out, up, down, gains)
 
 
 def body(
@@ -765,7 +875,7 @@
         tokens, gain_one, bias_one, jnp.swapaxes(w_attn, 1, 2), w_out, gain_two, bias_two,
         w_up, w_down, piece_lengths, cotangent,
     )
-    output, grad_in, grad_attn, grad_out, grad_up, grad_down, *gains = output_call(tokens, *found)
+    output, grad_in, grad_attn, grad_out, grad_up, grad_down, *gains = output_call(*found)
     return (output, grad_in, grad_attn, grad_out, grad_up, grad_down.T, *gains)
 
 

time: 113 us -> 101 us (0.89)
  Pallas kernels: 113 us -> 100 us
    pallas_call x1, Pallas kernels: 106 us -> 94.6 us  [layer_call(): pl.pallas_call(functools.partial(layer_kernel, lengths.shape[1], levels),...]
where the time goes in v5:
time: 101 us
  Pallas kernels  100 us (99%)
    pallas_call x1, Pallas kernels, layer_call(): pl.pallas_call(functools.partial(layer_kernel, lengths.shape[1], levels),...  94.6 us
    pallas_call x1, Pallas kernels, output_call(): pl.pallas_call(output_kernel, grid=(rows // CHUNK,), out_shape=outs, in_s...  5.66 us

profile of v5, /device:TPU:0, one launch (start us, length us, event | category | flops | bytes accessed | tf_op | source)
XLA Modules:
  0.0 101.1 jit_solution(13615174839185986441)
XLA Ops:
  0.6 94.6 %layer.1 = (bf16[1024,768]{1,0:T(8,128)(2,1)}, bf16[1024,768]{1,0:T(8,128)(2,1)}, f32[3,96,192]{2,1,0:T(8,128)}, f32[96,192]{1,0:T(8,128)}, bf16[96,768]{1,0:T(8...) custom-call(s32[1,8]{1,0:T(1,128)} %lengths.1, f32[768]{0:T(1024)} %gain_one.1, f32[768]{0:T(1024)} %bias_one.1, ...), custom_call_target="tpu_custom_call" | custom-call | tf_op jit(solution)/shard_map/layer/pallas_call | solution.py:819
  95.3 5.7 %outputs.1 = (f32[1024,768]{1,0:T(8,128)}, f32[1024,768]{1,0:T(8,128)}, f32[3,96,192]{2,1,0:T(8,128)}, f32[192,96]{1,0:T(8,128)}, f32[96,768]{1,0:T(8,128)}, /*i...) custom-call(bf16[1024,768]{1,0:T(8,128)(2,1)} %get-tuple-element.27.output, ...), custom_call_target="tpu_custom_call" | custom-call | tf_op jit(solution)/shard_map/outputs/pallas_call | solution.py:861

commit v6 on v5

--- a/solution.py
+++ b/solution.py
@@ -179,14 +179,14 @@
     pieces, levels,
     lengths, gain_one, bias_one, gain_two, bias_two,
     tokens_hbm, w_attn_hbm, w_out_hbm, w_up_hbm, w_down_hbm, cotangent_hbm,
-    output_hbm, grad_hbm, out_attn, out_out, out_up, out_down, out_gains,
+    output_hbm, grad_hbm, small_hbm, extra_hbm, gains_hbm,
     out_delta, grad_in, tokens, w_attn, w_out_all, w_zero, w_up, w_down, cotangent,
     act, query, key, value, query0, key0, probs, selected, mixed,
     stacks, scores, chances, offsets, lost,
     hidden_one, act_two, hidden, grad_pre, grad_mixed,
     feed_s, feed_a, feed_b, two_s, two_a, two_b, one_b,
     grad_key, grad_value, grad_sel, grad_key0, grad_proj, gain_sum, grad_query0,
-    exchange, *rest,
+    exchange, extra_parts, *rest,
 ):
     seq, width = tokens.shape
     local = w_attn.shape[1]
@@ -197,10 +197,10 @@
     own_rows = width // parts
     rest = list(rest)
     take = lambda count: [rest.pop(0) for _ in range(count)]
-    scatter_refs = [take(levels + 1) for _ in range(8)]
+    scatter_refs = [take(levels + 1) for _ in range(10)]
     part_send, part_recv, zero_send, zero_recv, out_send, out_recv, mix_send, mix_recv = take(8)
     sums_send, sums_recv, scat_send, scat_recv, ex_send, ex_recv = take(6)
-    load_sem, tokens_sem, store_sem = take(3)
+    load_sem, tokens_sem, store_sem, small_sem, extra_send, extra_recv = take(6)
     mine = lax.axis_index("tensor")
     me = lax.axis_index("dp")
     twin = {"tensor": mine ^ 1}
@@ -225,6 +225,7 @@
     attn_load.start()
     for chunk in range(1, chunks):
         token_load(chunk).start()
+    extra_parts[...] = jnp.zeros(extra_parts.shape, BF16)
     greet(tuple(peers) + tuple({"dp": me ^ (1 << level)} for level in range(levels)))
     for load in loads[2:]:
         load.start()
@@ -291,9 +292,6 @@
 
     lax.fori_loop(0, chunks, project, 0)
 
-    part_copy(0).wait_recv()
-    part_copy(1).start()
-
     for load in loads[2:]:
         load.wait()
 
@@ -309,6 +307,8 @@
         zero_copy(0, twin, w_zero).wait_recv()
         zero_copy(0, twin, w_zero).start()
 
+    part_copy(0).wait_recv()
+    part_copy(1).start()
     for ref in (grad_key, grad_value, grad_sel, grad_key0):
         ref[...] = jnp.zeros(ref.shape, ref.dtype)
     gain_sum[...] = jnp.zeros(gain_sum.shape, F32)
@@ -414,9 +414,9 @@
     one = Sum(two_s, two_a, one_b, grad_in, sums_send.at[2], sums_recv.at[2])
     straight = tuple(range(levels))
     turned = (1, 0, *straight[2:]) if levels > 1 else straight
-    ups_a, ups_b, downs_a, downs_b, firsts, lasts, extras, gains = (
+    ups_a, ups_b, downs_a, downs_b, firsts_a, firsts_b, lasts_a, lasts_b, extras, gains = (
         Scatter(refs, order, scat_send.at[at], scat_recv.at[at])
-        for at, (refs, order) in enumerate(zip(scatter_refs, (straight, straight, turned, turned, straight, turned, straight, straight)))
+        for at, (refs, order) in enumerate(zip(scatter_refs, (straight,) * 2 + (turned,) + (straight,) * 3 + (turned,) + (straight,) * 3))
     )
     gain_refs = gains.refs
 
@@ -435,6 +435,7 @@
         branch = sum(dot(mixed[shard, rows, :], w_out_all[shard]) for shard in range(shards))
         after = tokens[rows, :].astype(F32) + branch
         hidden_one[rows, :] = after
+        feed_s[rows, :] = branch.astype(BF16)
         center, scale = norm_stats(after)
         low = (center * scale * gain_two[...].reshape(1, width) + bias_two[...].reshape(1, width)).astype(BF16)
         act_two[rows, :] = low
@@ -443,10 +444,6 @@
         @pl.when(step > 1)
         def _():
             two.second(chunk + 1)
-
-        @pl.when(step > 1)
-        def _():
-            feed.second(chunk + 2)
 
         square = up * up
         bent = jnp.tanh(GELU_ROOT * (up + GELU_CUBE * (square * up)))
@@ -459,8 +456,6 @@
         grad_pre[rows, :] = before
         two_s[rows, :] = dot_nt(before, w_up[...]).astype(BF16)
         two.first(chunk)
-        feed_s[rows, :] = (dot(units, w_down[...]) + branch * (1.0 / shards)).astype(BF16)
-        feed.first(chunk)
 
         @pl.when(step == 0)
         def _():
@@ -470,7 +465,6 @@
 
     lax.fori_loop(0, chunks, feed_forward, 0)
     two.second(0)
-    feed.second(1)
 
     half = width // 2
     units = w_up.shape[1]
@@ -478,18 +472,36 @@
     cuts = [slice(strip * half, (strip + 1) * half) for strip in range(2)]
     fore, aft = slice(0, units // 2), slice(units // 2, units)
     for cut in cuts:
-        found = dot_tn(act_two[:, cut], grad_pre[...])
-        ups_a.put(every, found[:, fore], cut.start)
-        ups_b.put(every, found[:, aft], cut.start)
-    ups_a.go(0)
-    two.third(chunks - 1)
-    ups_b.go(0)
-    for cut in cuts:
         found = dot_tn(cotangent[:, cut].astype(BF16), hidden[...])
         downs_a.put(every, found[:, fore], cut.start)
         downs_b.put(every, found[:, aft], cut.start)
     downs_a.go(0)
     downs_b.go(0)
+    for cut in cuts:
+        found = dot_tn(act_two[:, cut], grad_pre[...])
+        ups_a.put(every, found[:, fore], cut.start)
+        ups_b.put(every, found[:, aft], cut.start)
+    ups_a.go(0)
+    ups_b.go(0)
+    two.third(chunks - 1)
+
+    def feeding(chunk):
+        rows = rows_at(chunk, CHUNK)
+        branch = feed_s[rows, :].astype(F32)
+        feed_s[rows, :] = (dot(hidden[rows, :], w_down[...]) + branch * (1.0 / shards)).astype(BF16)
+        feed.first(chunk)
+
+    def feed_early(step, carry):
+        chunk = chunks - 1 - step
+        feeding(chunk)
+
+        @pl.when(step > 0)
+        def _():
+            feed.second(chunk + 1)
+
+        return carry
+
+    lax.fori_loop(0, chunks // 2, feed_early, 0)
 
     across_row = lax.broadcasted_iota(jnp.int32, (1, BLOCK), 1)
     down_band = lax.broadcasted_iota(jnp.int32, (BAND, 1), 0) - PAD
@@ -560,16 +572,6 @@
             dot_nt(total.astype(BF16), w_out_all[mine]).astype(BF16).astype(F32) * valid.astype(F32)
         ).astype(BF16)
 
-        @pl.when(step == chunks - 2)
-        def _():
-            ups_a.step(0)
-            downs_a.step(0)
-
-        @pl.when(step == chunks - 1)
-        def _():
-            ups_a.step(1)
-            downs_a.step(1)
-
         upper, *upper_adds = attend_back(2 * chunk + 1, 1)
         lower, *lower_adds = attend_back(2 * chunk, 0)
 
@@ -579,12 +581,15 @@
 
         @pl.when(step == 0)
         def _():
-            feed.second(0)
-
-        @pl.when(step == chunks - 1)
-        def _():
-            ups_b.step(1)
-            downs_b.step(1)
+            feed.second(chunks // 2)
+
+        @pl.when(step == 2)
+        def _():
+            ups_a.step(0)
+
+        @pl.when(step == 3)
+        def _():
+            ups_b.step(0)
 
         attend_add(2 * chunk + 1, 1, *upper_adds)
         attend_add(2 * chunk, 0, *lower_adds)
@@ -610,10 +615,18 @@
         gain_sum[0] = gain_sum[0] + groups_of_eight(partial * (center * scale))
         gain_sum[1] = gain_sum[1] + groups_of_eight(partial)
 
-        @pl.when(step == chunks - 2)
-        def _():
-            ups_b.step(0)
+        @pl.when(step == 0)
+        def _():
             downs_b.step(0)
+            downs_a.step(0)
+
+        @pl.when(step == 1)
+        def _():
+            downs_b.step(1)
+
+        @pl.when(step == 3)
+        def _():
+            ups_a.step(1)
 
         @pl.when(step < chunks - 1)
         def _():
@@ -626,30 +639,66 @@
     for cut in cuts:
         extras.put(every, dot_tn(act[:, cut], grad_proj[:, :BLOCK]), cut.start)
     extras.go(0)
-    one.second(0)
     sums = [jnp.sum(gain_sum[at], axis=0, keepdims=True) for at in range(4)]
     sums = jnp.concatenate(sums[:2] + [found * (1.0 / shards) for found in sums[2:]], axis=0)
     gain_refs[0][...] = jnp.zeros(gain_refs[0].shape, F32)
     for at in range(parts):
         gain_refs[0][place(at, straight), 0:4, 0:own_rows] = sums[:, at * own_rows:(at + 1) * own_rows]
     gains.go(0)
+    edge = 2 * BLOCK
     for cut in cuts:
-        lasts.put(slice(0, local), dot_tn(act[:, cut], grad_proj[:, BLOCK + 2 * local:]), cut.start)
-        lasts.put(slice(local, 2 * local), dot_tn(hidden_one[:, cut].astype(BF16), mixed[mine]), cut.start)
-    lasts.go(0)
+        found = jnp.concatenate(
+            [
+                dot_tn(act[:, cut], grad_proj[:, BLOCK + 2 * local:]),
+                dot_tn(hidden_one[:, cut].astype(BF16), mixed[mine]),
+            ],
+            axis=1,
+        )
+        lasts_a.put(every, found[:, :edge], cut.start)
+        lasts_b.put(every, found[:, edge:], cut.start)
+    lasts_a.go(0)
+    lasts_b.go(0)
     for cut in cuts:
-        firsts.put(every, dot_tn(act[:, cut], grad_proj[:, BLOCK:BLOCK + 2 * local]), cut.start)
-    firsts.go(0)
+        found = dot_tn(act[:, cut], grad_proj[:, BLOCK:BLOCK + 2 * local])
+        firsts_a.put(every, found[:, :edge], cut.start)
+        firsts_b.put(every, found[:, edge:], cut.start)
+    firsts_a.go(0)
+    firsts_b.go(0)
+    downs_a.step(1)
+    ups_b.step(1)
+    one.second(0)
 
     def ex_copy(step, slot, peer):
         block = exchange.at[slot]
         return remote(block, block, ex_send.at[step], ex_recv.at[step], peer)
 
+    def extra_copy(step):
+        return remote(
+            extras.refs[-1].at[0], extra_parts.at[step], extra_send.at[0], extra_recv.at[step], {"tensor": 0}
+        )
+
     def swap():
-        exchange[mine, 0:8, :] = gain_refs[-1][0]
-        exchange[mine, 8:8 + own_rows, :] = extras.refs[-1][0].astype(F32)
+        exchange[mine] = gain_refs[-1][0]
         for step, peer in enumerate(peers):
             ex_copy(step, mine, peer).start()
+        for step in range(3):
+
+            @pl.when(mine == step + 1)
+            def _():
+                extra_copy(step).start()
+
+    def feed_late(step, carry):
+        chunk = chunks // 2 - 1 - step
+        feeding(chunk)
+
+        @pl.when(step > 0)
+        def _():
+            feed.second(chunk + 1)
+
+        return carry
+
+    lax.fori_loop(0, chunks // 2, feed_late, 0)
+    feed.second(0)
 
     def store(which, chunk):
         rows = rows_at(chunk, CHUNK)
@@ -679,44 +728,58 @@
         out_delta[rows, :] = found.astype(BF16)
         store(0, chunk).start()
 
+    small = (
+        (ups_a, 0, every), (ups_b, 1, every), (downs_a, 2, every), (downs_b, 3, every),
+        (firsts_a, 4, pl.ds(0, edge)), (firsts_b, 4, pl.ds(edge, 2 * local - edge)),
+        (lasts_a, 5, pl.ds(0, edge)), (lasts_b, 5, pl.ds(edge, 2 * local - edge)),
+    )
+
+    def small_store(at):
+        group, slot, columns = small[at]
+        return pltpu.make_async_copy(group.refs[-1].at[0], small_hbm.at[slot, :, columns], small_sem.at[at])
+
     left = list(range(chunks))
     finish(left.pop())
-    give(left[-1] + 1)
+    for each in (extras, gains):
+        each.step(0)
     finish(left.pop())
     for level in range(levels):
-        for each in (extras, gains):
+        for each in (lasts_a, firsts_a, lasts_b, firsts_b) if level == 0 else (firsts_a, lasts_a, firsts_b, lasts_b):
             each.step(level)
-        if level == levels - 1:
+        if level + 1 < levels:
+            for each in (extras, gains):
+                each.step(level + 1)
+        if level + 2 == levels:
             swap()
-        for each in (lasts, firsts):
-            each.step(level)
         if level >= 2:
             for each in (ups_a, downs_a, ups_b, downs_b):
                 each.step(level)
         if left:
-            give(left[-1] + 1)
+            give(left[-1] + 2)
             finish(left.pop())
-    while left:
-        give(left[-1] + 1)
-        finish(left.pop())
+    for at in range(8):
+        small_store(at).start()
+    give(1)
     give(0)
 
-    for ref, pair in ((out_up, (ups_a, ups_b)), (out_down, (downs_a, downs_b))):
-        ref[:, fore] = pair[0].refs[-1][0]
-        ref[:, aft] = pair[1].refs[-1][0]
     for step, peer in enumerate(peers):
         ex_copy(step, mine ^ (step + 1), peer).wait_recv()
-    total = exchange[0]
-    for shard in range(1, shards):
-        total = total + exchange[shard]
-    out_gains[...] = total[0:8]
-    final = firsts.refs[-1][0].astype(F32)
-    extra = total[8:8 + own_rows] * (mine == 0).astype(F32)
-    for at, found in enumerate((extra[:, :HEAD], extra[:, HEAD:])):
-        base = final[:, at * local:(at + 1) * local]
-        out_attn[at] = jnp.concatenate([base[:, :HEAD] + found, base[:, HEAD:]], axis=1)
-    out_attn[2] = lasts.refs[-1][0, :, :local].astype(F32)
-    out_out[...] = lasts.refs[-1][0, :, local:].astype(F32)
+    last = pltpu.make_async_copy(exchange, gains_hbm, small_sem.at[len(small)])
+    last.start()
+    for step in range(3):
+
+        @pl.when(mine == 0)
+        def _():
+            extra_copy(step).wait_recv()
+
+        @pl.when(mine == step + 1)
+        def _():
+            extra_copy(step).wait_send()
+
+    parts_store = pltpu.make_async_copy(extra_parts, extra_hbm.at[pl.ds(0, 3)], small_sem.at[len(small) + 1])
+    own_store = pltpu.make_async_copy(extras.refs[-1].at[0], extra_hbm.at[3], small_sem.at[len(small) + 2])
+    parts_store.start()
+    own_store.start()
 
     def settle(chunk, carry):
         feed.sent(chunk, 0)
@@ -732,8 +795,12 @@
         return carry
 
     lax.fori_loop(0, chunks, settle, 0)
-    for each in (ups_a, ups_b, downs_a, downs_b, firsts, lasts, extras, gains):
+    for each in (ups_a, ups_b, downs_a, downs_b, firsts_a, firsts_b, lasts_a, lasts_b, extras, gains):
         each.drain()
+    for at in range(len(small)):
+        small_store(at).wait()
+    for each in (last, parts_store, own_store):
+        each.wait()
     for step, peer in enumerate(peers):
         ex_copy(step, mine, peer).wait_send()
     for stage in range(3):
@@ -772,11 +839,9 @@
     outs = (
         shape((seq, width), BF16),
         shape((seq, width), BF16),
-        shape((3, own_rows, local), F32),
-        shape((own_rows, local), F32),
-        shape((own_rows, units), BF16),
-        shape((own_rows, units), BF16),
-        shape((8, BLOCK), F32),
+        shape((6, own_rows, 2 * local), BF16),
+        shape((4, own_rows, BLOCK), BF16),
+        shape((shards, 8, BLOCK), F32),
     )
 
     def scatter(columns, rows, dtype):
@@ -800,18 +865,20 @@
         + [wide(seq + PAD, local)] * 2
         + [wide(seq + PAD, BAND), wide(seq + PAD, HEAD)]
         + [low(seq, BLOCK + 3 * local), wide(4, 8, width), low(seq, HEAD)]
-        + [wide(shards, 8 - own_rows // -8 * 8, BLOCK)]
+        + [wide(shards, 8, BLOCK), low(3, own_rows, BLOCK)]
         + scatter(units // 2, own_rows, BF16)
         + scatter(units // 2, own_rows, BF16)
         + scatter(units // 2, own_rows, BF16)
         + scatter(units // 2, own_rows, BF16)
-        + scatter(2 * local, own_rows, BF16)
-        + scatter(2 * local, own_rows, BF16)
+        + scatter(2 * BLOCK, own_rows, BF16)
+        + scatter(2 * local - 2 * BLOCK, own_rows, BF16)
+        + scatter(2 * BLOCK, own_rows, BF16)
+        + scatter(2 * local - 2 * BLOCK, own_rows, BF16)
         + scatter(BLOCK, own_rows, BF16)
         + scatter(BLOCK, 8, F32)
         + [DMA((3,)), DMA((3,)), DMA((2,)), DMA((1,)), DMA((3,)), DMA((3,)), DMA((3, blocks)), DMA((3, blocks))]
-        + [DMA((3, 3, chunks)), DMA((3, 3, chunks)), DMA((8, levels)), DMA((8, levels)), DMA((3,)), DMA((3,))]
-        + [DMA((5,)), DMA((chunks,)), DMA((2, chunks))]
+        + [DMA((3, 3, chunks)), DMA((3, 3, chunks)), DMA((10, levels)), DMA((10, levels)), DMA((3,)), DMA((3,))]
+        + [DMA((5,)), DMA((chunks,)), DMA((2, chunks)), DMA((11,)), DMA((1,)), DMA((3,))]
     )
     operands = (
         lengths, gain_one, bias_one, gain_two, bias_two, tokens, w_attn, w_out, w_up, w_down, cotangent,
@@ -820,7 +887,7 @@
         functools.partial(layer_kernel, lengths.shape[1], levels),
         out_shape=outs,
         in_specs=[SMEM] + [VMEM] * 4 + [ANY] * 6,
-        out_specs=(ANY,) * 2 + (VMEM,) * (len(outs) - 2),
+        out_specs=(ANY,) * len(outs),
         scratch_shapes=scratch,
         compiler_params=pltpu.CompilerParams(
             collective_id=0, has_side_effects=True, vmem_limit_bytes=LIMIT
@@ -829,28 +896,43 @@
     )(*operands)
 
 
-def output_kernel(output, grad_in, attn, out, up, down, gains, to_output, to_grad, to_attn, to_out, to_up, to_down, *to_gains):
+def output_kernel(output, grad_in, small, extra, gains, to_output, to_grad, to_attn, to_out, to_up, to_down, *to_gains):
     to_output[...] = output[...].astype(F32)
     to_grad[...] = grad_in[...].astype(F32)
+    first = lax.axis_index("tensor") == 0
 
     @pl.when(pl.program_id(0) == 0)
     def _():
-        to_attn[...] = attn[...]
-        to_out[...] = out[...].T
-        to_up[...] = up[...].astype(F32)
-        to_down[...] = down[...].astype(F32)
+        half = small.shape[2]
+        local = half // 2
+        for ref, start in ((to_up, 0), (to_down, 2)):
+            ref[:, :half] = small[start].astype(F32)
+            ref[:, half:] = small[start + 1].astype(F32)
+        added = sum(extra[at].astype(F32) for at in range(4))
+        added = jnp.where(first, added, 0.0)
+        found = small[4].astype(F32)
+        for at in range(2):
+            base = found[:, at * local:(at + 1) * local]
+            head = base[:, :HEAD] + added[:, at * HEAD:(at + 1) * HEAD]
+            to_attn[at] = jnp.concatenate([head, base[:, HEAD:]], axis=1)
+        found = small[5].astype(F32)
+        to_attn[2] = found[:, :local]
+        to_out[...] = found[:, local:].T
+        total = gains[0]
+        for shard in range(1, gains.shape[0]):
+            total = total + gains[shard]
         for at, ref in enumerate(to_gains):
-            ref[...] = gains[at, :ref.shape[0]]
-
-
-def output_call(output, grad_in, attn, out, up, down, gains):
+            ref[...] = total[at, :ref.shape[0]]
+
+
+def output_call(output, grad_in, small, extra, gains):
     rows, width = output.shape
-    own = up.shape[0]
-    shape = jax.ShapeDtypeStruct
+    own, half = small.shape[1:]
+    shape = lambda *dims: jax.ShapeDtypeStruct(dims, F32)
     outs = (
-        [shape((rows, width), F32)] * 2
-        + [shape(attn.shape, F32), shape(out.shape[::-1], F32), shape(up.shape, F32), shape(down.shape, F32)]
-        + [shape((own,), F32)] * 4
+        [shape(rows, width)] * 2
+        + [shape(3, own, half // 2), shape(half // 2, own), shape(own, 2 * half), shape(own, 2 * half)]
+        + [shape(own)] * 4
     )
     block = pl.BlockSpec((CHUNK, width), lambda at: (at, 0))
 
@@ -862,10 +944,10 @@
         output_kernel,
         grid=(rows // CHUNK,),
         out_shape=outs,
-        in_specs=[block] * 2 + [whole(leaf) for leaf in (attn, out, up, down, gains)],
+        in_specs=[block] * 2 + [whole(small), whole(extra), whole(gains)],
         out_specs=[block] * 2 + [whole(leaf) for leaf in outs[2:]],
         name="outputs",
-    )(output, grad_in, attn, out, up, down, gains)
+    )(output, grad_in, small, extra, gains)
 
 
 def body(

time: 101 us -> 97.3 us (0.963)
  Pallas kernels: 100 us -> 96.2 us
    pallas_call x1, Pallas kernels: 94.6 us -> 90.5 us  [layer_call(): pl.pallas_call(functools.partial(layer_kernel, lengths.shape[1], levels),...]
where the time goes in v6:
time: 97.3 us; the launch traced here: 97 us
  Pallas kernels  96.2 us (99%)
    pallas_call x1, Pallas kernels, layer_call(): pl.pallas_call(functools.partial(layer_kernel, lengths.shape[1], levels),...  90.5 us
    pallas_call x1, Pallas kernels, output_call(): pl.pallas_call(output_kernel, grid=(rows // CHUNK,), out_shape=outs, in_s...  5.71 us

profile of v6, /device:TPU:0, one launch (start us, length us, event | category | flops | bytes accessed | tf_op | source)
XLA Modules:
  0.0 97.0 jit_solution(2230198002838378856)
XLA Ops:
  0.6 90.5 %layer.1 = (bf16[1024,768]{1,0:T(8,128)(2,1)}, bf16[1024,768]{1,0:T(8,128)(2,1)}, bf16[6,96,384]{2,1,0:T(8,128)(2,1)}, bf16[4,96,128]{2,1,0:T(8,128)(2,1)}, f32[4,8,128]{2,1,0:T(8,128)}) custom-call(s32[1,8]{1,0:T(1,128)} %lengths.1, f32[768]{0:T(1024)} %gain_one.1, f32[768]{0:T(1024)} %bias_one.1, f32[768]{0:T(1024)} %gain_two.1, f32[768]{0:T(1024)} %bias_two.1, ...), custom_call_target="tpu_custom_call" | custom-call | tf_op jit(solution)/shard_map/layer/pallas_call | solution.py:886
  91.2 5.7 %outputs.1 = (f32[1024,768]{1,0:T(8,128)}, f32[1024,768]{1,0:T(8,128)}, f32[3,96,192]{2,1,0:T(8,128)}, f32[192,96]{1,0:T(8,128)}, f32[96,768]{1,0:T(8,128)}, /*i...) custom-call(bf16[1024,768]{1,0:T(8,128)(2,1)} %get-tuple-element.25.output, ...), custom_call_target="tpu_custom_call" | custom-call | tf_op jit(solution)/shard_map/outputs/pallas_call | solution.py:943

commit v7 on v6

--- a/solution.py
+++ b/solution.py
@@ -186,7 +186,7 @@
     hidden_one, act_two, hidden, grad_pre, grad_mixed,
     feed_s, feed_a, feed_b, two_s, two_a, two_b, one_b,
     grad_key, grad_value, grad_sel, grad_key0, grad_proj, gain_sum, grad_query0,
-    exchange, extra_parts, *rest,
+    exchange, extra_parts, w_joined, *rest,
 ):
     seq, width = tokens.shape
     local = w_attn.shape[1]
@@ -292,6 +292,11 @@
 
     lax.fori_loop(0, chunks, project, 0)
 
+    @pl.when(mine != 2)
+    def _():
+        part_copy(0).wait_recv()
+        part_copy(1).start()
+
     for load in loads[2:]:
         load.wait()
 
@@ -306,9 +311,9 @@
     def _():
         zero_copy(0, twin, w_zero).wait_recv()
         zero_copy(0, twin, w_zero).start()
-
-    part_copy(0).wait_recv()
-    part_copy(1).start()
+        part_copy(0).wait_recv()
+        part_copy(1).start()
+
     for ref in (grad_key, grad_value, grad_sel, grad_key0):
         ref[...] = jnp.zeros(ref.shape, ref.dtype)
     gain_sum[...] = jnp.zeros(gain_sum.shape, F32)
@@ -316,6 +321,9 @@
     @pl.when((mine & 1) == 1)
     def _():
         zero_copy(0, twin, w_zero).wait_recv()
+
+    w_joined[:BLOCK, :] = w_zero[...].reshape(BLOCK, width)
+    w_joined[BLOCK:, :] = w_attn[...].reshape(3 * local, width)
 
     def project0(step, carry):
         rows = rows_at(step, CHUNK)
@@ -327,6 +335,11 @@
         return carry
 
     lax.fori_loop(0, chunks, project0, 0)
+
+    @pl.when(mine != 2)
+    def _():
+        part_copy(1).wait_recv()
+        part_copy(2).start()
 
     def select(block, carry):
         rows = rows_at(block, BLOCK)
@@ -339,8 +352,11 @@
         return carry
 
     lax.fori_loop(0, blocks, select, 0)
-    part_copy(1).wait_recv()
-    part_copy(2).start()
+
+    @pl.when(mine == 2)
+    def _():
+        part_copy(1).wait_recv()
+        part_copy(2).start()
 
     def mix_copy(stage, slot, block, peer):
         part = mixed.at[slot, rows_at(block, BLOCK)]
@@ -432,7 +448,8 @@
             block = 2 * chunk + lot
             mix_copy(1, mine ^ 1, block, twin).wait_recv()
             mix_copy(2, mine ^ 3, block, twin).wait_recv()
-        branch = sum(dot(mixed[shard, rows, :], w_out_all[shard]) for shard in range(shards))
+        joined = jnp.concatenate([mixed[shard, rows, :] for shard in range(shards)], axis=1)
+        branch = dot(joined, w_out_all[...].reshape(shards * local, width))
         after = tokens[rows, :].astype(F32) + branch
         hidden_one[rows, :] = after
         feed_s[rows, :] = branch.astype(BF16)
@@ -446,12 +463,12 @@
             two.second(chunk + 1)
 
         square = up * up
-        bent = jnp.tanh(GELU_ROOT * (up + GELU_CUBE * (square * up)))
-        units = (0.5 * up * (1.0 + bent)).astype(BF16)
+        bent = jnp.tanh(up * (GELU_ROOT + (GELU_ROOT * GELU_CUBE) * square))
+        share = 0.5 + 0.5 * bent
+        active = up * share
+        units = active.astype(BF16)
         hidden[rows, :] = units
-        slope = 0.5 * (1.0 + bent) + (0.5 * GELU_ROOT) * up * (1.0 - bent * bent) * (
-            1.0 + (3.0 * GELU_CUBE) * square
-        )
+        slope = share + active * (1.0 - bent) * (GELU_ROOT + (3.0 * GELU_ROOT * GELU_CUBE) * square)
         before = (grad_pre[rows, :].astype(F32) * slope).astype(BF16)
         grad_pre[rows, :] = before
         two_s[rows, :] = dot_nt(before, w_up[...]).astype(BF16)
@@ -492,13 +509,7 @@
         feed.first(chunk)
 
     def feed_early(step, carry):
-        chunk = chunks - 1 - step
-        feeding(chunk)
-
-        @pl.when(step > 0)
-        def _():
-            feed.second(chunk + 1)
-
+        feeding(chunks - 1 - step)
         return carry
 
     lax.fori_loop(0, chunks // 2, feed_early, 0)
@@ -572,6 +583,11 @@
             dot_nt(total.astype(BF16), w_out_all[mine]).astype(BF16).astype(F32) * valid.astype(F32)
         ).astype(BF16)
 
+        @pl.when(step == 1)
+        def _():
+            downs_b.step(0)
+            downs_a.step(0)
+
         upper, *upper_adds = attend_back(2 * chunk + 1, 1)
         lower, *lower_adds = attend_back(2 * chunk, 0)
 
@@ -581,7 +597,8 @@
 
         @pl.when(step == 0)
         def _():
-            feed.second(chunks // 2)
+            for late in range(chunks - 1, chunks // 2 - 1, -1):
+                feed.second(late)
 
         @pl.when(step == 2)
         def _():
@@ -601,24 +618,13 @@
         grad_proj[rows, :] = jnp.concatenate(
             [grad_q0.astype(F32), grad_k0, grad_q.astype(F32), grad_k.astype(F32), grad_v.astype(F32)], axis=1
         ).astype(BF16)
-        partial = (
-            dot(grad_q, w_attn[0])
-            + dot(grad_k, w_attn[1])
-            + dot(grad_v, w_attn[2])
-            + dot(grad_q0, w_zero[0])
-            + dot(grad_k0.astype(BF16), w_zero[1])
-        )
+        partial = dot(grad_proj[rows, :], w_joined[...])
         two.sent(chunk, 0, 2)
         two_s[rows, :] = partial.astype(BF16)
         one.first(chunk)
         center, scale = norm_stats(tokens[rows, :].astype(F32))
         gain_sum[0] = gain_sum[0] + groups_of_eight(partial * (center * scale))
         gain_sum[1] = gain_sum[1] + groups_of_eight(partial)
-
-        @pl.when(step == 0)
-        def _():
-            downs_b.step(0)
-            downs_a.step(0)
 
         @pl.when(step == 1)
         def _():
@@ -665,7 +671,6 @@
     firsts_a.go(0)
     firsts_b.go(0)
     downs_a.step(1)
-    ups_b.step(1)
     one.second(0)
 
     def ex_copy(step, slot, peer):
@@ -698,6 +703,7 @@
         return carry
 
     lax.fori_loop(0, chunks // 2, feed_late, 0)
+    ups_b.step(1)
     feed.second(0)
 
     def store(which, chunk):
@@ -865,7 +871,7 @@
         + [wide(seq + PAD, local)] * 2
         + [wide(seq + PAD, BAND), wide(seq + PAD, HEAD)]
         + [low(seq, BLOCK + 3 * local), wide(4, 8, width), low(seq, HEAD)]
-        + [wide(shards, 8, BLOCK), low(3, own_rows, BLOCK)]
+        + [wide(shards, 8, BLOCK), low(3, own_rows, BLOCK), low(BLOCK + 3 * local, width)]
         + scatter(units // 2, own_rows, BF16)
         + scatter(units // 2, own_rows, BF16)
         + scatter(units // 2, own_rows, BF16)

time: 97.3 us -> 96.4 us (level)
  no operation moved by 1% of the time
where the time goes in v7:
time: 96.4 us; the launch traced here: 96.2 us
  Pallas kernels  95.4 us (99%)
    pallas_call x1, Pallas kernels, layer_call(): pl.pallas_call(functools.partial(layer_kernel, lengths.shape[1], levels),...  89.6 us
    pallas_call x1, Pallas kernels, output_call(): pl.pallas_call(output_kernel, grid=(rows // CHUNK,), out_shape=outs, in_s...  5.71 us

profile of v7, /device:TPU:0, one launch (start us, length us, event | category | flops | bytes accessed | tf_op | source)
XLA Modules:
  0.0 96.2 jit_solution(9537955108279475380)
XLA Ops:
  0.6 89.6 %layer.1 = (bf16[1024,768]{1,0:T(8,128)(2,1)}, bf16[1024,768]{1,0:T(8,128)(2,1)}, bf16[6,96,384]{2,1,0:T(8,128)(2,1)}, bf16[4,96,128]{2,1,0:T(8,128)(2,1)}, f32[4,8,128]{2,1,0:T(8,128)}) custom-call(s32[1,8]{1,0:T(1,128)} %lengths.1, f32[768]{0:T(1024)} %gain_one.1, f32[768]{0:T(1024)} %bias_one.1, f32[768]{0:T(1024)} %gain_two.1, f32[768]{0:T(1024)} %bias_two.1, ...), custom_call_target="tpu_custom_call" | custom-call | tf_op jit(solution)/shard_map/layer/pallas_call | solution.py:892
  90.3 5.7 %outputs.1 = (f32[1024,768]{1,0:T(8,128)}, f32[1024,768]{1,0:T(8,128)}, f32[3,96,192]{2,1,0:T(8,128)}, f32[192,96]{1,0:T(8,128)}, f32[96,768]{1,0:T(8,128)}, /*i...) custom-call(bf16[1024,768]{1,0:T(8,128)(2,1)} %get-tuple-element.25.output, ...), custom_call_target="tpu_custom_call" | custom-call | tf_op jit(solution)/shard_map/outputs/pallas_call | solution.py:949
